TPU v7x, 32 devices: a whole 2x2x4 slice. The times are simulated.
32 devices in a mesh: dp: 8 (over y, x, core), rep: 4 (over z).
Axes of the slice: x: 2, y: 2, z: 4, core: 2. Of those that a mesh axis runs over, the one named last changes fastest.
Arguments:
- audio_patches: bfloat16 [2, 64, 228, 256], P(None, ('dp', 'rep')), may hold values from -6 to 6
- clip_lengths: int32 [2, 64], P(None, ('dp', 'rep')), may hold values from 114 to 228, as said below
- video_ids: int32 [2, 64], P(None, ('dp', 'rep')), may hold values from 0 to 31
- image_tokens: bfloat16 [2, 64, 256, 1280], P(None, ('dp', 'rep')), may hold values from -6 to 6
- i_qkv: bfloat16 [1280, 3840], P('dp'), may hold values from -0.15625 to 0.15625
- i_out: bfloat16 [1280, 1280], P('dp'), may hold values from -0.625 to 0.625
- i_up: bfloat16 [1280, 5120], P('dp'), may hold values from -0.15625 to 0.15625
- i_down: bfloat16 [5120, 1280], P('dp'), may hold values from -0.078125 to 0.078125
- i_proj: bfloat16 [1280, 1024], P('dp'), may hold values from -0.15625 to 0.15625
- i_gains: bfloat16 [3, 1280], P(None, 'dp'), may hold values from 0.5 to 1.5
- a_patch: float32 [256, 768], P('dp'), may hold values from -0.375 to 0.375
- a_qkv: float32 [768, 2304], P('dp'), may hold values from -0.21875 to 0.21875
- a_out: float32 [768, 768], P('dp'), may hold values from -0.875 to 0.875
- a_up: float32 [768, 3072], P('dp'), may hold values from -0.21875 to 0.21875
- a_down: float32 [3072, 768], P('dp'), may hold values from -0.109375 to 0.109375
- a_proj: float32 [768, 1024], P('dp'), may hold values from -0.21875 to 0.21875
- a_gains: float32 [3, 768], P(None, 'dp'), may hold values from 0.5 to 1.5
- m_patch: float32 [256, 768], P('dp'), may hold values from -5.722046e-06 to 5.722046e-06
- m_qkv: float32 [768, 2304], P('dp'), may hold values from -5.722046e-06 to 5.722046e-06
- m_out: float32 [768, 768], P('dp'), may hold values from -5.722046e-06 to 5.722046e-06
- m_up: float32 [768, 3072], P('dp'), may hold values from -5.722046e-06 to 5.722046e-06
- m_down: float32 [3072, 768], P('dp'), may hold values from -5.722046e-06 to 5.722046e-06
- m_proj: float32 [768, 1024], P('dp'), may hold values from -5.722046e-06 to 5.722046e-06
- m_gains: float32 [3, 768], P(None, 'dp'), may hold values from -2.2888184e-05 to 2.2888184e-05
- s_patch: float32 [256, 768], P('dp'), may hold values from 1.2405519e-14 to 4.9622077e-14
- s_qkv: float32 [768, 2304], P('dp'), may hold values from 1.2405519e-14 to 4.9622077e-14
- s_out: float32 [768, 768], P('dp'), may hold values from 1.2405519e-14 to 4.9622077e-14
- s_up: float32 [768, 3072], P('dp'), may hold values from 1.2405519e-14 to 4.9622077e-14
- s_down: float32 [3072, 768], P('dp'), may hold values from 1.2405519e-14 to 4.9622077e-14
- s_proj: float32 [768, 1024], P('dp'), may hold values from 1.2405519e-14 to 4.9622077e-14
- s_gains: float32 [3, 768], P(None, 'dp'), may hold values from 1.9848831e-13 to 7.9395323e-13
Outputs:
- loss: float32 [], replicated
- grad_norm: float32 [], replicated
- new_patch: float32 [256, 768], P('dp')
- new_qkv: float32 [768, 2304], P('dp')
- new_out: float32 [768, 768], P('dp')
- new_up: float32 [768, 3072], P('dp')
- new_down: float32 [3072, 768], P('dp')
- new_proj: float32 [768, 1024], P('dp')
- new_gains: float32 [3, 768], P(None, 'dp')
- first_patch: float32 [256, 768], P('dp')
- first_qkv: float32 [768, 2304], P('dp')
- first_out: float32 [768, 768], P('dp')
- first_up: float32 [768, 3072], P('dp')
- first_down: float32 [3072, 768], P('dp')
- first_proj: float32 [768, 1024], P('dp')
- first_gains: float32 [3, 768], P(None, 'dp')
- second_patch: float32 [256, 768], P('dp')
- second_qkv: float32 [768, 2304], P('dp')
- second_out: float32 [768, 768], P('dp')
- second_up: float32 [768, 3072], P('dp')
- second_down: float32 [3072, 768], P('dp')
- second_proj: float32 [768, 1024], P('dp')
- second_gains: float32 [3, 768], P(None, 'dp')
Inputs may be any that keep to these rules, and one draw needn't show every extreme that they name: `clip_lengths`: each clip has 228 or 114 patches; in every micro-batch the first clip has 228 and the second 228 // 2.
All inputs are finite; a program needn't handle non-finite values.
Results may differ from a plain program's by a relative error of at most 0.014.
Values may be sent and summed in bfloat16 or wider, within the bound.
No kernel may reach another device: no remote copies, remote signals or barrier semaphores. Data moves between devices by JAX's collectives and lax.ppermute only.
A program may use at most 256 MiB of HBM per device.

v0:
```python
import jax
import jax.numpy as jnp
from jax import lax
from jax.sharding import PartitionSpec as P

HEADS_A = 12
HEADS_I = 16
LEN = 228
IMG_LEN = 256
MICRO = 2
STEP = 7


HIGHEST = lax.Precision.HIGHEST
NORM_EPS = 1e-06
LOGIT_SCALE = 50.0
CLIP_NORM = 0.01
BETA_ONE = 0.9
BETA_TWO = 0.999
ADAM_EPS = 1e-08
WEIGHT_DECAY = 0.1
RATE_MATRIX = 0.05
RATE_GAIN = 0.3


def to_low(value_in):
    return value_in.astype(jnp.bfloat16)


def normed(resid, gain):
    center = resid - jnp.mean(resid, axis=-1, keepdims=True)
    spread = jnp.mean(center * center, axis=-1, keepdims=True)
    return center * lax.rsqrt(spread + NORM_EPS) * gain


def unit_rows(embed_raw):
    return embed_raw * lax.rsqrt(jnp.sum(embed_raw * embed_raw, axis=-1, keepdims=True) + NORM_EPS)


def matmul(left, right):
    return jnp.einsum("cld,de->cle", left, right, preferred_element_type=jnp.float32)


def matmul_back(left, right):
    return jnp.einsum("cle,de->cld", left, right, preferred_element_type=jnp.float32)


def outer_sum(left, right):
    return jnp.einsum("cld,cle->de", left, right, preferred_element_type=jnp.float32)


def attend(query, keyed, valid, score_scale):
    scores = (
        jnp.einsum("clhd,cmhd->chlm", query, keyed, preferred_element_type=jnp.float32)
        * score_scale
    )
    return jnp.where(valid[:, None, None, :], scores, -1e30)


def layer_forward(resid_in, weights, norm_gains, valid, heads):
    w_qkv, w_out, w_up, w_down = weights
    clip_count, length, feature = resid_in.shape
    head_dim = feature // heads
    h_one = to_low(normed(resid_in, norm_gains[0]))
    qkv = to_low(matmul(h_one, w_qkv)).reshape(clip_count, length, 3, heads, head_dim)
    scores = attend(qkv[:, :, 0], qkv[:, :, 1], valid, head_dim ** (-0.5))
    log_total = jax.nn.logsumexp(scores, axis=-1, keepdims=True)
    attn_probs = jnp.exp(scores - log_total)
    attn_mixed = jnp.einsum(
        "chlm,cmhd->clhd", to_low(attn_probs), qkv[:, :, 2], preferred_element_type=jnp.float32
    )
    attn_mixed = to_low(attn_mixed.reshape(clip_count, length, feature))
    resid_mid = resid_in + matmul(attn_mixed, w_out)
    h_two = to_low(normed(resid_mid, norm_gains[1]))
    pre_act = matmul(h_two, w_up)
    hidden = to_low(jax.nn.gelu(pre_act))
    resid_out = resid_mid + matmul(hidden, w_down)
    return (
        resid_out,
        (h_one, qkv, log_total, attn_mixed, resid_mid, h_two, pre_act, hidden, resid_out),
    )


def pool_embed(resid_out, gain, pool_weight, w_proj):
    pooled = jnp.sum(normed(resid_out, gain) * pool_weight[:, :, None], axis=1)
    embed_raw = jnp.dot(to_low(pooled), w_proj, preferred_element_type=jnp.float32)
    return (unit_rows(embed_raw), pooled, embed_raw)


def contrast(audio, image, ids):
    logits = jnp.dot(audio, image.T, precision=HIGHEST) * LOGIT_SCALE
    count_rows = ids.shape[0]
    same = jnp.arange(count_rows)[:, None] == jnp.arange(count_rows)[None, :]
    allowed = jnp.logical_or(ids[:, None] != ids[None, :], same)
    masked = jnp.where(allowed, logits, -1e30)
    matched = jnp.sum(jnp.where(same, logits, 0.0), axis=1)
    row_lse = jax.nn.logsumexp(masked, axis=1)
    col_lse = jax.nn.logsumexp(masked, axis=0)
    return jnp.sum(row_lse - matched) + jnp.sum(col_lse - matched)


def audio_backward(
    d_embed, patches, resid_in, kept, pooled, embed_raw, weights, norm_gains, valid, pool_weight
):
    w_patch, w_qkv, w_out, w_up, w_down, w_proj = weights
    h_one, qkv, log_total, attn_mixed, resid_mid, h_two, pre_act, hidden, resid_out = kept
    clip_count, length, feature = resid_in.shape
    head_dim = feature // HEADS_A
    score_scale = head_dim ** (-0.5)
    d_raw = to_low(jax.vjp(unit_rows, embed_raw)[1](d_embed)[0])
    g_proj = jnp.dot(to_low(pooled).T, d_raw, preferred_element_type=jnp.float32)
    d_pooled = jnp.dot(d_raw, w_proj.T, preferred_element_type=jnp.float32)
    d_normed = d_pooled[:, None, :] * pool_weight[:, :, None]
    d_out, g_three = jax.vjp(normed, resid_out, norm_gains[2])[1](d_normed)
    d_low = to_low(d_out)
    g_down = outer_sum(hidden, d_low)
    d_hidden = matmul_back(d_low, w_down)
    d_pre = to_low(jax.vjp(jax.nn.gelu, pre_act)[1](d_hidden)[0])
    g_up = outer_sum(h_two, d_pre)
    d_ln_two, g_two = jax.vjp(normed, resid_mid, norm_gains[1])[1](matmul_back(d_pre, w_up))
    d_mid = d_out + d_ln_two
    d_mid_low = to_low(d_mid)
    g_out = outer_sum(attn_mixed, d_mid_low)
    d_mixed = to_low(matmul_back(d_mid_low, w_out)).reshape(clip_count, length, HEADS_A, head_dim)
    query, keyed, values_h = (qkv[:, :, 0], qkv[:, :, 1], qkv[:, :, 2])
    attn_probs = jnp.exp(attend(query, keyed, valid, score_scale) - log_total)
    d_probs = jnp.einsum("clhd,cmhd->chlm", d_mixed, values_h, preferred_element_type=jnp.float32)
    d_values = jnp.einsum(
        "chlm,clhd->cmhd", to_low(attn_probs), d_mixed, preferred_element_type=jnp.float32
    )
    d_scores = to_low(
        attn_probs * (d_probs - jnp.sum(attn_probs * d_probs, axis=-1, keepdims=True))
    )
    d_query = (
        jnp.einsum("chlm,cmhd->clhd", d_scores, keyed, preferred_element_type=jnp.float32)
        * score_scale
    )
    d_keyed = (
        jnp.einsum("chlm,clhd->cmhd", d_scores, query, preferred_element_type=jnp.float32)
        * score_scale
    )
    d_qkv = to_low(
        jnp.stack([d_query, d_keyed, d_values], axis=2).reshape(clip_count, length, 3 * feature)
    )
    g_qkv = outer_sum(h_one, d_qkv)
    d_ln_one, g_one = jax.vjp(normed, resid_in, norm_gains[0])[1](matmul_back(d_qkv, w_qkv))
    d_in = to_low(d_mid + d_ln_one)
    g_patch = outer_sum(patches, d_in)
    return (g_patch, g_qkv, g_out, g_up, g_down, g_proj, jnp.stack([g_one, g_two, g_three]))


def adam_step(weight, gradient, moment_one, moment_two, step_rate, decay):
    first_new = BETA_ONE * moment_one + (1.0 - BETA_ONE) * gradient
    second_new = BETA_TWO * moment_two + (1.0 - BETA_TWO) * gradient * gradient
    fixed_one = first_new / (1.0 - BETA_ONE**STEP)
    fixed_two = second_new / (1.0 - BETA_TWO**STEP)
    update = fixed_one / (jnp.sqrt(fixed_two) + ADAM_EPS) + decay * weight
    return (weight - step_rate * update, first_new, second_new)


def local(
    audio_patches,
    clip_lengths,
    video_ids,
    image_tokens,
    i_qkv,
    i_out,
    i_up,
    i_down,
    i_proj,
    i_gains,
    a_patch,
    a_qkv,
    a_out,
    a_up,
    a_down,
    a_proj,
    a_gains,
    m_patch,
    m_qkv,
    m_out,
    m_up,
    m_down,
    m_proj,
    m_gains,
    s_patch,
    s_qkv,
    s_out,
    s_up,
    s_down,
    s_proj,
    s_gains,
):
    masters = (a_patch, a_qkv, a_out, a_up, a_down, a_proj, a_gains)
    firsts = (m_patch, m_qkv, m_out, m_up, m_down, m_proj, m_gains)
    seconds = (s_patch, s_qkv, s_out, s_up, s_down, s_proj, s_gains)
    all_ids = lax.all_gather(video_ids, ("dp", "rep"), axis=1, tiled=True)
    image_w = (
        lax.all_gather(i_qkv, "dp", axis=0, tiled=True),
        lax.all_gather(i_out, "dp", axis=0, tiled=True),
        lax.all_gather(i_up, "dp", axis=0, tiled=True),
        lax.all_gather(i_down, "dp", axis=0, tiled=True),
        lax.all_gather(i_proj, "dp", axis=0, tiled=True),
        lax.all_gather(i_gains, "dp", axis=1, tiled=True),
    )
    image_g = image_w[5].astype(jnp.float32)
    count_rows = all_ids.shape[1]
    same = jnp.arange(count_rows)[:, None] == jnp.arange(count_rows)[None, :]
    allowed = jnp.logical_or(all_ids[:, :, None] != all_ids[:, None, :], same[None])
    loss_scale = count_rows / jnp.sum(allowed.astype(jnp.float32))
    copies = tuple((to_low(w) for w in masters))
    clip_dev = audio_patches.shape[1]
    start_row = lax.axis_index(("dp", "rep")) * clip_dev
    image_valid = jnp.ones((clip_dev, IMG_LEN), dtype=bool)
    image_pool = jnp.ones((clip_dev, IMG_LEN), jnp.float32) / IMG_LEN
    positions = jnp.arange(LEN)
    loss_sum = 0.0
    accum = None
    for micro in range(MICRO):
        gathered = (
            lax.all_gather(copies[0], "dp", axis=0, tiled=True),
            lax.all_gather(copies[1], "dp", axis=0, tiled=True),
            lax.all_gather(copies[2], "dp", axis=0, tiled=True),
            lax.all_gather(copies[3], "dp", axis=0, tiled=True),
            lax.all_gather(copies[4], "dp", axis=0, tiled=True),
            lax.all_gather(copies[5], "dp", axis=0, tiled=True),
            lax.all_gather(copies[6], "dp", axis=1, tiled=True),
        )
        gains_now = gathered[6].astype(jnp.float32)
        lengths_now = clip_lengths[micro]
        valid = positions[None, :] < lengths_now[:, None]
        pool_weight = valid.astype(jnp.float32) / lengths_now[:, None].astype(jnp.float32)
        patches = audio_patches[micro]
        resid_in = matmul(patches, gathered[0])
        resid_out, kept = layer_forward(resid_in, gathered[1:5], gains_now, valid, HEADS_A)
        audio_embed, pooled, embed_raw = pool_embed(
            resid_out, gains_now[2], pool_weight, gathered[5]
        )
        image_out, unused = layer_forward(
            image_tokens[micro].astype(jnp.float32), image_w[:4], image_g, image_valid, HEADS_I
        )
        image_embed, unused_pool, unused_raw = pool_embed(
            image_out, image_g[2], image_pool, image_w[4]
        )
        audio_all, image_all = (
            lax.all_gather(to_low(audio_embed), ("dp", "rep"), axis=0, tiled=True),
            lax.all_gather(to_low(image_embed), ("dp", "rep"), axis=0, tiled=True),
        )
        image_full = image_all.astype(jnp.float32)
        ids_now = all_ids[micro]

        def micro_loss(audio_in):
            return contrast(audio_in, image_full, ids_now)

        part_loss, contrast_back = jax.vjp(micro_loss, audio_all.astype(jnp.float32))
        loss_sum = loss_sum + part_loss
        d_all = contrast_back(loss_scale)[0]
        d_embed = lax.dynamic_slice_in_dim(d_all, start_row, clip_dev, 0)
        back_weights = (
            lax.all_gather(copies[0], "dp", axis=0, tiled=True),
            lax.all_gather(copies[1], "dp", axis=0, tiled=True),
            lax.all_gather(copies[2], "dp", axis=0, tiled=True),
            lax.all_gather(copies[3], "dp", axis=0, tiled=True),
            lax.all_gather(copies[4], "dp", axis=0, tiled=True),
            lax.all_gather(copies[5], "dp", axis=0, tiled=True),
            lax.all_gather(copies[6], "dp", axis=1, tiled=True),
        )
        grads = audio_backward(
            d_embed,
            patches,
            resid_in,
            kept,
            pooled,
            embed_raw,
            back_weights[:6],
            gains_now,
            valid,
            pool_weight,
        )
        shards = (
            lax.psum_scatter(grads[0], "dp", scatter_dimension=0, tiled=True),
            lax.psum_scatter(grads[1], "dp", scatter_dimension=0, tiled=True),
            lax.psum_scatter(grads[2], "dp", scatter_dimension=0, tiled=True),
            lax.psum_scatter(grads[3], "dp", scatter_dimension=0, tiled=True),
            lax.psum_scatter(grads[4], "dp", scatter_dimension=0, tiled=True),
            lax.psum_scatter(grads[5], "dp", scatter_dimension=0, tiled=True),
            lax.psum_scatter(grads[6], "dp", scatter_dimension=1, tiled=True),
        )
        accum = shards if accum is None else tuple((a + b for a, b in zip(accum, shards)))
    summed = lax.psum(accum, "rep")
    local_squares = sum((jnp.sum(g * g) for g in summed))
    grad_norm = jnp.sqrt(lax.psum(local_squares, "dp"))
    factor = jnp.minimum(1.0, CLIP_NORM / grad_norm)
    results = []
    for index in range(7):
        step_rate = RATE_GAIN if index == 6 else RATE_MATRIX
        decay = 0.0 if index == 6 else WEIGHT_DECAY
        results.append(
            adam_step(
                masters[index],
                summed[index] * factor,
                firsts[index],
                seconds[index],
                step_rate,
                decay,
            )
        )
    new_w = tuple((r[0] for r in results))
    new_one = tuple((r[1] for r in results))
    new_two = tuple((r[2] for r in results))
    loss = loss_sum * loss_scale
    return (
        loss,
        grad_norm,
        new_w[0],
        new_w[1],
        new_w[2],
        new_w[3],
        new_w[4],
        new_w[5],
        new_w[6],
        new_one[0],
        new_one[1],
        new_one[2],
        new_one[3],
        new_one[4],
        new_one[5],
        new_one[6],
        new_two[0],
        new_two[1],
        new_two[2],
        new_two[3],
        new_two[4],
        new_two[5],
        new_two[6],
    )


def solution(mesh):
    placed = (
        P(None, ("dp", "rep"), None, None),
        P(None, ("dp", "rep")),
        P(None, ("dp", "rep")),
        P(None, ("dp", "rep"), None, None),
        P("dp", None),
        P("dp", None),
        P("dp", None),
        P("dp", None),
        P("dp", None),
        P(None, "dp"),
        P("dp", None),
        P("dp", None),
        P("dp", None),
        P("dp", None),
        P("dp", None),
        P("dp", None),
        P(None, "dp"),
        P("dp", None),
        P("dp", None),
        P("dp", None),
        P("dp", None),
        P("dp", None),
        P("dp", None),
        P(None, "dp"),
        P("dp", None),
        P("dp", None),
        P("dp", None),
        P("dp", None),
        P("dp", None),
        P("dp", None),
        P(None, "dp"),
    )
    return jax.shard_map(
        local,
        mesh=mesh,
        in_specs=placed,
        out_specs=(
            P(),
            P(),
            P("dp", None),
            P("dp", None),
            P("dp", None),
            P("dp", None),
            P("dp", None),
            P("dp", None),
            P(None, "dp"),
            P("dp", None),
            P("dp", None),
            P("dp", None),
            P("dp", None),
            P("dp", None),
            P("dp", None),
            P(None, "dp"),
            P("dp", None),
            P("dp", None),
            P("dp", None),
            P("dp", None),
            P("dp", None),
            P("dp", None),
            P(None, "dp"),
        ),
        check_vma=False,
    )
```

profile of v0, /device:TPU:0, one launch (start us, length us, event | category | flops | bytes accessed | tf_op | source)
XLA Modules:
  0.0 1388.9 jit_solution(7028372803511178560)
XLA Ops:
  17.8 12.7 all_gather.72
  31.3 8.8 all-gather.1
  55.1 68.0 %all-gather = s32[32,2,2]{2,1,0:T(2,128)S(1)} all-gather(s32[1,2,2]{2,1,0:T(2,128)S(1)} %bitcast.448), channel_id=1, replica_groups=mesh['dp'=8,'rep'=4] {'dp','rep'}, dimensions={0}, use_global_device_ids=true | all-gather | bytes 528 | tf_op jit(solution)/shard_map/all_gather | solution.py:197
  190.0 67.5 %all-gather.2 = bf16[32,2,1024]{2,1,0:T(2,128)(2,1)S(1)} all-gather(bf16[1,2,1024]{2,1,0:T(2,128)(2,1)S(1)} %fusion.251), channel_id=1, replica_groups=mesh['dp'=8,'rep'=4] {'dp','rep'}, dimensions={0}, use_global_device_ids=true | all-gather | bytes 135168 | tf_op jit(solution)/shard_map/all_gather | solution.py:246
  257.6 11.4 fusion.28
  291.6 12.1 fusion.31
  322.3 37.6 %all-gather.32.cloned.1.call-done = bf16[1280,5120]{1,0:T(8,128)(2,1)} async-done(((bf16[160,5120]{1,0:T(8,128)(2,1)}), bf16[1280,5120]{1,0:T(8,128)(2,1)}) %all-gather.32.cloned.1.call-update) | async-done | bytes 13107216 | tf_op jit(solution)/shard_map/all_gather | solution.py:201
  359.9 76.3 %all-gather.34.cloned.1.call-done = bf16[5120,1280]{1,0:T(8,128)(2,1)} async-done(((bf16[640,1280]{1,0:T(8,128)(2,1)}), bf16[5120,1280]{1,0:T(8,128)(2,1)}) %all-gather.34.cloned.1.call-update) | async-done | bytes 13107216 | tf_op jit(solution)/shard_map/all_gather | solution.py:202
  436.2 26.1 %fusion.333 = (f32[2,256]{1,0:T(2,128)S(1)}, f32[2,256,1280]{2,1,0:T(8,128)}) fusion(f32[2,256,1280]{2,1,0:T(8,128)} %copy-done.26, bf16[5120,1280]{1,0:T(8,128)(2,1)} %all-gather.34.cloned.1.call-done, bf16[1280,5120]{1,0:T(8,128)(2,1)} %all-gather.32.cloned.1.call-done, f32[1280]{0:T(1024)S(1)} %get-tuple-element.142, f32[2,256]{1,0:T(2,128)S(1)} %add_rsqrt_fusion.4, ...), kind=kOutput, calls=%fused_computation.521 | convolution fusion | flops 13449297920 | bytes 31468544 | tf_op jit(solution)/shard_map/cld,de->cle/dot_general | solution.py:41
  464.5 26.0 %fusion.329 = (f32[2,256]{1,0:T(2,128)S(1)}, f32[2,256,1280]{2,1,0:T(8,128)}) fusion(f32[2,256,1280]{2,1,0:T(8,128)} %copy-done.27, bf16[5120,1280]{1,0:T(8,128)(2,1)} %all-gather.34.cloned.1.call-done, bf16[1280,5120]{1,0:T(8,128)(2,1)} %all-gather.32.cloned.1.call-done, f32[2,256]{1,0:T(2,128)S(1)} %add_rsqrt_fusion.1, ...), kind=kOutput, calls=%fused_computation.519 | convolution fusion | flops 13449297920 | bytes 31468544 | tf_op jit(solution)/shard_map/cld,de->cle/dot_general | solution.py:41
  498.2 68.3 %all-gather.4 = bf16[32,2,1024]{2,1,0:T(2,128)(2,1)S(1)} all-gather(bf16[1,2,1024]{2,1,0:T(2,128)(2,1)S(1)} %fusion.252), channel_id=1, replica_groups=mesh['dp'=8,'rep'=4] {'dp','rep'}, dimensions={0}, use_global_device_ids=true | all-gather | bytes 135168 | tf_op jit(solution)/shard_map/all_gather | solution.py:247
  573.1 64.3 %all-gather.6 = bf16[32,2,1024]{2,1,0:T(2,128)(2,1)S(1)} all-gather(bf16[1,2,1024]{2,1,0:T(2,128)(2,1)S(1)} %fusion.254), channel_id=1, replica_groups=mesh['dp'=8,'rep'=4] {'dp','rep'}, dimensions={0}, use_global_device_ids=true | all-gather | bytes 135168 | tf_op jit(solution)/shard_map/all_gather | solution.py:247
  638.0 66.8 %all-gather.5 = bf16[32,2,1024]{2,1,0:T(2,128)(2,1)S(1)} all-gather(bf16[1,2,1024]{2,1,0:T(2,128)(2,1)S(1)} %fusion.253), channel_id=1, replica_groups=mesh['dp'=8,'rep'=4] {'dp','rep'}, dimensions={0}, use_global_device_ids=true | all-gather | bytes 135168 | tf_op jit(solution)/shard_map/all_gather | solution.py:246
  718.6 8.8 fusion.47
  813.2 9.9 bitcast_add_fusion
  835.9 29.7 %reduce-scatter.14.cloned.1.call-done = f32[96,768]{1,0:T(8,128)} async-done(((f32[768,768]{1,0:T(8,128)}), f32[96,768]{1,0:T(8,128)}) %reduce-scatter.14.cloned.1.call-update) | async-done | bytes 294928 | tf_op jit(solution)/shard_map/reduce_scatter | solution.py:283
  865.6 50.0 %reduce-scatter.20.cloned.1.call-done = f32[96,1024]{1,0:T(8,128)} async-done(((f32[768,1024]{1,0:T(8,128)}), f32[96,1024]{1,0:T(8,128)}) %reduce-scatter.20.cloned.1.call-update) | async-done | bytes 393232 | tf_op jit(solution)/shard_map/reduce_scatter | solution.py:286
  915.6 68.9 %reduce-scatter.12.cloned.1.call-done = f32[96,2304]{1,0:T(8,128)} async-done(((f32[768,2304]{1,0:T(8,128)}), f32[96,2304]{1,0:T(8,128)}) %reduce-scatter.12.cloned.1.call-update) | async-done | bytes 884752 | tf_op jit(solution)/shard_map/reduce_scatter | solution.py:282
  984.5 80.3 %reduce-scatter.18.cloned.1.call-done = f32[384,768]{1,0:T(8,128)} async-done(((f32[3072,768]{1,0:T(8,128)}), f32[384,768]{1,0:T(8,128)}) %reduce-scatter.18.cloned.1.call-update) | async-done | bytes 1179664 | tf_op jit(solution)/shard_map/reduce_scatter | solution.py:285
  1064.8 80.3 %reduce-scatter.16.cloned.1.call-done = f32[96,3072]{1,0:T(8,128)} async-done(((f32[768,3072]{1,0:T(8,128)}), f32[96,3072]{1,0:T(8,128)}) %reduce-scatter.16.cloned.1.call-update) | async-done | bytes 1179664 | tf_op jit(solution)/shard_map/reduce_scatter | solution.py:284
  1147.8 34.9 %reduce-scatter.24.cloned.1.call-done = f32[96,3]{1,0:T(8,128)} async-done(((f32[768,3]{1,0:T(8,128)}), f32[96,3]{1,0:T(8,128)}) %reduce-scatter.24.cloned.1.call-update) | async-done | bytes 1168
  1183.6 12.2 psum.62
  1196.3 140.8 %all-reduce.3.cloned.1.call-done = (f32[32,768]{1,0:T(8,128)}, f32[96,2304]{1,0:T(8,128)}, f32[96,768]{1,0:T(8,128)}, f32[96,3072]{1,0:T(8,128)}, f32[384,768]{1,0:T(8,128)}, /*index=5*/f32[96,1024]{1,0:T(8,128)}) async-done(((f32[32,768]{1,0:T(8,128)}, f32[96,2304]{1,0:T(8,128)}, f32[96,768]{1,0:T(8,128)}, f32[96,3072]{1,0:T(8,128)}, f32[384,768]{1,0:T(8,128)}, /*index=5*/f32[96,1024]{1,0:T(8,128)}), ...) | async-done | bytes 4030480 | tf_op jit(solution)/shard_map/psum | solution.py:290
  1350.7 14.2 %psum.63 = f32[]{:T(128)} all-reduce(f32[]{:T(128)S(6)} %add.527), channel_id=1, replica_groups=mesh['dp'=8,'rep'=4] {'dp'}, use_global_device_ids=true, to_apply=%region_105.106 | all-reduce | flops 1 | bytes 8 | tf_op jit(solution)/shard_map/psum | solution.py:292
  (553 shorter events, 285.3 us)
Async XLA Ops:
  7.2 118.6 %all-gather.18.cloned.1.call-start = ((), (), s32[]{:S(2)}) async-start(), calls=%async_computation.7 | async-start | bytes 3981312 | tf_op jit(solution)/shard_map/all_gather | solution.py:222
  9.4 135.7 %all-gather.20.cloned.1.call-start = ((), (), s32[]{:S(2)}) async-start(), calls=%async_computation.8 | async-start | bytes 1327104 | tf_op jit(solution)/shard_map/all_gather | solution.py:223
  11.1 155.2 %all-gather.22.cloned.1.call-start = ((), (), s32[]{:S(2)}) async-start(), calls=%async_computation.9 | async-start | bytes 5308416 | tf_op jit(solution)/shard_map/all_gather | solution.py:224
  12.1 161.7 %all-gather.24.cloned.1.call-start = ((), (), s32[]{:S(2)}) async-start(), calls=%async_computation.10 | async-start | bytes 5308416 | tf_op jit(solution)/shard_map/all_gather | solution.py:225
  13.1 175.0 %all-gather.26.cloned.1.call-start = ((), (), s32[]{:S(2)}) async-start(), calls=%async_computation.11 | async-start | bytes 1769472 | tf_op jit(solution)/shard_map/all_gather | solution.py:226
  13.9 243.7 %all-gather.28.cloned.1.call-start = ((), (), s32[]{:S(2)}) async-start(), calls=%async_computation.12 | async-start | bytes 11059200 | tf_op jit(solution)/shard_map/all_gather | solution.py:199
  14.4 269.7 %all-gather.30.cloned.1.call-start = ((), (), s32[]{:S(2)}) async-start(), calls=%async_computation.13 | async-start | bytes 3686400 | tf_op jit(solution)/shard_map/all_gather | solution.py:200
  15.2 344.7 %all-gather.32.cloned.1.call-start = ((), (), s32[]{:S(2)}) async-start(), calls=%async_computation.14 | async-start | bytes 14745600 | tf_op jit(solution)/shard_map/all_gather | solution.py:201
  16.0 420.2 %all-gather.34.cloned.1.call-start = ((), (), s32[]{:S(2)}) async-start(), calls=%async_computation.15 | async-start | bytes 14745600 | tf_op jit(solution)/shard_map/all_gather | solution.py:202
  16.7 479.1 %all-gather.36.cloned.1.call-start = ((), (), s32[]{:S(2)}) async-start(), calls=%async_computation.16 | async-start | bytes 2949120 | tf_op jit(solution)/shard_map/all_gather | solution.py:203
  17.3 818.6 %reduce-scatter.22.cloned.1.call-start = ((), (), s32[]{:S(2)}) async-start(), calls=%async_computation.22 | async-start | bytes 884736 | tf_op jit(solution)/shard_map/reduce_scatter | solution.py:281
  40.2 141.0 %copy-start.63 = (f32[768]{0:T(1024)}, f32[768]{0:T(1024)S(1)}, u32[]{:S(2)}) copy-start(f32[768]{0:T(1024)S(1)} %get-tuple-element.145) | copy-start | bytes 9220
  187.4 383.8 %copy-start.7 = (f32[2,228,768]{2,1,0:T(8,128)}, f32[2,228,768]{2,1,0:T(8,128)S(1)}, u32[]{:S(2)}) copy-start(f32[2,228,768]{2,1,0:T(8,128)S(1)} %get-tuple-element.211) | copy-start | bytes 4202500
  787.3 78.3 %reduce-scatter.14.cloned.1.call-start = ((), (), s32[]{:S(2)}) async-start(), calls=%async_computation.18 | async-start | bytes 2654208 | tf_op jit(solution)/shard_map/reduce_scatter | solution.py:283
  791.9 123.7 %reduce-scatter.20.cloned.1.call-start = ((), (), s32[]{:S(2)}) async-start(), calls=%async_computation.21 | async-start | bytes 3538944 | tf_op jit(solution)/shard_map/reduce_scatter | solution.py:286
  796.2 188.3 %reduce-scatter.12.cloned.1.call-start = ((), (), s32[]{:S(2)}) async-start(), calls=%async_computation.17 | async-start | bytes 7962624 | tf_op jit(solution)/shard_map/reduce_scatter | solution.py:282
  806.3 258.6 %reduce-scatter.18.cloned.1.call-start = ((), (), s32[]{:S(2)}) async-start(), calls=%async_computation.20 | async-start | bytes 10616832 | tf_op jit(solution)/shard_map/reduce_scatter | solution.py:285
  823.1 322.0 %reduce-scatter.16.cloned.1.call-start = ((), (), s32[]{:S(2)}) async-start(), calls=%async_computation.19 | async-start | bytes 10616832 | tf_op jit(solution)/shard_map/reduce_scatter | solution.py:284
  834.7 348.0 %reduce-scatter.24.cloned.1.call-start = ((), (), s32[]{:S(2)}) async-start(), calls=%async_computation.23 | async-start | bytes 442368
  835.8 501.3 %all-reduce.3.cloned.1.call-start = ((), (), s32[]{:S(2)}) async-start(), calls=%async_computation.24 | async-start | bytes 8060928 | tf_op jit(solution)/shard_map/psum | solution.py:290
  1145.1 220.5 %copy-start.128 = (f32[3,96]{1,0:T(4,128)S(1)}, f32[3,96]{1,0:T(4,128)}, u32[]{:S(2)}) copy-start(f32[3,96]{1,0:T(4,128)} %param.47) | copy-start | bytes 3460
  1145.1 220.5 %copy-start.130 = (f32[3,96]{1,0:T(4,128)S(1)}, f32[3,96]{1,0:T(4,128)}, u32[]{:S(2)}) copy-start(f32[3,96]{1,0:T(4,128)} %param.54) | copy-start | bytes 3460
  1145.1 220.5 %copy-start.131 = (f32[3,96]{1,0:T(4,128)S(1)}, f32[3,96]{1,0:T(4,128)}, u32[]{:S(2)}) copy-start(f32[3,96]{1,0:T(4,128)} %param.61) | copy-start | bytes 3460
  1145.2 221.1 %copy-start.61 = (f32[96,1024]{1,0:T(8,128)S(1)}, f32[96,1024]{1,0:T(8,128)}, u32[]{:S(2)}) copy-start(f32[96,1024]{1,0:T(8,128)} %param.46) | copy-start | bytes 1179652
  (141 other events, 1820.7 us)
Sparse Core Ops, SparseCore 0:
  10.5 38.2 all-gather.17
  51.2 24.0 all-gather.19
  77.8 38.9 all-gather.21
  119.1 38.9 all-gather.23
  160.4 25.6 all-gather.25
  187.9 60.9 all-gather.27
  250.8 32.8 all-gather.29
  285.5 74.3 all-gather.31
  361.8 74.3 all-gather.33
  437.9 30.1 all-gather.35
  787.4 32.4 reduce-scatter.21
  823.1 42.4 reduce-scatter.13
  869.4 46.2 reduce-scatter.19
  919.0 65.5 reduce-scatter.11
  988.3 76.4 reduce-scatter.17
  1068.6 76.4 reduce-scatter.15
  1148.9 33.7 reduce-scatter.23
  1185.6 151.4 all-reduce.2
where the time goes:
time: 1400 us; the launch traced here: 1390 us
  waiting for transfers between devices  602 us (43%)
  blocking collectives  391 us (28%)
  matrix products  252 us (18%)
  other arithmetic  62.3 us (4%)
  local copies, waits for them, and re-layouts  53.3 us (4%)
  between operations  27.9 us (2%)
    psum x1, waiting for transfers between devices, local(): summed = lax.psum(accum, 'rep')  141 us
    all_gather x2, blocking collectives, local(): lax.all_gather(to_low(audio_embed), ('dp', 'rep'), axis=0, tiled=True)  134 us
    all_gather x2, blocking collectives, local(): lax.all_gather(to_low(image_embed), ('dp', 'rep'), axis=0, tiled=True)  133 us
    dot_general x16, matrix products, matmul(): jnp.einsum('cld,de->cle', left, right, preferred_element_type=jnp.float32)  116 us
    reduce_scatter x1, waiting for transfers between devices, local(): lax.psum_scatter(grads[3], 'dp', scatter_dimension=0, tiled=True)  80.3 us
    reduce_scatter x1, waiting for transfers between devices, local(): lax.psum_scatter(grads[4], 'dp', scatter_dimension=0, tiled=True)  80.3 us
    all_gather x1, waiting for transfers between devices, local(): lax.all_gather(i_down, 'dp', axis=0, tiled=True)  76.3 us
    reduce_scatter x1, waiting for transfers between devices, local(): lax.psum_scatter(grads[1], 'dp', scatter_dimension=0, tiled=True)  68.9 us
  transfers between devices with their start and end apart: 18, of which 9 were waited for; matrix products, arithmetic and copies ran while one was open for 17% of the time, Pallas kernels for 0%

commit v1 on v0

v1 whole, which is shorter than its diff:
```python
import functools

import jax
import jax.numpy as jnp
from jax import lax
from jax.experimental import pallas as pl
from jax.experimental.pallas import tpu as pltpu
from jax.sharding import PartitionSpec as P

HEADS_A = 12
HEADS_I = 16
LEN = 228
IMG_LEN = 256
MICRO = 2
STEP = 7

HIGHEST = lax.Precision.HIGHEST
F32 = jnp.float32
BF16 = jnp.bfloat16
NORM_EPS = 1e-06
LOGIT_SCALE = 50.0
CLIP_NORM = 0.01
BETA_ONE = 0.9
BETA_TWO = 0.999
ADAM_EPS = 1e-08
WEIGHT_DECAY = 0.1
RATE_MATRIX = 0.05
RATE_GAIN = 0.3
PAD_LEN = 240
GELU_C = 0.7978845608028654
GELU_A = 0.044715
MIB = 1 << 20


def to_low(v):
    return v.astype(BF16)


def normed(resid, gain):
    center = resid - jnp.mean(resid, axis=-1, keepdims=True)
    spread = jnp.mean(center * center, axis=-1, keepdims=True)
    return center * lax.rsqrt(spread + NORM_EPS) * gain


def unit_rows(embed_raw):
    return embed_raw * lax.rsqrt(jnp.sum(embed_raw * embed_raw, axis=-1, keepdims=True) + NORM_EPS)


def dot_f32(a, b):
    return lax.dot_general(a, b, (((1,), (0,)), ((), ())), preferred_element_type=F32)


def dot_nt(a, b):
    return lax.dot_general(a, b, (((1,), (1,)), ((), ())), preferred_element_type=F32)


def dot_tn(a, b):
    return lax.dot_general(a, b, (((0,), (0,)), ((), ())), preferred_element_type=F32)


class Group:
    def __init__(self, arrays, index, rows, cols):
        self.arrays, self.index, self.rows, self.cols = arrays, index, rows, cols


class Weight:
    def __init__(self, k, n, segs=None, sub=1, whole=None):
        self.k, self.n, self.segs, self.sub, self.whole = k, n, segs, sub, whole

    def groups(self):
        seen = []
        for seg in self.segs:
            if seg[0] not in seen:
                seen.append(seg[0])
        return seen

    def operands(self):
        if self.whole is not None:
            return [self.whole]
        return [v for g in self.groups() for v in g.arrays]

    def indices(self):
        return [] if self.whole is not None else [g.index for g in self.groups()]

    def entries(self, tn):
        groups, out = self.groups(), []
        for g, col, width, dst, part in self.segs:
            out += [(groups.index(g), col + t * tn, dst + t * tn, part) for t in range(width // tn)]
        return sorted(out, key=lambda e: (e[2], e[3]))


def start_weight(w, tn, refs, idx, wbuf, sem):
    if w.whole is not None:
        for t in range(w.n // tn):
            cols = pl.ds(t * tn, tn)
            pltpu.make_async_copy(refs[0].at[:, cols], wbuf.at[:, cols], sem.at[t, 0]).start()
        return
    for e, (gi, col, dst, part) in enumerate(w.entries(tn)):
        rows = w.groups()[gi].rows
        for p in range(8):
            at = pl.multiple_of(idx[gi][p] * (rows * w.sub) + part * rows, rows)
            pltpu.make_async_copy(
                refs[8 * gi + p].at[:, pl.ds(w.groups()[gi].cols[p] + col, tn)],
                wbuf.at[pl.ds(at, rows), pl.ds(dst, tn)],
                sem.at[e, p],
            ).start()


def wait_weight(w, tn, refs, idx, wbuf, sem, t):
    cols = pl.ds(pl.multiple_of(t * tn, tn), tn)
    if w.whole is not None:
        pltpu.make_async_copy(refs[0].at[:, pl.ds(0, tn)], wbuf.at[:, cols], sem.at[t, 0]).wait()
        return
    rows = w.groups()[0].rows
    for part in range(w.sub):
        for p in range(8):
            pltpu.make_async_copy(
                refs[p].at[:, pl.ds(0, tn)], wbuf.at[pl.ds((p * w.sub + part) * rows, rows), cols],
                sem.at[t * w.sub + part, p],
            ).wait()


def weight_sems(w, tn):
    tiles = w.n // tn
    return pltpu.SemaphoreType.DMA((tiles, 1) if w.whole is not None else (tiles * w.sub, 8))


HBM = pltpu.MemorySpace.HBM


def hbm_spec():
    return pl.BlockSpec(memory_space=HBM)


def full_spec(shape):
    return pl.BlockSpec(shape, lambda *_: (0,) * len(shape))


def run_kernel(body, name, grid, scalars, ins, weights, outs, scratch, limit, flops):
    scal = list(scalars)
    for w, _ in weights:
        scal += w.indices()
    n_scal, n_user = len(scal), len(scalars)
    operands = [a for a, _ in ins]
    specs = [s for _, s in ins]
    for w, _ in weights:
        ops = w.operands()
        operands += ops
        specs += [hbm_spec()] * len(ops)
    n_in = len(ins)
    scr = list(scratch)
    for w, tn in weights:
        scr += [pltpu.VMEM((w.k, w.n), BF16), weight_sems(w, tn)]

    def kernel(*refs):
        s = refs[:n_scal]
        user_s, s = s[:n_user], s[n_user:]
        pos = n_scal
        in_refs = refs[pos : pos + n_in]
        pos += n_in
        w_refs = []
        for w, _ in weights:
            m = len(w.operands())
            w_refs.append(refs[pos : pos + m])
            pos += m
        out_refs = refs[pos : pos + len(outs)]
        pos += len(outs)
        scr_refs = refs[pos : pos + len(scratch)]
        pos += len(scratch)
        handles = []
        si = 0
        for wi, (w, tn) in enumerate(weights):
            gi = len(w.indices())
            handles.append((w, tn, w_refs[wi], s[si : si + gi], refs[pos], refs[pos + 1]))
            si += gi
            pos += 2
        first = pl.program_id(0) == 0

        @pl.when(first)
        def _():
            for h in handles:
                start_weight(*h)

        def wait(k, t):
            @pl.when(first)
            def _():
                wait_weight(*handles[k], t)

        body(user_s, in_refs, out_refs, scr_refs, [h[4] for h in handles], wait)

    bytes_acc = sum(int(a.size) * a.dtype.itemsize for a in operands) + sum(
        functools.reduce(lambda x, y: x * y, o[0], 1) * jnp.dtype(o[1]).itemsize for o in outs
    )
    return pl.pallas_call(
        kernel,
        grid_spec=pltpu.PrefetchScalarGridSpec(
            num_scalar_prefetch=n_scal,
            grid=grid,
            in_specs=specs,
            out_specs=[o[2] for o in outs],
            scratch_shapes=scr,
        ),
        out_shape=[jax.ShapeDtypeStruct(o[0], o[1]) for o in outs],
        compiler_params=pltpu.CompilerParams(vmem_limit_bytes=limit * MIB),
        cost_estimate=pl.CostEstimate(flops=flops, bytes_accessed=bytes_acc, transcendentals=0),
        name=name,
    )(*scal, *operands)


def rows_spec(length, width):
    return pl.BlockSpec((length, width), lambda i, *_: (i, 0))


def emitted(w, keep=True):
    return [((w.k, w.n), BF16, full_spec((w.k, w.n)))] if keep and w.whole is None else []


def emit_weight(w, outs, at, wbuf, keep=True, step=0):
    if keep and w.whole is None:

        @pl.when(pl.program_id(0) == step)
        def _():
            outs[at][...] = wbuf[...]


def take_weight(w, results, at):
    return w.whole if w.whole is not None else results[at]


def image_qkv(tokens, gains, w, clips, length, tn):
    d, n = w.k, w.n

    def body(_s, ins, outs, _scr, wb, wait):
        h = to_low(normed(ins[0][...].astype(F32), ins[1][0:1, :]))

        def step(t, c):
            wait(0, t)
            at = pl.ds(pl.multiple_of(t * tn, tn), tn)
            outs[0][:, at] = to_low(dot_f32(h, wb[0][:, at]))
            return c

        lax.fori_loop(0, n // tn, step, 0)

    return run_kernel(
        body, "image_qkv", (clips,), [],
        [(tokens, rows_spec(length, d)), (gains, full_spec((3, d)))], [(w, tn)],
        [((clips * length, n), BF16, rows_spec(length, n))], [], 40, 2 * clips * length * d * n,
    )[0]


def audio_in(patches, w_patch, gains, w, clips, length, tn):
    d, n, pk = w.k, w.n, w_patch.shape[0]

    def body(_s, ins, outs, _scr, wb, wait):
        x0 = dot_f32(ins[0][...], ins[1][...])
        outs[0][...] = x0
        h = to_low(normed(x0, ins[2][0:1, :]))
        outs[1][...] = h

        def step(t, c):
            wait(0, t)
            at = pl.ds(pl.multiple_of(t * tn, tn), tn)
            outs[2][:, at] = to_low(dot_f32(h, wb[0][:, at]))
            return c

        lax.fori_loop(0, n // tn, step, 0)

        emit_weight(w, outs, 3, wb[0])

    m = clips * length
    return run_kernel(
        body, "audio_in", (clips,), [],
        [(patches, rows_spec(length, pk)), (w_patch, full_spec((pk, d))), (gains, full_spec((3, d)))], [(w, tn)],
        [((m, d), F32, rows_spec(length, d)), ((m, d), BF16, rows_spec(length, d)),
         ((m, n), BF16, rows_spec(length, n))] + emitted(w),
        [], 40, 2 * m * d * (n + pk),
    )


def attn_forward(qkv, lengths, clips, length, heads, masked):
    d = qkv.shape[1] // 3
    hd = d // heads
    scale = hd ** (-0.5)
    tiles = d // 128

    def body(s_refs, ins, outs, _scr, _wb, _wait):
        qkv_ref, out = ins[0], outs[0]
        lane = lax.broadcasted_iota(jnp.int32, (1, 128), 1)
        if masked:
            keys = lax.broadcasted_iota(jnp.int32, (1, length), 1)
            ok = keys < s_refs[0][pl.program_id(0)]
        acc = {}
        for h in range(heads):
            lo, hi = h * hd, (h + 1) * hd
            t0, t1 = lo // 128, (hi - 1) // 128
            wide = (t1 - t0 + 1) * 128
            at = slice(t0 * 128, t0 * 128 + wide)
            col = lax.broadcasted_iota(jnp.int32, (1, wide), 1) + t0 * 128
            mine = (col >= lo) & (col < hi)
            q = qkv_ref[:, at]
            q = jnp.where(mine, q, jnp.zeros_like(q))
            k = qkv_ref[:, d + t0 * 128 : d + t0 * 128 + wide]
            v = qkv_ref[:, 2 * d + t0 * 128 : 2 * d + t0 * 128 + wide]
            sc = dot_nt(q, k) * scale
            if masked:
                sc = jnp.where(ok, sc, -1e30)
            e = jnp.exp(sc - jnp.max(sc, axis=-1, keepdims=True))
            p = to_low(e * (1.0 / jnp.sum(e, axis=-1, keepdims=True)))
            o = dot_f32(p, v)
            for t in range(t0, t1 + 1):
                part = o[:, (t - t0) * 128 : (t - t0 + 1) * 128]
                full = lane + t * 128
                sel = (full >= lo) & (full < hi)
                acc[t] = jnp.where(sel, part, acc[t]) if t in acc else part
                if min((t + 1) * 128, d) <= hi:
                    out[:, t * 128 : (t + 1) * 128] = to_low(acc.pop(t))

    m = clips * length
    return run_kernel(
        body, "attn_forward", (clips,), [lengths], [(qkv, rows_spec(length, 3 * d))], [],
        [((m, d), BF16, rows_spec(length, d))], [], 32, 4 * m * length * 256 * heads,
    )[0]


def out_norm(mixed, resid, gains, w, clips, length, keep):
    d = w.n

    def body(_s, ins, outs, _scr, wb, wait):
        wait(0, 0)
        x1 = ins[1][...].astype(F32) + dot_f32(ins[0][...], wb[0][...])
        outs[0][...] = x1
        outs[1][...] = to_low(normed(x1, ins[2][1:2, :]))
        emit_weight(w, outs, 2, wb[0], keep)

    m = clips * length
    outs = [((m, d), F32, rows_spec(length, d)), ((m, d), BF16, rows_spec(length, d))] + emitted(w, keep)
    return run_kernel(
        body, "out_norm", (clips,), [],
        [(mixed, rows_spec(length, d)), (resid, rows_spec(length, d)), (gains, full_spec((3, d)))], [(w, d)],
        outs, [], 32, 2 * m * d * d,
    )


def gelu_parts(z):
    zz = z * z
    t = jnp.tanh(GELU_C * z * (1.0 + GELU_A * zz))
    half = 0.5 * (1.0 + t)
    return z * half, half, t, zz


def up_gelu(h_two, w, clips, length, tn, keep):
    d, n = w.k, w.n

    def body(_s, ins, outs, _scr, wb, wait):
        h = ins[0][...]

        def step(t, c):
            wait(0, t)
            at = pl.ds(pl.multiple_of(t * tn, tn), tn)
            z = dot_f32(h, wb[0][:, at])
            u, half, tz, zz = gelu_parts(z)
            outs[0][:, at] = to_low(u)
            if keep:
                slope = half + z * (0.5 * GELU_C) * (1.0 - tz * tz) * (1.0 + (3.0 * GELU_A) * zz)
                outs[1][:, at] = to_low(slope)
            return c

        lax.fori_loop(0, n // tn, step, 0)
        emit_weight(w, outs, 2, wb[0], keep)

    m = clips * length
    outs = [((m, n), BF16, rows_spec(length, n))]
    if keep:
        outs += [((m, n), BF16, rows_spec(length, n))] + emitted(w)
    return run_kernel(
        body, "up_gelu", (clips,), [], [(h_two, rows_spec(length, d))], [(w, tn)], outs, [], 44, 2 * m * d * n,
    )


def down_left(hidden, resid, w, clips, length, kt):
    k, n = w.k, w.n

    def body(_s, ins, outs, _scr, wb, wait):
        wait(0, 0)
        outs[0][...] = ins[1][...]

        def step(t, c):
            at = pl.ds(pl.multiple_of(t * kt, kt), kt)
            outs[0][...] += dot_f32(ins[0][:, at], wb[0][at, :])
            return c

        lax.fori_loop(0, k // kt, step, 0)

    m = clips * length
    return run_kernel(
        body, "down_left", (clips,), [], [(hidden, rows_spec(length, k)), (resid, rows_spec(length, n))],
        [(w, n)], [((m, n), F32, rows_spec(length, n))], [], 44, 2 * m * n * k,
    )[0]


def down_embed(hidden, resid, left, gains, lengths, w, w_proj, clips, length, kt, keep):
    d, k, pj, n = resid.shape[1], w.k, w_proj.n, w.n
    have = d - n

    def body(s_refs, ins, outs, scr, wb, wait):
        g = pl.program_id(0)
        wait(0, 0)
        if have:
            scr[0][:, :have] = ins[3][...]
        scr[0][:, have:] = ins[1][:, have:]

        def step(t, c):
            at = pl.ds(pl.multiple_of(t * kt, kt), kt)
            scr[0][:, have:] += dot_f32(ins[0][:, at], wb[0][at, :])
            return c

        lax.fori_loop(0, k // kt, step, 0)
        x2 = scr[0][...]
        size = s_refs[0][g]
        row = lax.broadcasted_iota(jnp.int32, (length, 1), 0)
        weight = jnp.where(row < size, 1.0 / size.astype(F32), 0.0)
        pooled = jnp.sum(normed(x2, ins[2][2:3, :]) * weight, axis=0, keepdims=True)
        scr[1][pl.ds(g, 1), :] = pooled
        if keep:
            outs[3][...] = x2
            emit_weight(w, outs, 4, wb[0])
            emit_weight(w_proj, outs, 5, wb[1], True, clips - 1)
        wait(1, 0)

        @pl.when(g == clips - 1)
        def _():
            pool_all = scr[1][...]
            raw = dot_f32(to_low(pool_all), wb[1][...])
            outs[0][...] = to_low(unit_rows(raw))
            outs[1][...] = raw
            outs[2][...] = pool_all

    m = clips * length
    outs = [((clips, pj), BF16, full_spec((clips, pj))), ((clips, pj), F32, full_spec((clips, pj))),
            ((clips, d), F32, full_spec((clips, d)))]
    if keep:
        outs += [((m, d), F32, rows_spec(length, d))] + emitted(w) + emitted(w_proj)
    ins = [(hidden, rows_spec(length, k)), (resid, rows_spec(length, d)), (gains, full_spec((3, d)))]
    if have:
        ins.append((left, rows_spec(length, have)))
    return run_kernel(
        body, "down_embed", (clips,), [lengths], ins, [(w, n), (w_proj, pj)], outs,
        [pltpu.VMEM((length, d), F32), pltpu.VMEM((clips, d), F32)], 44, 2 * m * n * k,
    )


def attn_backward(qkv, d_mixed, lengths, clips, length, heads):
    d = qkv.shape[1] // 3
    hd = d // heads
    scale = hd ** (-0.5)
    per = 128 // hd

    def body(s_refs, ins, outs, _scr, _wb, _wait):
        qkv_ref, do_ref, out = ins[0], ins[1], outs[0]
        lane = lax.broadcasted_iota(jnp.int32, (1, 128), 1)
        ok = lax.broadcasted_iota(jnp.int32, (1, length), 1) < s_refs[0][pl.program_id(0)]
        for t in range(d // 128):
            at = slice(t * 128, (t + 1) * 128)
            q, do = qkv_ref[:, at], do_ref[:, at]
            k = qkv_ref[:, d + t * 128 : d + (t + 1) * 128]
            v = qkv_ref[:, 2 * d + t * 128 : 2 * d + (t + 1) * 128]
            dq = dk = dv = None
            for h in range(per):
                mine = (lane >= h * hd) & (lane < (h + 1) * hd)
                qm = jnp.where(mine, q, jnp.zeros_like(q))
                dom = jnp.where(mine, do, jnp.zeros_like(do))
                sc = jnp.where(ok, dot_nt(qm, k) * scale, -1e30)
                e = jnp.exp(sc - jnp.max(sc, axis=-1, keepdims=True))
                p = e * (1.0 / jnp.sum(e, axis=-1, keepdims=True))
                dp = dot_nt(dom, v)
                ds = to_low(p * (dp - jnp.sum(p * dp, axis=-1, keepdims=True)))
                dv_h = dot_tn(to_low(p), do)
                dq_h = dot_f32(ds, k)
                dk_h = dot_tn(ds, q)
                dq = dq_h if dq is None else jnp.where(mine, dq_h, dq)
                dk = dk_h if dk is None else jnp.where(mine, dk_h, dk)
                dv = dv_h if dv is None else jnp.where(mine, dv_h, dv)
            out[:, at] = to_low(dq * scale)
            out[:, d + t * 128 : d + (t + 1) * 128] = to_low(dk * scale)
            out[:, 2 * d + t * 128 : 2 * d + (t + 1) * 128] = to_low(dv)

    m = clips * length
    return run_kernel(
        body, "attn_backward", (clips,), [lengths],
        [(qkv, rows_spec(length, 3 * d)), (d_mixed, rows_spec(length, d))], [],
        [((m, 3 * d), BF16, rows_spec(length, 3 * d))], [], 32, 10 * m * length * 256 * heads,
    )[0]


AXES = ("dp", "rep")


def joint_perm(reps, fn):
    out = []
    for dp in range(8):
        for z in range(reps):
            dst = fn(dp, z)
            if dst is not None:
                out.append((dp * reps + z, dst[0] * reps + dst[1]))
    return out


def send(value, reps, fn):
    return lax.ppermute(value, AXES, joint_perm(reps, fn))


class Ring:
    def __init__(self, packed, col, width, reps):
        self.own, self.col, self.width, self.reps = packed, col, width, reps
        self.mine = packed[:, col : col + width]

    def first(self):
        self.near = send(self.mine, self.reps, lambda dp, z: (dp ^ (2 if z % 2 == 0 else 4), z))

    def second(self):
        self.diag = send(self.near, self.reps, lambda dp, z: (dp ^ (4 if z % 2 == 0 else 2), z))
        self.other = send(self.near, self.reps, lambda dp, z: (dp, z ^ 1))

    def twin(self, *names):
        for name in names:
            setattr(self, name + "_twin", send(getattr(self, name), self.reps, lambda dp, z: (dp ^ 1, z)))

    def group(self, own_twin):
        odd = lax.axis_index("rep") % 2 == 1
        x, y = jnp.int32(2), jnp.int32(4)
        flip = jnp.stack([jnp.int32(0), jnp.where(odd, y, x), jnp.int32(6), jnp.where(odd, x, y)])
        base = jnp.bitwise_xor(flip, lax.axis_index("dp").astype(jnp.int32))
        arrays = [self.own, self.near, self.diag, self.other, own_twin, self.near_twin, self.diag_twin, self.other_twin]
        index = jnp.concatenate([base, jnp.bitwise_xor(base, 1)])
        return Group(arrays, index, self.own.shape[0], (self.col, 0, 0, 0) * 2)


def fence(held, values):
    flat = [(r, n) for r, names in held for n in names.split()]
    out = lax.optimization_barrier(tuple(getattr(r, n) for r, n in flat) + tuple(values))
    for (r, n), v in zip(flat, out):
        setattr(r, n, v)
    return out[len(flat) :]


def take(v, i, axis):
    return lax.dynamic_index_in_dim(v, i, axis, keepdims=False)


def in_width(v, width):
    n = v.shape[-1]
    blocks = [v[..., i * width : (i + 1) * width] for i in range(n // width)]
    rest = n % width
    if rest:
        last, k, rows = v[..., n - rest :], width // rest, v.shape[-2]
        blocks.append(jnp.concatenate(
            [last[..., i * (rows // k) : (i + 1) * (rows // k), :] for i in range(k)], axis=-1))
    return jnp.concatenate(blocks, axis=-2)


def from_width(v, rows, n):
    width = v.shape[-1]
    full = n // width
    blocks = [v[i * rows : (i + 1) * rows] for i in range(full)]
    rest = n % width
    if rest:
        last, k = v[full * rows :], width // rest
        blocks.append(jnp.concatenate([last[:, i * rest : (i + 1) * rest] for i in range(k)], axis=0))
    return jnp.concatenate(blocks, axis=1)


def reduce_group(grads, kind, reps, width):
    me, rep = lax.axis_index("dp"), lax.axis_index("rep")
    y, x, c = me // 4, (me // 2) % 2, me % 2
    split = [v.reshape(2, 2, 2, v.shape[0] // 8, v.shape[1]) for v in grads]
    pick = lambda i: jnp.concatenate([in_width(take(v, i, 2), width) for v in split], axis=-2)
    s = pick(c) + send(to_low(pick(1 - c)), reps, lambda dp, z: (dp ^ 1, z)).astype(F32)
    for step in ((0, 1) if kind == 0 else (1, 0)):
        bit, at, axis = ((2, x, s.ndim - 3), (4, y, 0))[step]
        got = send(to_low(take(s, 1 - at, axis)), reps, lambda dp, z: (dp ^ bit, z))
        s = take(s, at, axis) + got.astype(F32)
    low = to_low(s)
    got = send(low, reps, lambda dp, z: {0: (dp, 1), 3: (dp, 2)}.get(z))
    low = to_low(low.astype(F32) + got.astype(F32))
    got = send(low, reps, lambda dp, z: {1: (dp, 2), 2: (dp, 1)}.get(z))
    low = to_low(low.astype(F32) + got.astype(F32))
    got = send(low, reps, lambda dp, z: {1: (dp, 0), 2: (dp, 3)}.get(z))
    total = jnp.where((rep == 1) | (rep == 2), low, got).astype(F32)
    out, at = [], 0
    for v in split:
        rows, n = v.shape[-2:]
        size = rows * n // width
        out.append(from_width(total[at : at + size], rows, n))
        at += size
    return out


def adam_step(weight, gradient, moment_one, moment_two, step_rate, decay):
    first_new = BETA_ONE * moment_one + (1.0 - BETA_ONE) * gradient
    second_new = BETA_TWO * moment_two + (1.0 - BETA_TWO) * gradient * gradient
    fixed_one = first_new / (1.0 - BETA_ONE**STEP)
    fixed_two = second_new / (1.0 - BETA_TWO**STEP)
    update = fixed_one / (jnp.sqrt(fixed_two) + ADAM_EPS) + decay * weight
    return (weight - step_rate * update, first_new, second_new)


def as_columns(v, rows):
    return jnp.concatenate([v[i * rows : (i + 1) * rows] for i in range(v.shape[0] // rows)], axis=1)


def local(dp_size, rep_size, *args):
    (audio_patches, clip_lengths, video_ids, image_tokens, i_qkv, i_out, i_up, i_down, i_proj, i_gains) = args[:10]
    masters, firsts_in, seconds_in = args[10:17], args[17:24], args[24:31]
    a_patch, a_qkv, a_out, a_up, a_down, a_proj, a_gains = (to_low(w) for w in masters)
    fast = dp_size == 8 and rep_size == 4
    clip_dev = audio_patches.shape[1]
    clips = MICRO * clip_dev
    d_i, d_a, ff_a, pj = i_out.shape[1], a_out.shape[1], a_up.shape[1], a_proj.shape[1]
    ff_i = i_up.shape[1]

    rp = a_patch.shape[0]
    small = jnp.concatenate(
        [a_patch, jnp.pad(a_gains.reshape(1, -1), ((0, 0), (0, d_a - a_gains.size))),
         jnp.pad(i_gains.reshape(1, -1), ((0, 0), (0, d_a - i_gains.size)))], axis=0)
    small = lax.all_gather(small, "dp", axis=0)
    img_sizes = jnp.full((clips,), IMG_LEN, jnp.int32)
    tokens = image_tokens.reshape(clips * IMG_LEN, d_i)
    sizes = clip_lengths.reshape(clips)
    patches = jnp.pad(audio_patches.reshape(clips, LEN, -1), ((0, 0), (0, PAD_LEN - LEN), (0, 0)))
    patches = patches.reshape(clips * PAD_LEN, -1)
    half, sub_i, sub_a = ff_i // 2, ff_i // d_i, ff_a // d_a
    dl = d_i * 3 // 5
    fr = d_a * 8 // 3
    if fast:
        down_i, down_a = as_columns(i_down, i_qkv.shape[0]), as_columns(a_down, a_qkv.shape[0])
        left = [down_i[:, j * d_i : j * d_i + dl] for j in range(sub_i)]
        right = [down_i[:, j * d_i + dl : (j + 1) * d_i] for j in range(sub_i)]
        own_a = jnp.concatenate([a_qkv, a_out, a_up, down_a, a_proj], axis=1)
        own_i = jnp.concatenate([i_qkv, i_out, i_up, i_proj] + left + right, axis=1)
        small, own_a, own_i = lax.optimization_barrier((small, own_a, own_i))
        cut_a = 4 * d_a + fr
        ca = Ring(own_a, 0, cut_a, rep_size), Ring(own_a, cut_a, own_a.shape[1] - cut_a, rep_size)
        widths, at, ci = [3 * d_i, d_i + half, half + pj, sub_i * dl, sub_i * (d_i - dl)], 0, []
        for wd in widths:
            ci.append(Ring(own_i, at, wd, rep_size))
            at += wd
        swap = lambda v: send(v, rep_size, lambda dp, z: (dp ^ 1, z))
        twin_a, twin_i = swap(own_a), swap(own_i)

        ca[0].first()
        fence([(ca[0], "near"), (ca[1], "mine")], ())
        ca[0].second()
        ca[0].twin("near")
        ca[1].first()
        patches, twin_a = fence([(ca[0], "diag other near_twin"), (ca[1], "near"), (ci[0], "mine")], (patches, twin_a))
        ca[0].twin("diag", "other")
        ca[1].second()
        ca[1].twin("near")
        ci[0].first()
        ga0 = ca[0].group(twin_a)
        wa_qkv = Weight(d_a, 3 * d_a, [(ga0, 0, 3 * d_a, 0, 0)])
        wa_out = Weight(d_a, d_a, [(ga0, 3 * d_a, d_a, 0, 0)])
    else:
        whole = lambda v: lax.all_gather(v, "dp", axis=0, tiled=True)
        make = lambda v: Weight(v.shape[0] * dp_size, v.shape[1], whole=whole(v))
        cut = lambda v: Weight(v.shape[0], v.shape[1], whole=v)
        wi_qkv, wi_out, wi_up, wi_proj = (make(v) for v in (i_qkv, i_out, i_up, i_proj))
        wi_left, wi_right = cut(whole(i_down)[:, :dl]), cut(whole(i_down)[:, dl:])
        wa_qkv, wa_out, wa_up, wa_down, wa_proj = (make(v) for v in (a_qkv, a_out, a_up, a_down, a_proj))

    w_patch = small[:, :rp].reshape(rp * dp_size, d_a)
    unpack = lambda v, g: v[:, : g.size].reshape(dp_size, 3, -1).transpose(1, 0, 2).reshape(3, -1).astype(F32)
    gains_a, gains_i = unpack(small[:, rp], a_gains), unpack(small[:, rp + 1], i_gains)

    got = audio_in(patches, w_patch, gains_a, wa_qkv, clips, PAD_LEN, d_a)
    resid_in, h_one, qkv = got[:3]
    full_qkv = take_weight(wa_qkv, got, 3)
    mixed = attn_forward(qkv, sizes, clips, PAD_LEN, HEADS_A, True)
    got = out_norm(mixed, resid_in, gains_a, wa_out, clips, PAD_LEN, True)
    resid_mid, h_two = got[:2]
    full_out = take_weight(wa_out, got, 2)

    if fast:
        (h_two,) = fence([(ca[1], "diag other near_twin"), (ci[0], "near"), (ci[1], "mine")], (h_two,))
        ca[1].twin("diag", "other")
        ci[0].second()
        ci[0].twin("near")
        ci[1].first()
        ga1 = ca[1].group(twin_a)
        wa_up = Weight(d_a, ff_a, [(ga0, 4 * d_a, fr, 0, 0), (ga1, 0, ff_a - fr, fr, 0)])
        wa_down = Weight(ff_a, d_a, [(ga1, ff_a - fr + j * d_a, d_a, 0, j) for j in range(sub_a)], sub=sub_a)
        wa_proj = Weight(d_a, pj, [(ga1, 2 * ff_a - fr, pj, 0, 0)])
    got = up_gelu(h_two, wa_up, clips, PAD_LEN, 1024, True)
    hidden, slope = got[:2]
    full_up = take_weight(wa_up, got, 2)

    if fast:
        hidden, tokens, twin_i = fence(
            [(ci[0], "diag other near_twin"), (ci[1], "near"), (ci[2], "mine")], (hidden, tokens, twin_i))
        ci[0].twin("diag", "other")
        ci[1].second()
        ci[1].twin("near")
        ci[2].first()
        gi = [ci[0].group(twin_i)]
        wi_qkv = Weight(d_i, 3 * d_i, [(gi[0], 0, 3 * d_i, 0, 0)])
    qkv_i = image_qkv(tokens, gains_i, wi_qkv, clips, IMG_LEN, d_i)
    mixed_i = attn_forward(qkv_i, img_sizes, clips, IMG_LEN, HEADS_I, False)

    if fast:
        mixed_i, hidden = fence(
            [(ci[1], "diag other near_twin"), (ci[2], "near"), (ci[3], "mine")], (mixed_i, hidden))
        ci[1].twin("diag", "other")
        ci[2].second()
        ci[2].twin("near")
        ci[3].first()
        gi.append(ci[1].group(twin_i))
        wi_out = Weight(d_i, d_i, [(gi[1], 0, d_i, 0, 0)])
    got = down_embed(hidden, resid_mid, None, gains_a, sizes, wa_down, wa_proj, clips, PAD_LEN, d_a, True)
    aud_emb, embed_raw, pooled, resid_out = got[:4]
    full_down, full_proj = take_weight(wa_down, got, 4), take_weight(wa_proj, got, 5)
    mid_i, h_two_i = out_norm(mixed_i, tokens, gains_i, wi_out, clips, IMG_LEN, False)

    if fast:
        h_two_i, aud_emb = fence(
            [(ci[2], "diag other near_twin"), (ci[3], "near"), (ci[4], "mine")], (h_two_i, aud_emb))
        ci[2].twin("diag", "other")
        ci[3].second()
        ci[3].twin("near")
        ci[4].first()
        gi.append(ci[2].group(twin_i))
        wi_up = Weight(d_i, ff_i, [(gi[1], d_i, half, 0, 0), (gi[2], 0, half, half, 0)])
        wi_proj = Weight(d_i, pj, [(gi[2], half, pj, 0, 0)])
    hidden_i = up_gelu(h_two_i, wi_up, clips, IMG_LEN, d_i, False)[0]

    if fast:
        (hidden_i,) = fence([(ci[3], "diag other near_twin"), (ci[4], "near")], (hidden_i,))
        ci[3].twin("diag", "other")
        ci[4].second()
        ci[4].twin("near")
        gi.append(ci[3].group(twin_i))
        wi_left = Weight(ff_i, dl, [(gi[3], j * dl, dl, 0, j) for j in range(sub_i)], sub=sub_i)
    left_i = down_left(hidden_i, mid_i, wi_left, clips, IMG_LEN, d_i)

    if fast:
        (left_i,) = fence([(ci[4], "diag other near_twin")], (left_i,))
        ci[4].twin("diag", "other")
        gi.append(ci[4].group(twin_i))
        dr = d_i - dl
        wi_right = Weight(ff_i, dr, [(gi[4], j * dr, dr, 0, j) for j in range(sub_i)], sub=sub_i)
    img_emb = down_embed(hidden_i, mid_i, left_i, gains_i, img_sizes, wi_right, wi_proj, clips, IMG_LEN, d_i, False)[0]

    ids_low = jnp.broadcast_to(to_low(video_ids.reshape(clips, 1)), (clips, 128))
    joined = jnp.concatenate([aud_emb, img_emb, ids_low], axis=1).reshape(MICRO, clip_dev, 2 * pj + 128)
    joined = lax.all_gather(lax.all_gather(joined, "rep", axis=1, tiled=True), "dp", axis=1, tiled=True)
    aud_all, img_all, all_ids = joined[:, :, :pj], joined[:, :, pj : 2 * pj], joined[:, :, 2 * pj]
    rows = all_ids.shape[1]
    same = jnp.arange(rows)[:, None] == jnp.arange(rows)[None, :]
    allowed = jnp.logical_or(all_ids[:, :, None] != all_ids[:, None, :], same[None])
    loss_scale = rows / jnp.sum(allowed.astype(F32))
    logits = jnp.einsum("mid,mjd->mij", aud_all, img_all, preferred_element_type=F32) * LOGIT_SCALE
    masked = jnp.where(allowed, logits, -1e30)
    matched = jnp.sum(jnp.where(same, logits, 0.0), axis=2)
    row_lse = jax.nn.logsumexp(masked, axis=2)
    col_lse = jax.nn.logsumexp(masked, axis=1)
    loss = (jnp.sum(row_lse - matched) + jnp.sum(col_lse - matched)) * loss_scale
    start_row = lax.axis_index(AXES) * clip_dev
    own = lambda v: lax.dynamic_slice_in_dim(v, start_row, clip_dev, 1)
    own_masked = own(masked)
    d_logits = (
        jnp.exp(own_masked - own(row_lse)[:, :, None])
        + jnp.exp(own_masked - col_lse[:, None, :])
        - 2.0 * lax.dynamic_slice_in_dim(same.astype(F32), start_row, clip_dev, 0)[None]
    ) * (loss_scale * LOGIT_SCALE)
    d_embed = jnp.einsum("mij,mjd->mid", d_logits, img_all.astype(F32), precision=HIGHEST).reshape(clips, pj)

    d_raw = to_low(jax.vjp(unit_rows, embed_raw)[1](d_embed)[0])
    g_proj = dot_tn(to_low(pooled), d_raw)
    d_pooled = dot_nt(d_raw, full_proj)
    valid = jnp.arange(PAD_LEN)[None, :] < sizes[:, None]
    pool_weight = valid.astype(F32) / sizes[:, None].astype(F32)
    d_normed = (d_pooled[:, None, :] * pool_weight[:, :, None]).reshape(clips * PAD_LEN, d_a)
    d_out, g_three = jax.vjp(normed, resid_out, gains_a[2])[1](d_normed)
    d_low = to_low(d_out)
    g_down = dot_tn(hidden, d_low)
    d_pre = to_low(dot_nt(d_low, full_down) * slope.astype(F32))
    g_up = dot_tn(h_two, d_pre)
    d_ln_two, g_two = jax.vjp(normed, resid_mid, gains_a[1])[1](dot_nt(d_pre, full_up))
    d_mid = d_out + d_ln_two
    d_mid_low = to_low(d_mid)
    g_out = dot_tn(mixed, d_mid_low)
    d_mixed = to_low(dot_nt(d_mid_low, full_out))
    d_qkv = attn_backward(qkv, d_mixed, sizes, clips, PAD_LEN, HEADS_A)
    g_qkv = dot_tn(h_one, d_qkv)
    d_ln_one, g_one = jax.vjp(normed, resid_in, gains_a[0])[1](dot_nt(d_qkv, full_qkv))
    d_in = to_low(d_mid + d_ln_one)
    g_patch = dot_tn(patches, d_in)
    g_gains = jnp.stack([g_one, g_two, g_three])

    if fast:
        share = d_a // dp_size
        gain_rows = jnp.pad(g_gains.reshape(3, dp_size, share).transpose(1, 0, 2).reshape(dp_size, 1, 3 * share),
                            ((0, 0), (0, 7), (0, d_a - 3 * share))).reshape(dp_size * 8, d_a)
        r_down, r_proj = reduce_group([g_down, g_proj], 0, rep_size, d_a)
        (r_up,) = reduce_group([g_up], 1, rep_size, d_a)
        r_qkv, r_out, r_patch, r_gain = reduce_group([g_qkv, g_out, g_patch, gain_rows], 0, rep_size, d_a)
        summed = [r_patch, r_qkv, r_out, r_up, r_down, r_proj, r_gain[0, : 3 * share].reshape(3, share)]
    else:
        summed = [lax.psum(lax.psum_scatter(v, "dp", scatter_dimension=0, tiled=True), "rep")
                  for v in (g_patch, g_qkv, g_out, g_up, g_down, g_proj)]
        summed.append(lax.psum(lax.psum_scatter(g_gains, "dp", scatter_dimension=1, tiled=True), "rep"))
    local_squares = sum(jnp.sum(v * v) for v in summed)
    grad_norm = jnp.sqrt(lax.psum(local_squares, "dp"))
    factor = jnp.minimum(1.0, CLIP_NORM / grad_norm)
    results = []
    for index in range(7):
        step_rate = RATE_GAIN if index == 6 else RATE_MATRIX
        decay = 0.0 if index == 6 else WEIGHT_DECAY
        results.append(
            adam_step(masters[index], summed[index] * factor, firsts_in[index], seconds_in[index], step_rate, decay)
        )
    return (loss, grad_norm, *(r[0] for r in results), *(r[1] for r in results), *(r[2] for r in results))


def solution(mesh):
    batch4 = P(None, AXES, None, None)
    batch2 = P(None, AXES)
    split = P("dp", None)
    gain = P(None, "dp")
    weights = (split,) * 6 + (gain,)
    placed = (batch4, batch2, batch2, batch4) + (split,) * 5 + (gain,) + weights * 3
    return jax.shard_map(
        functools.partial(local, mesh.shape["dp"], mesh.shape["rep"]),
        mesh=mesh,
        in_specs=placed,
        out_specs=(P(), P()) + weights * 3,
        check_vma=False,
    )
```

time: 1400 us -> 706 us (0.50)
  waiting for transfers between devices: 602 us -> 185 us
  blocking collectives: 391 us -> 46.1 us
  matrix products: 252 us -> 50.1 us
  Pallas kernels: 0 us -> 181 us
  local copies, waits for them, and re-layouts: 53.3 us -> 112 us
  starting transfers between devices: 0.98 us -> 53.1 us
  between operations: 27.9 us -> 12.5 us
    all_gather x8 -> x3, blocking collectives: 364 us -> 33.8 us  [the longest x1 13.4 us: local(): lax.all_gather(joined, 'rep', axis=1, tiled=True)]
    reduce_scatter x6 -> x0, waiting for transfers between devices: 309 us -> none  [the longest x1 80.3 us: local(): lax.psum_scatter(grads[3], 'dp', scatter_dimension=0, tiled=True)]
    dot_general x62 -> x13, matrix products: 252 us -> 50.1 us  [the longest x6 24.9 us: dot_tn(): lax.dot_general(a, b, (((0,), (0,)), ((), ())), preferred_element_type=F32)]
    ppermute x0 -> x62, waiting for transfers between devices: none -> 185 us  [send(): return lax.ppermute(value, AXES, joint_perm(reps, fn))]
    pallas_call x0 -> x12, Pallas kernels: none -> 181 us  [run_kernel(): pl.pallas_call(kernel, grid_spec=pltpu.PrefetchScalarGridSpec(num_scalar_...]
    psum x1 -> x0, waiting for transfers between devices: 141 us -> none  [local(): summed = lax.psum(accum, 'rep')]
    all_gather x10 -> x0, waiting for transfers between devices: 114 us -> none  [the longest x1 76.3 us: local(): lax.all_gather(i_down, 'dp', axis=0, tiled=True)]
    unnamed x303 -> x336, local copies, waits for them, and re-layouts: 25 us -> 84.3 us
  transfers between devices with their start and end apart: 18 -> 62, of which waited for: 9 -> 20; matrix products, arithmetic and copies ran while one was open for 17% -> 14% of each run, Pallas kernels for 0% -> 23%
where the time goes in v1:
time: 706 us; the launch traced here: 701 us
  waiting for transfers between devices  185 us (26%)
  Pallas kernels  181 us (26%)
  local copies, waits for them, and re-layouts  112 us (16%)
  other arithmetic  61.6 us (9%)
  starting transfers between devices  53.1 us (8%)
  matrix products  50.1 us (7%)
  blocking collectives  46.1 us (7%)
  between operations  12.5 us (2%)
    ppermute x62, waiting for transfers between devices, send(): return lax.ppermute(value, AXES, joint_perm(reps, fn))  185 us
    pallas_call x12, Pallas kernels, run_kernel(): pl.pallas_call(kernel, grid_spec=pltpu.PrefetchScalarGridSpec(num_scalar_...  181 us
    unnamed x336, local copies, waits for them, and re-layouts  84.3 us
    ppermute x62, starting transfers between devices, send(): return lax.ppermute(value, AXES, joint_perm(reps, fn))  53.1 us
    dot_general x6, matrix products, dot_tn(): lax.dot_general(a, b, (((0,), (0,)), ((), ())), preferred_element_type=F32)  24.9 us
    dot_general x5, matrix products, dot_nt(): lax.dot_general(a, b, (((1,), (1,)), ((), ())), preferred_element_type=F32)  22.3 us
  transfers between devices with their start and end apart: 62, of which 20 were waited for; matrix products, arithmetic and copies ran while one was open for 14% of the time, Pallas kernels for 23%

profile of v1, /device:TPU:0, one launch (start us, length us, event | category | flops | bytes accessed | tf_op | source)
XLA Modules:
  0.0 701.0 jit_solution(9049998239590684425)
XLA Ops:
  13.8 11.3 %all-gather.1 = bf16[8,34,768]{2,1,0:T(8,128)(2,1)S(1)} all-gather(bf16[1,34,768]{2,1,0:T(8,128)(2,1)S(1)} %fusion.41), channel_id=2, replica_groups=mesh['dp'=8,'rep'=4] {'dp'}, dimensions={0}, use_global_device_ids=true | all-gather | bytes 470016 | tf_op jit(solution)/shard_map/all_gather | solution.py:625
  26.8 22.5 %collective-permute-done.refs_5_.refs_4_ = bf16[96,5120]{1,0:T(8,128)(2,1)S(1)} collective-permute-done((bf16[96,5120]{1,0:T(8,128)(2,1)S(1)}, bf16[96,5120]{1,0:T(8,128)(2,1)S(1)}, u32[]{:S(2)}, u32[]{:S(2)}) %collective-permute-start) | collective-permute-done | bytes 983072 | tf_op jit(solution)/shard_map/ppermute | solution.py:509
  53.1 19.4 %collective-permute-done.1.refs_6_.refs_5_ = bf16[96,5120]{1,0:T(8,128)(2,1)S(1)} collective-permute-done((bf16[96,5120]{1,0:T(8,128)(2,1)S(1)}, bf16[96,5120]{1,0:T(8,128)(2,1)S(1)}, u32[]{:S(2)}, u32[]{:S(2)}) %collective-permute-start.1) | collective-permute-done | bytes 983072 | tf_op jit(solution)/shard_map/ppermute | solution.py:509
  78.3 16.6 %collective-permute-done.4.refs_12_.refs_7_.refs_15_ = bf16[96,5120]{1,0:T(8,128)(2,1)S(1)} collective-permute-done((bf16[96,5120]{1,0:T(8,128)(2,1)S(1)}, bf16[96,5120]{1,0:T(8,128)(2,1)S(1)}, u32[]{:S(2)}, u32[]{:S(2)}) %collective-permute-start.4) | collective-permute-done | bytes 983072 | tf_op jit(solution)/shard_map/ppermute | solution.py:509
  115.1 12.0 %audio_in.1 = (f32[960,768]{1,0:T(8,128)}, bf16[960,768]{1,0:T(8,128)(2,1)S(1)}, bf16[960,2304]{1,0:T(8,128)(2,1)}, bf16[768,2304]{1,0:T(8,128)(2,1)}) custom-call(s32[8]{0:T(128)S(1)} %pad_add_fusion.refs_0_.refs_1_.refs_2_, bf16[960,256]{1,0:T(8,128)(2,1)S(1)} %bitcast.117, bf16[256,768]{1,0:T(8,128)(2,1)S(1)} %bitcast.119, ...), custom_call_target="tpu_custom_call" | custom-call | flops 3774873600 | bytes 23110656 | tf_op jit(solution)/shard_map/audio_in/pallas_call | solution.py:194
  154.5 18.7 %up_gelu.2 = (bf16[960,3072]{1,0:T(8,128)(2,1)}, bf16[960,3072]{1,0:T(8,128)(2,1)}, bf16[768,3072]{1,0:T(8,128)(2,1)}) custom-call(s32[8]{0:T(128)S(1)} %pad_add_fusion.refs_0_.refs_1_.refs_2_, s32[8]{0:T(128)S(1)} %pad_add_fusion.refs_0_.refs_1_.refs_2_, bf16[960,768]{1,0:T(8,128)(2,1)} %copy-done.42, bf16[96,10240]{1,0:T(8,128)(2,1)} %copy-done, ...), custom_call_target="tpu_custom_call" | custom-call | flops 4529848320 | bytes 37650432 | tf_op jit(solution)/shard_map/up_gelu/pallas_call | solution.py:194
  189.3 17.6 %image_qkv.1.refs_1_ = bf16[1024,3840]{1,0:T(8,128)(2,1)} custom-call(s32[8]{0:T(128)S(1)} %pad_add_fusion.refs_0_.refs_1_.refs_2_, bf16[1024,1280]{1,0:T(8,128)(2,1)S(1)} %bitcast.115, f32[3,1280]{1,0:T(4,128)S(1)} %reshape.323.refs_2_.refs_3_.refs_5_, bf16[160,16384]{1,0:T(8,128)(2,1)} %slice_dynamic-update-slice_fusion.10.refs_3_.refs_4_.refs_11_.refs_7_.refs_15_, ...), custom_call_target="tpu_custom_call" | custom-call | flops 10066329600 | bytes 28359680 | tf_op jit(solution)/shard_map/image_qkv/pallas_call | solution.py:194
  210.2 11.1 %attn_forward.3.refs_1_ = bf16[1024,1280]{1,0:T(8,128)(2,1)S(1)} custom-call(s32[4]{0:T(128)S(1)} %broadcast_29_refs_0_.2.refs_0_, bf16[1024,3840]{1,0:T(8,128)(2,1)S(1)} %copy-done.64), custom_call_target="tpu_custom_call" | custom-call | flops 4294967296 | bytes 10485760 | tf_op jit(solution)/shard_map/attn_forward/pallas_call | solution.py:194
  230.1 16.8 %down_embed.2 = (bf16[4,1024]{1,0:T(4,128)(2,1)S(1)}, f32[4,1024]{1,0:T(4,128)S(1)}, f32[4,768]{1,0:T(4,128)S(1)}, f32[960,768]{1,0:T(8,128)}, bf16[3072,768]{1,0:T(8,128)(2,1)}, /*index=5*/bf16[768,1024]{1,0:T(8,128)(2,1)S(1)}) custom-call(s32[4]{0:T(128)S(1)} %reshape.311.refs_0_, s32[8]{0:T(128)S(1)} %pad_add_fusion.refs_0_.refs_1_.refs_2_, ...), custom_call_target="tpu_custom_call" | custom-call | flops 4529848320 | bytes 37794816 | tf_op jit(solution)/shard_map/down_embed/pallas_call | solution.py:194
  269.0 26.1 %up_gelu.3.refs_1_.refs_3_ = bf16[1024,5120]{1,0:T(8,128)(2,1)} custom-call(s32[8]{0:T(128)S(1)} %pad_add_fusion.refs_0_.refs_1_.refs_2_, s32[8]{0:T(128)S(1)} %pad_add_fusion.refs_0_.refs_1_.refs_2_, bf16[1024,1280]{1,0:T(8,128)(2,1)} %copy-done.56, bf16[160,16384]{1,0:T(8,128)(2,1)} %slice_dynamic-update-slice_fusion.10.refs_3_.refs_4_.refs_11_.refs_7_.refs_15_, ...), custom_call_target="tpu_custom_call" | custom-call | flops 13421772800 | bytes 48332800 | tf_op jit(solution)/shard_map/up_gelu/pallas_call | solution.py:194
  306.8 17.7 %down_left.1.refs_6_ = f32[1024,768]{1,0:T(8,128)S(1)} custom-call(s32[8]{0:T(128)S(1)} %pad_add_fusion.refs_0_.refs_1_.refs_2_, bf16[1024,5120]{1,0:T(8,128)(2,1)} %up_gelu.3.refs_1_.refs_3_, f32[1024,1280]{1,0:T(8,128)} %copy-done.11, bf16[160,16384]{1,0:T(8,128)(2,1)} %slice_dynamic-update-slice_fusion.10.refs_3_.refs_4_.refs_11_.refs_7_.refs_15_, ...), custom_call_target="tpu_custom_call" | custom-call | flops 8053063680 | bytes 35258368 | tf_op jit(solution)/shard_map/down_left/pallas_call | solution.py:194
  329.4 16.9 %down_embed.3 = (bf16[4,1024]{1,0:T(4,128)(2,1)S(1)}, f32[4,1024]{1,0:T(4,128)}, f32[4,1280]{1,0:T(4,128)}) custom-call(s32[4]{0:T(128)S(1)} %broadcast_29_refs_0_.2.refs_0_, s32[8]{0:T(128)S(1)} %pad_add_fusion.refs_0_.refs_1_.refs_2_, s32[8]{0:T(128)S(1)} %pad_add_fusion.refs_0_.refs_1_.refs_2_, bf16[1024,5120]{1,0:T(8,128)(2,1)} %up_gelu.3.refs_1_.refs_3_, ...), custom_call_target="tpu_custom_call" | custom-call | flops 5368709120 | bytes 50719744 | tf_op jit(solution)/shard_map/down_embed/pallas_call | solution.py:194
  346.5 13.4 %all_gather.14 = bf16[2,8,2176]{2,0,1:T(2,128)(2,1)S(1)} all-gather(bf16[2,2,2176]{2,0,1:T(2,128)(2,1)S(1)} %copy.106), channel_id=1, replica_groups=mesh['dp'=8,'rep'=4] {'rep'}, dimensions={1}, use_global_device_ids=true | all-gather | bytes 87040 | tf_op jit(solution)/shard_map/all_gather | solution.py:754
  359.9 9.1 %all_gather.15 = bf16[2,64,2176]{2,1,0:T(8,128)(2,1)S(1)} all-gather(bf16[2,8,2176]{2,1,0:T(8,128)(2,1)S(1)} %copy.107), channel_id=1, replica_groups=mesh['dp'=8,'rep'=4] {'dp'}, dimensions={1}, use_global_device_ids=true | all-gather | bytes 626688 | tf_op jit(solution)/shard_map/all_gather | solution.py:754
  384.8 8.3 %fusion.63 = f32[3072,768]{1,0:T(8,128)S(1)} fusion(bf16[960,3072]{1,0:T(8,128)(2,1)} %get-tuple-element.128.refs_3_, f32[960,768]{1,0:T(8,128)} %add_add_fusion.2, f32[960]{0:T(1024)S(1)} %negate_multiply_fusion.2), kind=kOutput, calls=%fused_computation.244 | convolution fusion | flops 4531322880 | bytes 18288384 | tf_op jit(solution)/shard_map/dot_general | solution.py:58
  398.9 8.7 %multiply_convert_fusion = bf16[960,3072]{1,0:T(8,128)(2,1)S(1)} fusion(bf16[960,3072]{1,0:T(8,128)(2,1)} %get-tuple-element.154, bf16[3072,768]{1,0:T(8,128)(2,1)} %get-tuple-element.153, f32[960,768]{1,0:T(8,128)S(1)} %copy-done.67, f32[960]{0:T(1024)S(1)} %negate_multiply_fusion.2), kind=kOutput, calls=%fused_computation | convolution fusion | flops 4540170240 | bytes 19468032 | tf_op jit(solution)/shard_map/dot_general | solution.py:54
  435.7 25.0 %attn_backward.1 = bf16[960,2304]{1,0:T(8,128)(2,1)S(1)} custom-call(s32[4]{0:T(128)S(1)} %reshape.311.refs_0_, bf16[960,2304]{1,0:T(8,128)(2,1)S(1)} %bitcast.121, bf16[960,768]{1,0:T(8,128)(2,1)S(1)} %convolution_convert_fusion.refs_2_), custom_call_target="tpu_custom_call" | custom-call | flops 7077888000 | bytes 10321920 | tf_op jit(solution)/shard_map/attn_backward/pallas_call | solution.py:194
  511.1 13.3 %collective-permute-done.51 = bf16[2,384,768]{2,1,0:T(8,128)(2,1)S(1)} collective-permute-done((bf16[2,384,768]{2,1,0:T(8,128)(2,1)S(1)}, bf16[2,384,768]{2,1,0:T(8,128)(2,1)S(1)}, u32[]{:S(2)}, u32[]{:S(2)}) %collective-permute-start.51) | collective-permute-done | bytes 1179680 | tf_op jit(solution)/shard_map/ppermute | solution.py:509
  537.5 41.5 %collective-permute-done.52 = bf16[384,768]{1,0:T(8,128)(2,1)S(1)} collective-permute-done((bf16[384,768]{1,0:T(8,128)(2,1)}, bf16[384,768]{1,0:T(8,128)(2,1)S(1)}, u32[]{:S(2)}, u32[]{:S(2)}) %collective-permute-start.52) | collective-permute-done | bytes 589856 | tf_op jit(solution)/shard_map/ppermute | solution.py:509
  586.3 8.6 %collective-permute-done.53 = bf16[384,768]{1,0:T(8,128)(2,1)S(1)} collective-permute-done((bf16[384,768]{1,0:T(8,128)(2,1)S(1)}, bf16[384,768]{1,0:T(8,128)(2,1)S(1)}, u32[]{:S(2)}, u32[]{:S(2)}) %collective-permute-start.53) | collective-permute-done | bytes 589856 | tf_op jit(solution)/shard_map/ppermute | solution.py:509
  613.4 11.0 %collective-permute-done.59 = bf16[512,768]{1,0:T(8,128)(2,1)S(1)} collective-permute-done((bf16[512,768]{1,0:T(8,128)(2,1)S(1)}, bf16[512,768]{1,0:T(8,128)(2,1)S(1)}, u32[]{:S(2)}, u32[]{:S(2)}) %collective-permute-start.59) | collective-permute-done | bytes 786464 | tf_op jit(solution)/shard_map/ppermute | solution.py:509
  631.6 14.5 %collective-permute-done.49 = bf16[424,768]{1,0:T(8,128)(2,1)S(1)} collective-permute-done((bf16[424,768]{1,0:T(8,128)(2,1)S(1)}, bf16[424,768]{1,0:T(8,128)(2,1)S(1)}, u32[]{:S(2)}, u32[]{:S(2)}) %collective-permute-start.49) | collective-permute-done | bytes 651296 | tf_op jit(solution)/shard_map/ppermute | solution.py:509
  651.6 12.9 %collective-permute-done.61 = bf16[512,768]{1,0:T(8,128)(2,1)} collective-permute-done((bf16[512,768]{1,0:T(8,128)(2,1)S(1)}, bf16[512,768]{1,0:T(8,128)(2,1)}, u32[]{:S(2)}, u32[]{:S(2)}) %collective-permute-start.61) | collective-permute-done | bytes 786464 | tf_op jit(solution)/shard_map/ppermute | solution.py:509
  671.1 12.3 %psum.7 = f32[]{:T(128)} all-reduce(f32[]{:T(128)S(6)} %add.365), channel_id=1, replica_groups=mesh['dp'=8,'rep'=4] {'dp'}, use_global_device_ids=true, to_apply=%region_32.33 | all-reduce | flops 1 | bytes 8 | tf_op jit(solution)/shard_map/psum | solution.py:812
  (619 shorter events, 303.3 us)
Async XLA Ops:
  50.8 44.0 %collective-permute-start.5 = (bf16[96,10240]{1,0:T(8,128)(2,1)S(1)}, bf16[96,10240]{1,0:T(8,128)(2,1)S(1)}, u32[]{:S(2)}, u32[]{:S(2)}) collective-permute-start(bf16[96,10240]{1,0:T(8,128)(2,1)S(1)} %convert_dynamic-update-slice_fusion.2.refs_4_.refs_3_.refs_11_.refs_6_.refs_14_), channel_id=1, source_target_pairs={{0,4},{1,5},{2,6},{3,7},{4,0},{5,1},{6,2},{7,3},{8,12},{9,13},{10,... | collective-permute-start | bytes 5898248 | tf_op jit(solution)/shard_map/ppermute | solution.py:509
  50.8 129.2 %collective-permute-start.18 = (bf16[160,16384]{1,0:T(8,128)(2,1)}, bf16[160,16384]{1,0:T(8,128)(2,1)}, u32[]{:S(2)}, u32[]{:S(2)}) collective-permute-start(bf16[160,16384]{1,0:T(8,128)(2,1)} %slice_dynamic-update-slice_fusion.10.refs_3_.refs_4_.refs_11_.refs_7_.refs_15_), channel_id=1, source_target_pairs={{0,4},{1,5},{2,6},{3,7},{4,0},{5,1},{6,2},{7,3},{8,12},{9,13},{10,... | collective-permute-start | bytes 15728648 | tf_op jit(solution)/shard_map/ppermute | solution.py:509
  97.6 48.6 %collective-permute-start.9 = (bf16[160,3840]{1,0:T(8,128)(2,1)}, bf16[160,3840]{1,0:T(8,128)(2,1)}, u32[]{:S(2)}, u32[]{:S(2)}) collective-permute-start(bf16[160,3840]{1,0:T(8,128)(2,1)} %get-tuple-element.96), channel_id=1, source_target_pairs={{0,8},{1,17},{2,10},{3,19},{4,12},{5,21},{6,14},{7,23},{8,0},{9,25... | collective-permute-start | bytes 3686408 | tf_op jit(solution)/shard_map/ppermute | solution.py:509
  99.2 47.0 %collective-permute-start.6 = (bf16[96,5120]{1,0:T(8,128)(2,1)S(1)}, bf16[96,5120]{1,0:T(8,128)(2,1)}, u32[]{:S(2)}, u32[]{:S(2)}) collective-permute-start(bf16[96,5120]{1,0:T(8,128)(2,1)S(1)} %collective-permute-done.4.refs_12_.refs_7_.refs_15_), channel_id=1, source_target_pairs={{0,16},{1,9},{2,18},{3,11},{4,20},{5,13},{6,22},{7,15},{8,24},{9,1... | collective-permute-start | bytes 2949128 | tf_op jit(solution)/shard_map/ppermute | solution.py:509
  100.7 45.5 %collective-permute-start.7 = (bf16[96,5120]{1,0:T(8,128)(2,1)S(1)}, bf16[96,5120]{1,0:T(8,128)(2,1)}, u32[]{:S(2)}, u32[]{:S(2)}) collective-permute-start(bf16[96,5120]{1,0:T(8,128)(2,1)S(1)} %collective-permute-done.4.refs_12_.refs_7_.refs_15_), channel_id=1, source_target_pairs={{0,1},{1,0},{2,3},{3,2},{4,5},{5,4},{6,7},{7,6},{8,9},{9,8},{10,11... | collective-permute-start | bytes 2949128 | tf_op jit(solution)/shard_map/ppermute | solution.py:509
  103.2 43.0 %collective-permute-start.8 = (bf16[96,5120]{1,0:T(8,128)(2,1)S(1)}, bf16[96,5120]{1,0:T(8,128)(2,1)}, u32[]{:S(2)}, u32[]{:S(2)}) collective-permute-start(bf16[96,5120]{1,0:T(8,128)(2,1)S(1)} %collective-permute-done.4.refs_12_.refs_7_.refs_15_), channel_id=1, source_target_pairs={{0,4},{1,5},{2,6},{3,7},{4,0},{5,1},{6,2},{7,3},{8,12},{9,13},{10,... | collective-permute-start | bytes 2949128 | tf_op jit(solution)/shard_map/ppermute | solution.py:509
  146.9 29.6 %collective-permute-start.12 = (bf16[160,3840]{1,0:T(8,128)(2,1)}, bf16[160,3840]{1,0:T(8,128)(2,1)S(1)}, u32[]{:S(2)}, u32[]{:S(2)}) collective-permute-start(bf16[160,3840]{1,0:T(8,128)(2,1)} %collective-permute-done.9.refs_4_), channel_id=1, source_target_pairs={{0,16},{1,9},{2,18},{3,11},{4,20},{5,13},{6,22},{7,15},{8,24},{9,1... | collective-permute-start | bytes 3686408 | tf_op jit(solution)/shard_map/ppermute | solution.py:509
  148.4 29.4 %collective-permute-start.13 = (bf16[160,3840]{1,0:T(8,128)(2,1)}, bf16[160,3840]{1,0:T(8,128)(2,1)}, u32[]{:S(2)}, u32[]{:S(2)}) collective-permute-start(bf16[160,3840]{1,0:T(8,128)(2,1)} %collective-permute-done.9.refs_4_), channel_id=1, source_target_pairs={{0,1},{1,0},{2,3},{3,2},{4,5},{5,4},{6,7},{7,6},{8,9},{9,8},{10,11... | collective-permute-start | bytes 3686408 | tf_op jit(solution)/shard_map/ppermute | solution.py:509
  182.9 38.4 %collective-permute-start.19 = (bf16[160,3840]{1,0:T(8,128)(2,1)}, bf16[160,3840]{1,0:T(8,128)(2,1)S(1)}, u32[]{:S(2)}, u32[]{:S(2)}) collective-permute-start(bf16[160,3840]{1,0:T(8,128)(2,1)} %collective-permute-done.15.refs_5_.refs_4_), channel_id=1, source_target_pairs={{0,16},{1,9},{2,18},{3,11},{4,20},{5,13},{6,22},{7,15},{8,24},{9,1... | collective-permute-start | bytes 3686408 | tf_op jit(solution)/shard_map/ppermute | solution.py:509
  184.5 36.8 %collective-permute-start.20 = (bf16[160,3840]{1,0:T(8,128)(2,1)}, bf16[160,3840]{1,0:T(8,128)(2,1)S(1)}, u32[]{:S(2)}, u32[]{:S(2)}) collective-permute-start(bf16[160,3840]{1,0:T(8,128)(2,1)} %collective-permute-done.15.refs_5_.refs_4_), channel_id=1, source_target_pairs={{0,1},{1,0},{2,3},{3,2},{4,5},{5,4},{6,7},{7,6},{8,9},{9,8},{10,11... | collective-permute-start | bytes 3686408 | tf_op jit(solution)/shard_map/ppermute | solution.py:509
  185.0 36.4 %collective-permute-start.21 = (bf16[160,3840]{1,0:T(8,128)(2,1)}, bf16[160,3840]{1,0:T(8,128)(2,1)S(1)}, u32[]{:S(2)}, u32[]{:S(2)}) collective-permute-start(bf16[160,3840]{1,0:T(8,128)(2,1)} %collective-permute-done.15.refs_5_.refs_4_), channel_id=1, source_target_pairs={{0,4},{1,5},{2,6},{3,7},{4,0},{5,1},{6,2},{7,3},{8,12},{9,13},{10,... | collective-permute-start | bytes 3686408 | tf_op jit(solution)/shard_map/ppermute | solution.py:509
  185.0 36.3 %collective-permute-start.22 = (bf16[160,3584]{1,0:T(8,128)(2,1)}, bf16[160,3584]{1,0:T(8,128)(2,1)}, u32[]{:S(2)}, u32[]{:S(2)}) collective-permute-start(bf16[160,3584]{1,0:T(8,128)(2,1)} %slice.267), channel_id=1, source_target_pairs={{0,8},{1,17},{2,10},{3,19},{4,12},{5,21},{6,14},{7,23},{8,0},{9,25... | collective-permute-start | bytes 3440648 | tf_op jit(solution)/shard_map/ppermute | solution.py:509
  223.0 38.5 %collective-permute-start.25 = (bf16[160,3584]{1,0:T(8,128)(2,1)}, bf16[160,3584]{1,0:T(8,128)(2,1)}, u32[]{:S(2)}, u32[]{:S(2)}) collective-permute-start(bf16[160,3584]{1,0:T(8,128)(2,1)} %collective-permute-done.22.refs_12_.refs_16_), channel_id=1, source_target_pairs={{0,16},{1,9},{2,18},{3,11},{4,20},{5,13},{6,22},{7,15},{8,24},{9,1... | collective-permute-start | bytes 3440648 | tf_op jit(solution)/shard_map/ppermute | solution.py:509
  223.6 37.8 %collective-permute-start.26 = (bf16[160,3584]{1,0:T(8,128)(2,1)}, bf16[160,3584]{1,0:T(8,128)(2,1)}, u32[]{:S(2)}, u32[]{:S(2)}) collective-permute-start(bf16[160,3584]{1,0:T(8,128)(2,1)} %collective-permute-done.22.refs_12_.refs_16_), channel_id=1, source_target_pairs={{0,1},{1,0},{2,3},{3,2},{4,5},{5,4},{6,7},{7,6},{8,9},{9,8},{10,11... | collective-permute-start | bytes 3440648 | tf_op jit(solution)/shard_map/ppermute | solution.py:509
  225.2 36.2 %collective-permute-start.27 = (bf16[160,3584]{1,0:T(8,128)(2,1)}, bf16[160,3584]{1,0:T(8,128)(2,1)}, u32[]{:S(2)}, u32[]{:S(2)}) collective-permute-start(bf16[160,3584]{1,0:T(8,128)(2,1)} %collective-permute-done.22.refs_12_.refs_16_), channel_id=1, source_target_pairs={{0,4},{1,5},{2,6},{3,7},{4,0},{5,1},{6,2},{7,3},{8,12},{9,13},{10,... | collective-permute-start | bytes 3440648 | tf_op jit(solution)/shard_map/ppermute | solution.py:509
  228.1 33.3 %collective-permute-start.28 = (bf16[160,3072]{1,0:T(8,128)(2,1)}, bf16[160,3072]{1,0:T(8,128)(2,1)}, u32[]{:S(2)}, u32[]{:S(2)}) collective-permute-start(bf16[160,3072]{1,0:T(8,128)(2,1)} %slice.268), channel_id=1, source_target_pairs={{0,8},{1,17},{2,10},{3,19},{4,12},{5,21},{6,14},{7,23},{8,0},{9,25... | collective-permute-start | bytes 2949128 | tf_op jit(solution)/shard_map/ppermute | solution.py:509
  265.1 30.1 %collective-permute-start.31 = (bf16[160,3072]{1,0:T(8,128)(2,1)}, bf16[160,3072]{1,0:T(8,128)(2,1)}, u32[]{:S(2)}, u32[]{:S(2)}) collective-permute-start(bf16[160,3072]{1,0:T(8,128)(2,1)} %collective-permute-done.28.refs_4_), channel_id=1, source_target_pairs={{0,16},{1,9},{2,18},{3,11},{4,20},{5,13},{6,22},{7,15},{8,24},{9,1... | collective-permute-start | bytes 2949128 | tf_op jit(solution)/shard_map/ppermute | solution.py:509
  398.5 104.7 %collective-permute-start.56 = (bf16[2,2,512,768]{3,2,0,1:T(8,128)(2,1)}, bf16[2,2,512,768]{3,2,0,1:T(8,128)(2,1)}, u32[]{:S(2)}, u32[]{:S(2)}) collective-permute-start(bf16[2,2,512,768]{3,2,0,1:T(8,128)(2,1)} %maximum_maximum_fusion), channel_id=1, source_target_pairs={{0,4},{1,5},{2,6},{3,7},{4,0},{5,1},{6,2},{7,3},{8,12},{9,13},{10,... | collective-permute-start | bytes 9437192 | tf_op jit(solution)/shard_map/ppermute | solution.py:509
  419.0 74.8 %collective-permute-start.50 = (bf16[2,2,384,768]{3,2,1,0:T(8,128)(2,1)}, bf16[2,2,384,768]{3,2,1,0:T(8,128)(2,1)}, u32[]{:S(2)}, u32[]{:S(2)}) collective-permute-start(bf16[2,2,384,768]{3,2,1,0:T(8,128)(2,1)} %pad_maximum_fusion), channel_id=1, source_target_pairs={{0,4},{1,5},{2,6},{3,7},{4,0},{5,1},{6,2},{7,3},{8,12},{9,13},{10,... | collective-permute-start | bytes 7077896 | tf_op jit(solution)/shard_map/ppermute | solution.py:509
  501.4 31.7 %collective-permute-start.45 = (bf16[2,424,768]{2,1,0:T(8,128)(2,1)}, bf16[2,424,768]{2,1,0:T(8,128)(2,1)}, u32[]{:S(2)}, u32[]{:S(2)}) collective-permute-start(bf16[2,424,768]{2,1,0:T(8,128)(2,1)} %fusion.10), channel_id=1, source_target_pairs={{0,8},{1,9},{2,10},{3,11},{4,12},{5,13},{6,14},{7,15},{8,0},{9,1},... | collective-permute-start | bytes 3907592 | tf_op jit(solution)/shard_map/ppermute | solution.py:509
  509.6 71.6 %collective-permute-start.57 = (bf16[2,512,768]{2,1,0:T(8,128)(2,1)}, bf16[2,512,768]{2,1,0:T(8,128)(2,1)}, u32[]{:S(2)}, u32[]{:S(2)}) collective-permute-start(bf16[2,512,768]{2,1,0:T(8,128)(2,1)} %fusion.6), channel_id=1, source_target_pairs={{0,8},{1,9},{2,10},{3,11},{4,12},{5,13},{6,14},{7,15},{8,0},{9,1},... | collective-permute-start | bytes 4718600 | tf_op jit(solution)/shard_map/ppermute | solution.py:509
  528.7 50.2 %collective-permute-start.52 = (bf16[384,768]{1,0:T(8,128)(2,1)}, bf16[384,768]{1,0:T(8,128)(2,1)S(1)}, u32[]{:S(2)}, u32[]{:S(2)}) collective-permute-start(bf16[384,768]{1,0:T(8,128)(2,1)} %fusion.23), channel_id=1, source_target_pairs={{0,8},{1,9},{2,10},{3,11},{4,12},{5,13},{6,14},{7,15},{8,0},{9,1},... | collective-permute-start | bytes 1769480 | tf_op jit(solution)/shard_map/ppermute | solution.py:509
  535.6 49.3 %collective-permute-start.46 = (bf16[424,768]{1,0:T(8,128)(2,1)S(1)}, bf16[424,768]{1,0:T(8,128)(2,1)S(1)}, u32[]{:S(2)}, u32[]{:S(2)}) collective-permute-start(bf16[424,768]{1,0:T(8,128)(2,1)S(1)} %fusion.22), channel_id=1, source_target_pairs={{0,16},{1,17},{2,18},{3,19},{4,20},{5,21},{6,22},{7,23},{8,24},{9,... | collective-permute-start | bytes 1953800 | tf_op jit(solution)/shard_map/ppermute | solution.py:509
  630.3 34.2 %collective-permute-start.61 = (bf16[512,768]{1,0:T(8,128)(2,1)S(1)}, bf16[512,768]{1,0:T(8,128)(2,1)}, u32[]{:S(2)}, u32[]{:S(2)}) collective-permute-start(bf16[512,768]{1,0:T(8,128)(2,1)S(1)} %add_convert_fusion.2), channel_id=1, source_target_pairs={{1,0},{2,3},{5,4},{6,7},{9,8},{10,11},{13,12},{14,15},{17,16},{18,... | collective-permute-start | bytes 2359304 | tf_op jit(solution)/shard_map/ppermute | solution.py:509
  (195 other events, 1935.8 us)

commit v2 on v1

--- a/solution.py
+++ b/solution.py
@@ -29,7 +29,7 @@
 PAD_LEN = 240
 GELU_C = 0.7978845608028654
 GELU_A = 0.044715
-MIB = 1 << 20
+VMEM_GRANT = 60 << 20
 
 
 def to_low(v):
@@ -85,6 +85,7 @@
     def entries(self, tn):
         groups, out = self.groups(), []
         for g, col, width, dst, part in self.segs:
+            assert width % tn == 0
             out += [(groups.index(g), col + t * tn, dst + t * tn, part) for t in range(width // tn)]
         return sorted(out, key=lambda e: (e[2], e[3]))
 
@@ -136,7 +137,7 @@
     return pl.BlockSpec(shape, lambda *_: (0,) * len(shape))
 
 
-def run_kernel(body, name, grid, scalars, ins, weights, outs, scratch, limit, flops):
+def run_kernel(body, name, grid, scalars, ins, weights, outs, scratch, flops, alias=None):
     scal = list(scalars)
     for w, _ in weights:
         scal += w.indices()
@@ -201,7 +202,8 @@
             scratch_shapes=scr,
         ),
         out_shape=[jax.ShapeDtypeStruct(o[0], o[1]) for o in outs],
-        compiler_params=pltpu.CompilerParams(vmem_limit_bytes=limit * MIB),
+        input_output_aliases={} if alias is None else {n_scal + alias: 0},
+        compiler_params=pltpu.CompilerParams(vmem_limit_bytes=VMEM_GRANT),
         cost_estimate=pl.CostEstimate(flops=flops, bytes_accessed=bytes_acc, transcendentals=0),
         name=name,
     )(*scal, *operands)
@@ -209,22 +211,6 @@
 
 def rows_spec(length, width):
     return pl.BlockSpec((length, width), lambda i, *_: (i, 0))
-
-
-def emitted(w, keep=True):
-    return [((w.k, w.n), BF16, full_spec((w.k, w.n)))] if keep and w.whole is None else []
-
-
-def emit_weight(w, outs, at, wbuf, keep=True, step=0):
-    if keep and w.whole is None:
-
-        @pl.when(pl.program_id(0) == step)
-        def _():
-            outs[at][...] = wbuf[...]
-
-
-def take_weight(w, results, at):
-    return w.whole if w.whole is not None else results[at]
 
 
 def image_qkv(tokens, gains, w, clips, length, tn):
@@ -244,7 +230,7 @@
     return run_kernel(
         body, "image_qkv", (clips,), [],
         [(tokens, rows_spec(length, d)), (gains, full_spec((3, d)))], [(w, tn)],
-        [((clips * length, n), BF16, rows_spec(length, n))], [], 40, 2 * clips * length * d * n,
+        [((clips * length, n), BF16, rows_spec(length, n))], [], 2 * clips * length * d * n,
     )[0]
 
 
@@ -265,15 +251,13 @@
 
         lax.fori_loop(0, n // tn, step, 0)
 
-        emit_weight(w, outs, 3, wb[0])
-
     m = clips * length
     return run_kernel(
         body, "audio_in", (clips,), [],
         [(patches, rows_spec(length, pk)), (w_patch, full_spec((pk, d))), (gains, full_spec((3, d)))], [(w, tn)],
         [((m, d), F32, rows_spec(length, d)), ((m, d), BF16, rows_spec(length, d)),
-         ((m, n), BF16, rows_spec(length, n))] + emitted(w),
-        [], 40, 2 * m * d * (n + pk),
+         ((m, n), BF16, rows_spec(length, n))],
+        [], 2 * m * d * (n + pk),
     )
 
 
@@ -318,11 +302,11 @@
     m = clips * length
     return run_kernel(
         body, "attn_forward", (clips,), [lengths], [(qkv, rows_spec(length, 3 * d))], [],
-        [((m, d), BF16, rows_spec(length, d))], [], 32, 4 * m * length * 256 * heads,
+        [((m, d), BF16, rows_spec(length, d))], [], 4 * m * length * 256 * heads,
     )[0]
 
 
-def out_norm(mixed, resid, gains, w, clips, length, keep):
+def out_norm(mixed, resid, gains, w, clips, length):
     d = w.n
 
     def body(_s, ins, outs, _scr, wb, wait):
@@ -330,14 +314,13 @@
         x1 = ins[1][...].astype(F32) + dot_f32(ins[0][...], wb[0][...])
         outs[0][...] = x1
         outs[1][...] = to_low(normed(x1, ins[2][1:2, :]))
-        emit_weight(w, outs, 2, wb[0], keep)
 
     m = clips * length
-    outs = [((m, d), F32, rows_spec(length, d)), ((m, d), BF16, rows_spec(length, d))] + emitted(w, keep)
+    outs = [((m, d), F32, rows_spec(length, d)), ((m, d), BF16, rows_spec(length, d))]
     return run_kernel(
         body, "out_norm", (clips,), [],
         [(mixed, rows_spec(length, d)), (resid, rows_spec(length, d)), (gains, full_spec((3, d)))], [(w, d)],
-        outs, [], 32, 2 * m * d * d,
+        outs, [], 2 * m * d * d,
     )
 
 
@@ -366,14 +349,13 @@
             return c
 
         lax.fori_loop(0, n // tn, step, 0)
-        emit_weight(w, outs, 2, wb[0], keep)
 
     m = clips * length
     outs = [((m, n), BF16, rows_spec(length, n))]
     if keep:
-        outs += [((m, n), BF16, rows_spec(length, n))] + emitted(w)
+        outs += [((m, n), BF16, rows_spec(length, n))]
     return run_kernel(
-        body, "up_gelu", (clips,), [], [(h_two, rows_spec(length, d))], [(w, tn)], outs, [], 44, 2 * m * d * n,
+        body, "up_gelu", (clips,), [], [(h_two, rows_spec(length, d))], [(w, tn)], outs, [], 2 * m * d * n,
     )
 
 
@@ -394,7 +376,7 @@
     m = clips * length
     return run_kernel(
         body, "down_left", (clips,), [], [(hidden, rows_spec(length, k)), (resid, rows_spec(length, n))],
-        [(w, n)], [((m, n), F32, rows_spec(length, n))], [], 44, 2 * m * n * k,
+        [(w, n)], [((m, n), F32, rows_spec(length, n))], [], 2 * m * n * k,
     )[0]
 
 
@@ -423,8 +405,6 @@
         scr[1][pl.ds(g, 1), :] = pooled
         if keep:
             outs[3][...] = x2
-            emit_weight(w, outs, 4, wb[0])
-            emit_weight(w_proj, outs, 5, wb[1], True, clips - 1)
         wait(1, 0)
 
         @pl.when(g == clips - 1)
@@ -439,17 +419,17 @@
     outs = [((clips, pj), BF16, full_spec((clips, pj))), ((clips, pj), F32, full_spec((clips, pj))),
             ((clips, d), F32, full_spec((clips, d)))]
     if keep:
-        outs += [((m, d), F32, rows_spec(length, d))] + emitted(w) + emitted(w_proj)
+        outs += [((m, d), F32, rows_spec(length, d))]
     ins = [(hidden, rows_spec(length, k)), (resid, rows_spec(length, d)), (gains, full_spec((3, d)))]
     if have:
         ins.append((left, rows_spec(length, have)))
     return run_kernel(
         body, "down_embed", (clips,), [lengths], ins, [(w, n), (w_proj, pj)], outs,
-        [pltpu.VMEM((length, d), F32), pltpu.VMEM((clips, d), F32)], 44, 2 * m * n * k,
+        [pltpu.VMEM((length, d), F32), pltpu.VMEM((clips, d), F32)], 2 * m * n * k,
     )
 
 
-def attn_backward(qkv, d_mixed, lengths, clips, length, heads):
+def attn_backward(qkv, d_mixed, lengths, clips, length, heads, first=0, so_far=None):
     d = qkv.shape[1] // 3
     hd = d // heads
     scale = hd ** (-0.5)
@@ -458,7 +438,7 @@
     def body(s_refs, ins, outs, _scr, _wb, _wait):
         qkv_ref, do_ref, out = ins[0], ins[1], outs[0]
         lane = lax.broadcasted_iota(jnp.int32, (1, 128), 1)
-        ok = lax.broadcasted_iota(jnp.int32, (1, length), 1) < s_refs[0][pl.program_id(0)]
+        ok = lax.broadcasted_iota(jnp.int32, (1, length), 1) < s_refs[0][pl.program_id(0) + first]
         for t in range(d // 128):
             at = slice(t * 128, (t + 1) * 128)
             q, do = qkv_ref[:, at], do_ref[:, at]
@@ -484,12 +464,269 @@
             out[:, d + t * 128 : d + (t + 1) * 128] = to_low(dk * scale)
             out[:, 2 * d + t * 128 : 2 * d + (t + 1) * 128] = to_low(dv)
 
+    m = qkv.shape[0]
+    rows = lambda n: pl.BlockSpec((length, n), lambda i, *_: (i + first, 0))
+    ins = [(qkv, rows(3 * d)), (d_mixed, rows(d))] + ([] if so_far is None else [(so_far, hbm_spec())])
+    return run_kernel(
+        body, "attn_backward", (clips,), [lengths], ins, [], [((m, 3 * d), BF16, rows(3 * d))], [],
+        10 * clips * length * length * 256 * heads, None if so_far is None else 2,
+    )[0]
+
+
+def norm_back(resid, gain, d_out):
+    center = resid - jnp.mean(resid, axis=-1, keepdims=True)
+    rate = lax.rsqrt(jnp.mean(center * center, axis=-1, keepdims=True) + NORM_EPS)
+    unit = center * rate
+    d_unit = d_out * gain
+    tail = unit * jnp.mean(d_unit * unit, axis=-1, keepdims=True)
+    return rate * (d_unit - jnp.mean(d_unit, axis=-1, keepdims=True) - tail), jnp.sum(d_out * unit, axis=0, keepdims=True)
+
+
+def packed_rows(parts):
+    return sum(k // 8 * n // w for k, n, w in parts)
+
+
+def gradient_outs(parts, fast):
+    if not fast:
+        return [((k, n), F32, full_spec((k, n))) for k, n, _ in parts]
+    shape = (4, packed_rows(parts), parts[0][2])
+    return [(shape, BF16, full_spec(shape)), (shape, F32, full_spec(shape))]
+
+
+def emit_gradients(parts, accs, outs, core, fast):
+    if not fast:
+        for acc, out in zip(accs, outs):
+            out[...] = acc[...]
+        return
+    for yx in range(4):
+        for out, c in ((outs[0], 1 - core), (outs[1], core)):
+            at = 0
+            for (k, n, width), acc in zip(parts, accs):
+                rows = k // 8
+                first = pl.multiple_of((2 * yx + c) * rows, rows)
+                for j in range(n // width):
+                    out[yx, at : at + rows, :] = acc[pl.ds(first, rows), j * width : (j + 1) * width].astype(out.dtype)
+                    at += rows
+                rest = n % width
+                if rest:
+                    k2 = width // rest
+                    for i in range(k2):
+                        sub = rows // k2
+                        part = acc[pl.ds(pl.multiple_of(first + i * sub, sub), sub), n - rest : n]
+                        out[yx, at : at + sub, i * rest : (i + 1) * rest] = part.astype(out.dtype)
+                    at += rows // k2
+
+
+def contrast_back(joined, embed_raw, first_row, pj, micro, per):
+    rows = joined.shape[1]
+    row = lax.broadcasted_iota(jnp.int32, (rows, rows), 0)
+    col = lax.broadcasted_iota(jnp.int32, (rows, rows), 1)
+    same = row == col
+    lane = lax.broadcasted_iota(jnp.int32, (rows, 128), 1)
+    allowed, count = [], 0.0
+    for m in range(micro):
+        ids = joined[m, :, 2 * pj :].astype(F32)
+        left = jnp.where(lane == 0, ids, jnp.where(lane == 1, 1.0, 0.0))
+        right = jnp.where(lane == 0, 1.0, jnp.where(lane == 1, -ids, 0.0))
+        allowed.append((dot_nt(to_low(left), to_low(right)) != 0.0) | same)
+        count = count + jnp.sum(allowed[m].astype(F32))
+    scale = rows / count
+    total, d_embed = 0.0, None
+    pick_row = lax.broadcasted_iota(jnp.int32, (micro * per, rows), 0)
+    pick_col = lax.broadcasted_iota(jnp.int32, (micro * per, rows), 1)
+    for m in range(micro):
+        image = joined[m, :, pj : 2 * pj]
+        logits = dot_nt(joined[m, :, :pj], image) * LOGIT_SCALE
+        masked = jnp.where(allowed[m], logits, -1e30)
+        row_top, col_top = jnp.max(masked, axis=1, keepdims=True), jnp.max(masked, axis=0, keepdims=True)
+        row_lse = row_top + jnp.log(jnp.sum(jnp.exp(masked - row_top), axis=1, keepdims=True))
+        col_lse = col_top + jnp.log(jnp.sum(jnp.exp(masked - col_top), axis=0, keepdims=True))
+        matched = jnp.sum(jnp.where(same, logits, 0.0))
+        total = total + (jnp.sum(row_lse) - matched) + (jnp.sum(col_lse) - matched)
+        d_logits = jnp.exp(masked - row_lse) + jnp.exp(masked - col_lse) - jnp.where(same, 2.0, 0.0)
+        here = (pick_row >= m * per) & (pick_row < (m + 1) * per) & (pick_col == first_row + pick_row - m * per)
+        own = jnp.dot(here.astype(F32), d_logits * (scale * LOGIT_SCALE), precision=HIGHEST, preferred_element_type=F32)
+        part = jnp.dot(own, image.astype(F32), precision=HIGHEST, preferred_element_type=F32)
+        d_embed = part if d_embed is None else d_embed + part
+    rate = lax.rsqrt(jnp.sum(embed_raw * embed_raw, axis=-1, keepdims=True) + NORM_EPS)
+    inner = jnp.sum(embed_raw * d_embed, axis=-1, keepdims=True)
+    return total * scale, rate * d_embed - embed_raw * (rate * rate * rate * inner)
+
+
+def down_backward(joined, embed_raw, pooled, resid_out, hidden, slope, gains, lengths, place, w, w_proj, clips, length,
+                  fast):
+    k, d, pj = w.k, w.n, w_proj.n
+    kt = d
+    parts = [(k, d, d), (d, pj, d)]
+
+    def body(s_refs, ins, outs, scr, wb, wait):
+        g = pl.program_id(0)
+        sizes, at = s_refs
+        joined_ref, raw_ref, pooled_ref, x2_ref, u_ref, slope_ref, gain_ref = ins
+        loss_ref, dpre_ref, dout_ref, g3_ref = outs[:4]
+        d_pooled, d_raw_ref, acc = scr
+        wait(1, 0)
+
+        @pl.when(g == 0)
+        def _():
+            loss, d_raw = contrast_back(joined_ref[...], raw_ref[...], at[1], pj, MICRO, clips // MICRO)
+            loss_ref[...] = jnp.full((1, 128), loss, F32)
+            d_raw_ref[...] = to_low(d_raw)
+            d_pooled[...] = dot_nt(to_low(d_raw), wb[1][...])
+            acc[...] = jnp.zeros_like(acc)
+            g3_ref[...] = jnp.zeros_like(g3_ref)
+
+        size = sizes[g]
+        row = lax.broadcasted_iota(jnp.int32, (length, 1), 0)
+        weight = jnp.where(row < size, 1.0 / size.astype(F32), 0.0)
+        d_out, g_three = norm_back(x2_ref[...], gain_ref[2:3, :], d_pooled[pl.ds(g, 1), :] * weight)
+        g3_ref[...] += g_three
+        dout_ref[...] = d_out
+        d_low = to_low(d_out)
+        wait(0, 0)
+
+        def step(t, c):
+            cols = pl.ds(pl.multiple_of(t * kt, kt), kt)
+            d_hidden = dot_nt(d_low, wb[0][cols, :])
+            dpre_ref[:, cols] = to_low(d_hidden * slope_ref[:, cols].astype(F32))
+            acc[cols, :] += dot_tn(u_ref[:, cols], d_low)
+            return c
+
+        lax.fori_loop(0, k // kt, step, 0)
+
+        @pl.when(g == clips - 1)
+        def _():
+            g_proj = dot_tn(to_low(pooled_ref[...]), d_raw_ref[...])
+            outs[6][...] = g_proj
+            emit_gradients(parts, [acc, outs[6]], outs[4:6], at[0], fast)
+
     m = clips * length
+    outs = [((1, 128), F32, full_spec((1, 128))), ((m, k), BF16, rows_spec(length, k)),
+            ((m, d), F32, rows_spec(length, d)), ((1, d), F32, full_spec((1, d)))]
+    outs += gradient_outs(parts, fast) + [((d, pj), F32, full_spec((d, pj)))]
+    ins = [(joined, full_spec(joined.shape)), (embed_raw, full_spec((clips, pj))), (pooled, full_spec((clips, d))),
+           (resid_out, rows_spec(length, d)), (hidden, rows_spec(length, k)), (slope, rows_spec(length, k)),
+           (gains, full_spec((3, d)))]
     return run_kernel(
-        body, "attn_backward", (clips,), [lengths],
-        [(qkv, rows_spec(length, 3 * d)), (d_mixed, rows_spec(length, d))], [],
-        [((m, 3 * d), BF16, rows_spec(length, 3 * d))], [], 32, 10 * m * length * 256 * heads,
-    )[0]
+        body, "down_backward", (clips,), [lengths, place], ins, [(w, d), (w_proj, pj)], outs,
+        [pltpu.VMEM((clips, d), F32), pltpu.VMEM((clips, pj), BF16), pltpu.VMEM((k, d), F32)], 4 * m * d * k,
+    )
+
+
+def up_backward(d_pre, h_two, resid_mid, d_out, mixed, gains, place, w, w_out, clips, length, kt, fast):
+    d, n = w.k, w.n
+    parts = [(d, n, d), (d, d, d)]
+
+    def body(s_refs, ins, outs, scr, wb, wait):
+        g = pl.program_id(0)
+        (at,) = s_refs
+        dpre_ref, h_ref, x1_ref, dout_ref, o_ref, gain_ref = ins
+        dmid_ref, dmix_ref, g2_ref = outs[:3]
+        acc, acc_out, back = scr
+
+        @pl.when(g == 0)
+        def _():
+            acc[...] = jnp.zeros_like(acc)
+            acc_out[...] = jnp.zeros_like(acc_out)
+            g2_ref[...] = jnp.zeros_like(g2_ref)
+
+        h = h_ref[...]
+        back[...] = jnp.zeros_like(back)
+
+        def step(t, c):
+            cols = pl.ds(pl.multiple_of(t * kt, kt), kt)
+            wait(0, t)
+            dp = dpre_ref[:, cols]
+            acc[:, cols] += dot_tn(h, dp)
+            back[...] += dot_nt(dp, wb[0][:, cols])
+            return c
+
+        lax.fori_loop(0, n // kt, step, 0)
+        d_ln, g_two = norm_back(x1_ref[...], gain_ref[1:2, :], back[...])
+        g2_ref[...] += g_two
+        d_mid = dout_ref[...] + d_ln
+        dmid_ref[...] = d_mid
+        d_low = to_low(d_mid)
+        wait(1, 0)
+        acc_out[...] += dot_tn(o_ref[...], d_low)
+        dmix_ref[...] = to_low(dot_nt(d_low, wb[1][...]))
+
+        @pl.when(g == clips - 1)
+        def _():
+            emit_gradients(parts, [acc, acc_out], outs[3:5], at[0], fast)
+
+    m = clips * length
+    rows = rows_spec(length, d)
+    outs = [((m, d), F32, rows), ((m, d), BF16, rows), ((1, d), F32, full_spec((1, d)))] + gradient_outs(parts, fast)
+    ins = [(d_pre, rows_spec(length, n)), (h_two, rows), (resid_mid, rows), (d_out, rows), (mixed, rows),
+           (gains, full_spec((3, d)))]
+    return run_kernel(
+        body, "up_backward", (clips,), [place], ins, [(w, kt), (w_out, d)], outs,
+        [pltpu.VMEM((d, n), F32), pltpu.VMEM((d, d), F32), pltpu.VMEM((length, d), F32)], 4 * m * d * (n + d),
+    )
+
+
+def qkv_backward(d_qkv, h_one, resid_in, d_mid, patches, gains, g_two, g_three, place, w, clips, length, fast):
+    d, n, pk = w.k, w.n, patches.shape[1]
+    parts = [(d, n, d), (pk, d, d)]
+    extra = 16
+
+    def body(s_refs, ins, outs, scr, wb, wait):
+        g = pl.program_id(0)
+        (at,) = s_refs
+        dqkv_ref, h_ref, x0_ref, dmid_ref, patch_ref, gain_ref, g2_ref, g3_ref = ins
+        acc, acc_patch, back, acc_gain = scr
+
+        @pl.when(g == 0)
+        def _():
+            acc[...] = jnp.zeros_like(acc)
+            acc_patch[...] = jnp.zeros_like(acc_patch)
+            acc_gain[...] = jnp.zeros_like(acc_gain)
+            acc_gain[1:2, :] = g2_ref[...]
+            acc_gain[2:3, :] = g3_ref[...]
+
+        h = h_ref[...]
+        back[...] = jnp.zeros_like(back)
+
+        def step(t, c):
+            cols = pl.ds(pl.multiple_of(t * d, d), d)
+            wait(0, t)
+            dq = dqkv_ref[:, cols]
+            acc[:, cols] += dot_tn(h, dq)
+            back[...] += dot_nt(dq, wb[0][:, cols])
+            return c
+
+        lax.fori_loop(0, n // d, step, 0)
+        d_ln, g_one = norm_back(x0_ref[...], gain_ref[0:1, :], back[...])
+        acc_gain[0:1, :] += g_one
+        acc_patch[...] += dot_tn(patch_ref[...], to_low(dmid_ref[...] + d_ln))
+
+        @pl.when(g == clips - 1)
+        def _():
+            emit_gradients(parts, [acc, acc_patch], outs[:2], at[0], fast)
+            if fast:
+                rows = packed_rows(parts)
+                for yx in range(4):
+                    for out in outs[:2]:
+                        out[yx, rows : rows + extra, :] = acc_gain[...].astype(out.dtype)
+            else:
+                outs[2][...] = acc_gain[...]
+
+    m = clips * length
+    rows = rows_spec(length, d)
+    if fast:
+        shape = (4, packed_rows(parts) + extra, d)
+        outs = [(shape, BF16, full_spec(shape)), (shape, F32, full_spec(shape))]
+    else:
+        outs = gradient_outs(parts, fast) + [((extra, d), F32, full_spec((extra, d)))]
+    ins = [(d_qkv, rows_spec(length, n)), (h_one, rows), (resid_in, rows), (d_mid, rows),
+           (patches, rows_spec(length, pk)), (gains, full_spec((3, d))), (g_two, full_spec((1, d))),
+           (g_three, full_spec((1, d)))]
+    return run_kernel(
+        body, "qkv_backward", (clips,), [place], ins, [(w, d)], outs,
+        [pltpu.VMEM((d, n), F32), pltpu.VMEM((pk, d), F32), pltpu.VMEM((length, d), F32), pltpu.VMEM((extra, d), F32)],
+        4 * m * d * n,
+    )
 
 
 AXES = ("dp", "rep")
@@ -545,17 +782,6 @@
 
 def take(v, i, axis):
     return lax.dynamic_index_in_dim(v, i, axis, keepdims=False)
-
-
-def in_width(v, width):
-    n = v.shape[-1]
-    blocks = [v[..., i * width : (i + 1) * width] for i in range(n // width)]
-    rest = n % width
-    if rest:
-        last, k, rows = v[..., n - rest :], width // rest, v.shape[-2]
-        blocks.append(jnp.concatenate(
-            [last[..., i * (rows // k) : (i + 1) * (rows // k), :] for i in range(k)], axis=-1))
-    return jnp.concatenate(blocks, axis=-2)
 
 
 def from_width(v, rows, n):
@@ -569,30 +795,76 @@
     return jnp.concatenate(blocks, axis=1)
 
 
-def reduce_group(grads, kind, reps, width):
-    me, rep = lax.axis_index("dp"), lax.axis_index("rep")
-    y, x, c = me // 4, (me // 2) % 2, me % 2
-    split = [v.reshape(2, 2, 2, v.shape[0] // 8, v.shape[1]) for v in grads]
-    pick = lambda i: jnp.concatenate([in_width(take(v, i, 2), width) for v in split], axis=-2)
-    s = pick(c) + send(to_low(pick(1 - c)), reps, lambda dp, z: (dp ^ 1, z)).astype(F32)
-    for step in ((0, 1) if kind == 0 else (1, 0)):
-        bit, at, axis = ((2, x, s.ndim - 3), (4, y, 0))[step]
-        got = send(to_low(take(s, 1 - at, axis)), reps, lambda dp, z: (dp ^ bit, z))
-        s = take(s, at, axis) + got.astype(F32)
-    low = to_low(s)
-    got = send(low, reps, lambda dp, z: {0: (dp, 1), 3: (dp, 2)}.get(z))
-    low = to_low(low.astype(F32) + got.astype(F32))
-    got = send(low, reps, lambda dp, z: {1: (dp, 2), 2: (dp, 1)}.get(z))
-    low = to_low(low.astype(F32) + got.astype(F32))
-    got = send(low, reps, lambda dp, z: {1: (dp, 0), 2: (dp, 3)}.get(z))
-    total = jnp.where((rep == 1) | (rep == 2), low, got).astype(F32)
-    out, at = [], 0
-    for v in split:
-        rows, n = v.shape[-2:]
-        size = rows * n // width
-        out.append(from_width(total[at : at + size], rows, n))
-        at += size
-    return out
+class Sum:
+    def __init__(self, leave, stay, parts, reps):
+        self.reps, self.leave, self.stay, self.parts = reps, leave, stay, parts
+        me = lax.axis_index("dp")
+        self.y, self.x = me // 4, (me // 2) % 2
+        self.odd = lax.axis_index("rep") % 2 == 1
+
+    def hops(self, *pairs):
+        self.due = [(to_low(v), fn) for v, fn in pairs]
+
+    def core(self):
+        self.hops((self.leave, lambda dp, z: (dp ^ 1, z)))
+
+    def plane(self):
+        s = (self.stay + self.got[0].astype(F32)).reshape((2, 2) + self.stay.shape[1:])
+        half = s.shape[-2] // 2
+        self.a, self.b = s[:, :, :half], s[:, :, half:]
+        self.hops((take(self.a, 1 - self.x, 1), lambda dp, z: (dp ^ 2, z)),
+                  (take(self.b, 1 - self.y, 0), lambda dp, z: (dp ^ 4, z)))
+
+    def plane_again(self):
+        self.a = take(self.a, self.x, 1) + self.got[0].astype(F32)
+        self.b = take(self.b, self.y, 0) + self.got[1].astype(F32)
+        self.hops((take(self.a, 1 - self.y, 0), lambda dp, z: (dp ^ 4, z)),
+                  (take(self.b, 1 - self.x, 0), lambda dp, z: (dp ^ 2, z)))
+
+    def pair(self):
+        a = take(self.a, self.y, 0) + self.got[0].astype(F32)
+        b = take(self.b, self.x, 0) + self.got[1].astype(F32)
+        self.a = jnp.where(self.odd, b, a)
+        self.hops((jnp.where(self.odd, a, b), lambda dp, z: (dp, z ^ 1)))
+
+    def across(self):
+        self.a = to_low(self.a + self.got[0].astype(F32))
+        self.hops((self.a, lambda dp, z: (dp, z ^ 2)))
+
+    def share(self):
+        self.a = to_low(self.a.astype(F32) + self.got[0].astype(F32))
+        self.hops((self.a, lambda dp, z: (dp, z ^ 1)))
+
+    def result(self):
+        other = self.got[0]
+        total = jnp.concatenate([jnp.where(self.odd, other, self.a), jnp.where(self.odd, self.a, other)], axis=0)
+        total, out, at = total.astype(F32), [], 0
+        for k, n, width in self.parts:
+            rows = k // 8
+            size = rows * n // width
+            out.append(from_width(total[at : at + size], rows, n))
+            at += size
+        return out
+
+
+def go(sums, *values):
+    flat = [v for s in sums for v, _ in s.due]
+    out = lax.optimization_barrier(tuple(flat) + values)
+    at = 0
+    for s in sums:
+        s.got = tuple(send(out[at + i], s.reps, fn) for i, (_, fn) in enumerate(s.due))
+        at += len(s.due)
+    return out[at:]
+
+
+def order(sums, *values):
+    flat = [g for s in sums for g in s.got]
+    out = lax.optimization_barrier(tuple(flat) + values)
+    at = 0
+    for s in sums:
+        s.got = out[at : at + len(s.got)]
+        at += len(s.got)
+    return out[at:]
 
 
 def adam_step(weight, gradient, moment_one, moment_two, step_rate, decay):
@@ -637,7 +909,7 @@
         right = [down_i[:, j * d_i + dl : (j + 1) * d_i] for j in range(sub_i)]
         own_a = jnp.concatenate([a_qkv, a_out, a_up, down_a, a_proj], axis=1)
         own_i = jnp.concatenate([i_qkv, i_out, i_up, i_proj] + left + right, axis=1)
-        small, own_a, own_i = lax.optimization_barrier((small, own_a, own_i))
+        small, own_a = lax.optimization_barrier((small, own_a))
         cut_a = 4 * d_a + fr
         ca = Ring(own_a, 0, cut_a, rep_size), Ring(own_a, cut_a, own_a.shape[1] - cut_a, rep_size)
         widths, at, ci = [3 * d_i, d_i + half, half + pj, sub_i * dl, sub_i * (d_i - dl)], 0, []
@@ -645,7 +917,7 @@
             ci.append(Ring(own_i, at, wd, rep_size))
             at += wd
         swap = lambda v: send(v, rep_size, lambda dp, z: (dp ^ 1, z))
-        twin_a, twin_i = swap(own_a), swap(own_i)
+        twin_a = swap(own_a)
 
         ca[0].first()
         fence([(ca[0], "near"), (ca[1], "mine")], ())
@@ -674,11 +946,9 @@
 
     got = audio_in(patches, w_patch, gains_a, wa_qkv, clips, PAD_LEN, d_a)
     resid_in, h_one, qkv = got[:3]
-    full_qkv = take_weight(wa_qkv, got, 3)
     mixed = attn_forward(qkv, sizes, clips, PAD_LEN, HEADS_A, True)
-    got = out_norm(mixed, resid_in, gains_a, wa_out, clips, PAD_LEN, True)
+    got = out_norm(mixed, resid_in, gains_a, wa_out, clips, PAD_LEN)
     resid_mid, h_two = got[:2]
-    full_out = take_weight(wa_out, got, 2)
 
     if fast:
         (h_two,) = fence([(ca[1], "diag other near_twin"), (ci[0], "near"), (ci[1], "mine")], (h_two,))
@@ -686,13 +956,13 @@
         ci[0].second()
         ci[0].twin("near")
         ci[1].first()
+        twin_i = swap(own_i)
         ga1 = ca[1].group(twin_a)
         wa_up = Weight(d_a, ff_a, [(ga0, 4 * d_a, fr, 0, 0), (ga1, 0, ff_a - fr, fr, 0)])
         wa_down = Weight(ff_a, d_a, [(ga1, ff_a - fr + j * d_a, d_a, 0, j) for j in range(sub_a)], sub=sub_a)
         wa_proj = Weight(d_a, pj, [(ga1, 2 * ff_a - fr, pj, 0, 0)])
     got = up_gelu(h_two, wa_up, clips, PAD_LEN, 1024, True)
     hidden, slope = got[:2]
-    full_up = take_weight(wa_up, got, 2)
 
     if fast:
         hidden, tokens, twin_i = fence(
@@ -717,8 +987,7 @@
         wi_out = Weight(d_i, d_i, [(gi[1], 0, d_i, 0, 0)])
     got = down_embed(hidden, resid_mid, None, gains_a, sizes, wa_down, wa_proj, clips, PAD_LEN, d_a, True)
     aud_emb, embed_raw, pooled, resid_out = got[:4]
-    full_down, full_proj = take_weight(wa_down, got, 4), take_weight(wa_proj, got, 5)
-    mid_i, h_two_i = out_norm(mixed_i, tokens, gains_i, wi_out, clips, IMG_LEN, False)
+    mid_i, h_two_i = out_norm(mixed_i, tokens, gains_i, wi_out, clips, IMG_LEN)
 
     if fast:
         h_two_i, aud_emb = fence(
@@ -752,62 +1021,74 @@
     ids_low = jnp.broadcast_to(to_low(video_ids.reshape(clips, 1)), (clips, 128))
     joined = jnp.concatenate([aud_emb, img_emb, ids_low], axis=1).reshape(MICRO, clip_dev, 2 * pj + 128)
     joined = lax.all_gather(lax.all_gather(joined, "rep", axis=1, tiled=True), "dp", axis=1, tiled=True)
-    aud_all, img_all, all_ids = joined[:, :, :pj], joined[:, :, pj : 2 * pj], joined[:, :, 2 * pj]
-    rows = all_ids.shape[1]
-    same = jnp.arange(rows)[:, None] == jnp.arange(rows)[None, :]
-    allowed = jnp.logical_or(all_ids[:, :, None] != all_ids[:, None, :], same[None])
-    loss_scale = rows / jnp.sum(allowed.astype(F32))
-    logits = jnp.einsum("mid,mjd->mij", aud_all, img_all, preferred_element_type=F32) * LOGIT_SCALE
-    masked = jnp.where(allowed, logits, -1e30)
-    matched = jnp.sum(jnp.where(same, logits, 0.0), axis=2)
-    row_lse = jax.nn.logsumexp(masked, axis=2)
-    col_lse = jax.nn.logsumexp(masked, axis=1)
-    loss = (jnp.sum(row_lse - matched) + jnp.sum(col_lse - matched)) * loss_scale
-    start_row = lax.axis_index(AXES) * clip_dev
-    own = lambda v: lax.dynamic_slice_in_dim(v, start_row, clip_dev, 1)
-    own_masked = own(masked)
-    d_logits = (
-        jnp.exp(own_masked - own(row_lse)[:, :, None])
-        + jnp.exp(own_masked - col_lse[:, None, :])
-        - 2.0 * lax.dynamic_slice_in_dim(same.astype(F32), start_row, clip_dev, 0)[None]
-    ) * (loss_scale * LOGIT_SCALE)
-    d_embed = jnp.einsum("mij,mjd->mid", d_logits, img_all.astype(F32), precision=HIGHEST).reshape(clips, pj)
-
-    d_raw = to_low(jax.vjp(unit_rows, embed_raw)[1](d_embed)[0])
-    g_proj = dot_tn(to_low(pooled), d_raw)
-    d_pooled = dot_nt(d_raw, full_proj)
-    valid = jnp.arange(PAD_LEN)[None, :] < sizes[:, None]
-    pool_weight = valid.astype(F32) / sizes[:, None].astype(F32)
-    d_normed = (d_pooled[:, None, :] * pool_weight[:, :, None]).reshape(clips * PAD_LEN, d_a)
-    d_out, g_three = jax.vjp(normed, resid_out, gains_a[2])[1](d_normed)
-    d_low = to_low(d_out)
-    g_down = dot_tn(hidden, d_low)
-    d_pre = to_low(dot_nt(d_low, full_down) * slope.astype(F32))
-    g_up = dot_tn(h_two, d_pre)
-    d_ln_two, g_two = jax.vjp(normed, resid_mid, gains_a[1])[1](dot_nt(d_pre, full_up))
-    d_mid = d_out + d_ln_two
-    d_mid_low = to_low(d_mid)
-    g_out = dot_tn(mixed, d_mid_low)
-    d_mixed = to_low(dot_nt(d_mid_low, full_out))
-    d_qkv = attn_backward(qkv, d_mixed, sizes, clips, PAD_LEN, HEADS_A)
-    g_qkv = dot_tn(h_one, d_qkv)
-    d_ln_one, g_one = jax.vjp(normed, resid_in, gains_a[0])[1](dot_nt(d_qkv, full_qkv))
-    d_in = to_low(d_mid + d_ln_one)
-    g_patch = dot_tn(patches, d_in)
-    g_gains = jnp.stack([g_one, g_two, g_three])
-
-    if fast:
-        share = d_a // dp_size
-        gain_rows = jnp.pad(g_gains.reshape(3, dp_size, share).transpose(1, 0, 2).reshape(dp_size, 1, 3 * share),
-                            ((0, 0), (0, 7), (0, d_a - 3 * share))).reshape(dp_size * 8, d_a)
-        r_down, r_proj = reduce_group([g_down, g_proj], 0, rep_size, d_a)
-        (r_up,) = reduce_group([g_up], 1, rep_size, d_a)
-        r_qkv, r_out, r_patch, r_gain = reduce_group([g_qkv, g_out, g_patch, gain_rows], 0, rep_size, d_a)
-        summed = [r_patch, r_qkv, r_out, r_up, r_down, r_proj, r_gain[0, : 3 * share].reshape(3, share)]
+    me = lax.axis_index("dp").astype(jnp.int32)
+    first_row = lax.axis_index(AXES).astype(jnp.int32) * clip_dev
+    place = jnp.stack([me % 2, first_row])
+    got = down_backward(joined, embed_raw, pooled, resid_out, hidden, slope, gains_a, sizes, place, wa_down, wa_proj,
+                        clips, PAD_LEN, fast)
+    loss, d_pre, d_out, g_three = got[0][0, 0], *got[1:4]
+    if fast:
+        s_down = Sum(got[4], got[5], [(ff_a, d_a, d_a), (d_a, pj, d_a)], rep_size)
+        s_down.core()
+        (d_pre,) = go([s_down], d_pre)
+    up = up_backward(d_pre, h_two, resid_mid, d_out, mixed, gains_a, place, wa_up, wa_out, clips, PAD_LEN, 1024, fast)
+    d_mid, d_mixed, g_two = up[:3]
+    if fast:
+        (d_mixed,) = order([s_down], d_mixed)
+        s_down.plane()
+        s_up = Sum(up[3], up[4], [(d_a, ff_a, d_a), (d_a, d_a, d_a)], rep_size)
+        s_up.core()
+        (d_mixed,) = go([s_down, s_up], d_mixed)
+    d_qkv = attn_backward(qkv, d_mixed, sizes, clip_dev, PAD_LEN, HEADS_A)
+    if fast:
+        d_qkv, d_mixed = order([s_down, s_up], d_qkv, d_mixed)
+        s_down.plane_again()
+        s_up.plane()
+        d_qkv, d_mixed = go([s_down, s_up], d_qkv, d_mixed)
+    d_qkv = attn_backward(qkv, d_mixed, sizes, clips - clip_dev, PAD_LEN, HEADS_A, clip_dev, d_qkv)
+    if fast:
+        (d_qkv,) = order([s_down, s_up], d_qkv)
+        s_down.pair()
+        s_up.plane_again()
+        (d_qkv,) = go([s_down, s_up], d_qkv)
+    last = qkv_backward(d_qkv, h_one, resid_in, d_mid, patches, gains_a, g_two, g_three, place, wa_qkv, clips, PAD_LEN,
+                        fast)
+    share = d_a // dp_size
+    mine = lambda v: lax.dynamic_slice_in_dim(v[:3], me * share, share, 1)
+    if fast:
+        leave, stay = order([s_down, s_up], last[0], last[1])
+        s_qkv = Sum(leave, stay, [(d_a, 3 * d_a, d_a), (w_patch.shape[0], d_a, d_a), (128, d_a, d_a)], rep_size)
+        s_qkv.core()
+        s_down.across()
+        s_up.pair()
+        go([s_qkv, s_down, s_up])
+        order([s_qkv])
+        s_qkv.plane()
+        go([s_qkv])
+        order([s_down, s_up])
+        s_up.across()
+        s_down.share()
+        go([s_up, s_down])
+        order([s_qkv])
+        s_qkv.plane_again()
+        go([s_qkv])
+        order([s_qkv, s_up])
+        s_qkv.pair()
+        s_up.share()
+        go([s_qkv, s_up])
+        order([s_qkv])
+        s_qkv.across()
+        go([s_qkv])
+        s_qkv.share()
+        go([s_qkv])
+        r_down, r_proj = s_down.result()
+        r_up, r_out = s_up.result()
+        r_qkv, r_patch, r_gain = s_qkv.result()
+        summed = [r_patch, r_qkv, r_out, r_up, r_down, r_proj, mine(r_gain)]
     else:
-        summed = [lax.psum(lax.psum_scatter(v, "dp", scatter_dimension=0, tiled=True), "rep")
-                  for v in (g_patch, g_qkv, g_out, g_up, g_down, g_proj)]
-        summed.append(lax.psum(lax.psum_scatter(g_gains, "dp", scatter_dimension=1, tiled=True), "rep"))
+        grads = (last[1], last[0], up[4], up[3], got[4], got[5])
+        summed = [lax.psum(lax.psum_scatter(v, "dp", scatter_dimension=0, tiled=True), "rep") for v in grads]
+        summed.append(mine(lax.psum(last[2], AXES)))
     local_squares = sum(jnp.sum(v * v) for v in summed)
     grad_norm = jnp.sqrt(lax.psum(local_squares, "dp"))
     factor = jnp.minimum(1.0, CLIP_NORM / grad_norm)

time: 706 us -> 596 us (0.84)
  Pallas kernels: 181 us -> 283 us
  waiting for transfers between devices: 185 us -> 105 us
  local copies, waits for them, and re-layouts: 112 us -> 40.3 us
  matrix products: 50.1 us -> 0 us
    pallas_call x12 -> x16, Pallas kernels: 181 us -> 283 us  [run_kernel(): pl.pallas_call(kernel, grid_spec=pltpu.PrefetchScalarGridSpec(num_scalar_...]
    ppermute x62 -> x68, waiting for transfers between devices: 185 us -> 105 us  [send(): return lax.ppermute(value, AXES, joint_perm(reps, fn))]
    unnamed x336 -> x214, local copies, waits for them, and re-layouts: 84.3 us -> 21.8 us
    dot_general x13 -> x0, matrix products: 50.1 us -> none  [the longest x6 24.9 us: dot_tn(): lax.dot_general(a, b, (((0,), (0,)), ((), ())), preferred_element_type=F32)]
    reduce_sum x13 -> x0, other arithmetic: 11.8 us -> none  [the longest x6 8.34 us: normed(): center = resid - jnp.mean(resid, axis=-1, keepdims=True)]
    slice x5 -> x1, local copies, waits for them, and re-layouts: 9.95 us -> 0.13 us  [__init__(): self.mine = packed[:, col:col + width]]
    add x7 -> x8, other arithmetic: 13.1 us -> 17.9 us  [the longest x3 10.2 us: plane(): self.stay + self.got[0].astype(F32)]
    ppermute x62 -> x68, starting transfers between devices: 53.1 us -> 53 us  [send(): return lax.ppermute(value, AXES, joint_perm(reps, fn))]
  transfers between devices with their start and end apart: 62 -> 68, of which waited for: 20 -> 26; matrix products, arithmetic and copies ran while one was open for 14% -> 6% of each run, Pallas kernels for 23% -> 39%
where the time goes in v2:
time: 596 us; the launch traced here: 592 us
  Pallas kernels  283 us (47%)
  waiting for transfers between devices  105 us (18%)
  other arithmetic  54.7 us (9%)
  starting transfers between devices  53 us (9%)
  blocking collectives  47.1 us (8%)
  local copies, waits for them, and re-layouts  40.3 us (7%)
  between operations  8.62 us (1%)
    pallas_call x16, Pallas kernels, run_kernel(): pl.pallas_call(kernel, grid_spec=pltpu.PrefetchScalarGridSpec(num_scalar_...  283 us
    ppermute x68, waiting for transfers between devices, send(): return lax.ppermute(value, AXES, joint_perm(reps, fn))  105 us
    ppermute x68, starting transfers between devices, send(): return lax.ppermute(value, AXES, joint_perm(reps, fn))  53 us
    unnamed x214, local copies, waits for them, and re-layouts  21.8 us
    all_gather x1, blocking collectives, local(): lax.all_gather(joined, 'rep', axis=1, tiled=True)  13.4 us
    sub x7, other arithmetic, adam_step(): return (weight - step_rate * update, first_new, second_new)  13.3 us
    psum x1, blocking collectives, local(): grad_norm = jnp.sqrt(lax.psum(local_squares, 'dp'))  12.3 us
  transfers between devices with their start and end apart: 68, of which 26 were waited for; matrix products, arithmetic and copies ran while one was open for 6% of the time, Pallas kernels for 39%

profile of v2, /device:TPU:0, one launch (start us, length us, event | category | flops | bytes accessed | tf_op | source)
XLA Modules:
  0.0 591.5 jit_solution(6622872575296548494)
XLA Ops:
  3.8 11.3 %all-gather.1 = bf16[8,34,768]{2,1,0:T(8,128)(2,1)S(1)} all-gather(bf16[1,34,768]{2,1,0:T(8,128)(2,1)S(1)} %fusion.26), channel_id=2, replica_groups=mesh['dp'=8,'rep'=4] {'dp'}, dimensions={0}, use_global_device_ids=true | all-gather | bytes 470016 | tf_op jit(solution)/shard_map/all_gather | solution.py:897
  25.8 14.7 %collective-permute-done.refs_5_.refs_4_.refs_11_.refs_27_ = bf16[96,5120]{1,0:T(8,128)(2,1)S(1)} collective-permute-done((bf16[96,5120]{1,0:T(8,128)(2,1)S(1)}, bf16[96,5120]{1,0:T(8,128)(2,1)S(1)}, u32[]{:S(2)}, u32[]{:S(2)}) %collective-permute-start) | collective-permute-done | bytes 983072 | tf_op jit(solution)/shard_map/ppermute | solution.py:746
  47.8 15.8 %collective-permute-done.1.refs_6_.refs_5_.refs_12_.refs_28_ = bf16[96,5120]{1,0:T(8,128)(2,1)S(1)} collective-permute-done((bf16[96,5120]{1,0:T(8,128)(2,1)S(1)}, bf16[96,5120]{1,0:T(8,128)(2,1)S(1)}, u32[]{:S(2)}, u32[]{:S(2)}) %collective-permute-start.1) | collective-permute-done | bytes 983072 | tf_op jit(solution)/shard_map/ppermute | solution.py:746
  79.0 12.5 %audio_in.1 = (f32[960,768]{1,0:T(8,128)}, bf16[960,768]{1,0:T(8,128)(2,1)}, bf16[960,2304]{1,0:T(8,128)(2,1)}) custom-call(s32[8]{0:T(128)} %pad_add_fusion.1.refs_0_.refs_1_.refs_2_.refs_3_, bf16[960,256]{1,0:T(8,128)(2,1)} %bitcast.117, bf16[256,768]{1,0:T(8,128)(2,1)} %bitcast.119, f32[3,768]{1,0:T(4,128)} %reshape.123.refs_3_.refs_5_.refs_10_.refs_9_.refs_7_, ...), custom_call_target="tpu_custom_call" | custom-call | flops 3774873600 | bytes 19571712 | tf_op jit(solution)/shard_map/audio_in/pallas_call | solution.py:195
  91.5 10.2 %attn_forward.2.refs_1_.refs_8_ = bf16[960,768]{1,0:T(8,128)(2,1)} custom-call(s32[4]{0:T(128)} %reshape.112.refs_0_, bf16[960,2304]{1,0:T(8,128)(2,1)} %get-tuple-element.160.refs_1_), custom_call_target="tpu_custom_call" | custom-call | flops 2831155200 | bytes 5898240 | tf_op jit(solution)/shard_map/attn_forward/pallas_call | solution.py:195
  101.7 7.7 %out_norm.2 = (f32[960,768]{1,0:T(8,128)}, bf16[960,768]{1,0:T(8,128)(2,1)}) custom-call(s32[8]{0:T(128)} %pad_add_fusion.1.refs_0_.refs_1_.refs_2_.refs_3_, bf16[960,768]{1,0:T(8,128)(2,1)} %attn_forward.2.refs_1_.refs_8_, f32[960,768]{1,0:T(8,128)} %get-tuple-element.161.refs_2_.refs_4_, f32[3,768]{1,0:T(4,128)} %reshape.123.refs_3_.refs_5_.refs_10_.refs_9_.refs_7_, ...), custom_call_target="tpu_custom_call" | custom-call | flops 1132462080 | bytes 18686976 | tf_op jit(solution)/shard_map/out_norm/pallas_call | solution.py:195
  118.3 17.5 %up_gelu.2 = (bf16[960,3072]{1,0:T(8,128)(2,1)}, bf16[960,3072]{1,0:T(8,128)(2,1)}) custom-call(s32[8]{0:T(128)} %pad_add_fusion.1.refs_0_.refs_1_.refs_2_.refs_3_, s32[8]{0:T(128)} %pad_add_fusion.1.refs_0_.refs_1_.refs_2_.refs_3_, bf16[960,768]{1,0:T(8,128)(2,1)} %get-tuple-element.165.refs_2_.refs_5_, bf16[96,10240]{1,0:T(8,128)(2,1)} %copy-done, ...), custom_call_target="tpu_custom_call" | custom-call | flops 4529848320 | bytes 32931840 | tf_op jit(solution)/shard_map/up_gelu/pallas_call | solution.py:195
  149.8 19.1 %image_qkv.1.refs_1_ = bf16[1024,3840]{1,0:T(8,128)(2,1)} custom-call(s32[8]{0:T(128)} %pad_add_fusion.1.refs_0_.refs_1_.refs_2_.refs_3_, bf16[1024,1280]{1,0:T(8,128)(2,1)} %bitcast.114, f32[3,1280]{1,0:T(4,128)} %reshape.124.refs_2_.refs_3_.refs_5_, bf16[160,16384]{1,0:T(8,128)(2,1)} %constant_dynamic-update-slice_fusion.refs_3_.refs_4_.refs_11_.refs_7_.refs_15_, ...), custom_call_target="tpu_custom_call" | custom-call | flops 10066329600 | bytes 28359680 | tf_op jit(solution)/shard_map/image_qkv/pallas_call | solution.py:195
  169.4 13.5 %attn_forward.3.refs_1_ = bf16[1024,1280]{1,0:T(8,128)(2,1)} custom-call(s32[4]{0:T(128)} %broadcast_15_refs_0_.2.refs_0_, bf16[1024,3840]{1,0:T(8,128)(2,1)} %image_qkv.1.refs_1_), custom_call_target="tpu_custom_call" | custom-call | flops 4294967296 | bytes 10485760 | tf_op jit(solution)/shard_map/attn_forward/pallas_call | solution.py:195
  190.2 16.0 %down_embed.2 = (bf16[4,1024]{1,0:T(4,128)(2,1)}, f32[4,1024]{1,0:T(4,128)}, f32[4,768]{1,0:T(4,128)}, f32[960,768]{1,0:T(8,128)}) custom-call(s32[4]{0:T(128)} %reshape.112.refs_0_, s32[8]{0:T(128)} %pad_add_fusion.1.refs_0_.refs_1_.refs_2_.refs_3_, s32[8]{0:T(128)} %pad_add_fusion.1.refs_0_.refs_1_.refs_2_.refs_3_, ...), custom_call_target="tpu_custom_call" | custom-call | flops 4529848320 | bytes 31503360 | tf_op jit(solution)/shard_map/down_embed/pallas_call | solution.py:195
  206.2 11.0 %out_norm.3 = (f32[1024,1280]{1,0:T(8,128)}, bf16[1024,1280]{1,0:T(8,128)(2,1)}) custom-call(s32[8]{0:T(128)} %pad_add_fusion.1.refs_0_.refs_1_.refs_2_.refs_3_, bf16[1024,1280]{1,0:T(8,128)(2,1)} %attn_forward.3.refs_1_, bf16[1024,1280]{1,0:T(8,128)(2,1)} %bitcast.115, f32[3,1280]{1,0:T(4,128)} %reshape.124.refs_2_.refs_3_.refs_5_, ...), custom_call_target="tpu_custom_call" | custom-call | flops 3355443200 | bytes 30981120 | tf_op jit(solution)/shard_map/out_norm/pallas_call | solution.py:195
  223.0 26.4 %up_gelu.3.refs_1_.refs_3_ = bf16[1024,5120]{1,0:T(8,128)(2,1)} custom-call(s32[8]{0:T(128)} %pad_add_fusion.1.refs_0_.refs_1_.refs_2_.refs_3_, s32[8]{0:T(128)} %pad_add_fusion.1.refs_0_.refs_1_.refs_2_.refs_3_, bf16[1024,1280]{1,0:T(8,128)(2,1)} %get-tuple-element.191.refs_2_, ...), custom_call_target="tpu_custom_call" | custom-call | flops 13421772800 | bytes 48332800 | tf_op jit(solution)/shard_map/up_gelu/pallas_call | solution.py:195
  254.6 18.8 %down_left.1.refs_6_ = f32[1024,768]{1,0:T(8,128)} custom-call(s32[8]{0:T(128)} %pad_add_fusion.1.refs_0_.refs_1_.refs_2_.refs_3_, bf16[1024,5120]{1,0:T(8,128)(2,1)} %up_gelu.3.refs_1_.refs_3_, f32[1024,1280]{1,0:T(8,128)} %get-tuple-element.196.refs_2_.refs_4_, ...), custom_call_target="tpu_custom_call" | custom-call | flops 8053063680 | bytes 35258368 | tf_op jit(solution)/shard_map/down_left/pallas_call | solution.py:195
  277.6 19.3 %down_embed.3 = (bf16[4,1024]{1,0:T(4,128)(2,1)}, f32[4,1024]{1,0:T(4,128)}, f32[4,1280]{1,0:T(4,128)}) custom-call(s32[4]{0:T(128)} %broadcast_15_refs_0_.2.refs_0_, s32[8]{0:T(128)} %pad_add_fusion.1.refs_0_.refs_1_.refs_2_.refs_3_, s32[8]{0:T(128)} %pad_add_fusion.1.refs_0_.refs_1_.refs_2_.refs_3_, bf16[1024,5120]{1,0:T(8,128)(2,1)} %up_gelu.3.refs_1_.refs_3_, ...), custom_call_target="tpu_custom_call" | custom-call | flops 5368709120 | bytes 50719744 | tf_op jit(solution)/shard_map/down_embed/pallas_call | solution.py:195
  297.8 13.4 %all_gather.14 = bf16[2,8,2176]{2,0,1:T(2,128)(2,1)S(1)} all-gather(bf16[2,2,2176]{2,0,1:T(2,128)(2,1)S(1)} %copy.78), channel_id=1, replica_groups=mesh['dp'=8,'rep'=4] {'rep'}, dimensions={1}, use_global_device_ids=true | all-gather | bytes 87040 | tf_op jit(solution)/shard_map/all_gather | solution.py:1023
  311.2 10.1 %all_gather.15.refs_4_ = bf16[2,64,2176]{2,1,0:T(8,128)(2,1)} all-gather(bf16[2,8,2176]{2,1,0:T(8,128)(2,1)S(1)} %copy.79), channel_id=1, replica_groups=mesh['dp'=8,'rep'=4] {'dp'}, dimensions={1}, use_global_device_ids=true | all-gather | bytes 626688 | tf_op jit(solution)/shard_map/all_gather | solution.py:1023
  321.3 31.4 %down_backward.1 = (f32[1,128]{1,0:T(1,128)}, bf16[960,3072]{1,0:T(8,128)(2,1)}, f32[960,768]{1,0:T(8,128)}, f32[1,768]{1,0:T(1,128)}, bf16[4,512,768]{2,1,0:T(8...) custom-call(s32[4]{0:T(128)} %reshape.112.refs_0_, s32[2]{0:T(128)} %pad_add_fusion.refs_1_.refs_0_, ...), custom_call_target="tpu_custom_call" | custom-call | flops 9059696640 | bytes 56435200 | tf_op jit(solution)/shard_map/down_backward/pallas_call | solution.py:195
  353.2 27.6 %up_backward.1 = (f32[960,768]{1,0:T(8,128)}, bf16[960,768]{1,0:T(8,128)(2,1)}, f32[1,768]{1,0:T(1,128)}, bf16[4,480,768]{2,1,0:T(8,128)(2,1)}, f32[4,480,768]{2,1,0:T(8,128)}) custom-call(s32[2]{0:T(128)} %pad_add_fusion.refs_1_.refs_0_, s32[8]{0:T(128)} %pad_add_fusion.1.refs_0_.refs_1_.refs_2_.refs_3_, s32[8]{0:T(128)} %pad_add_fusion.1.refs_0_.refs_1_.refs_2_.refs_3_, ...), custom_call_target="tpu_custom_call" | custom-call | flops 11324620800 | bytes 57520128 | tf_op jit(solution)/shard_map/up_backward/pallas_call | solution.py:195
  389.3 15.4 %attn_backward.2.refs_3_ = bf16[960,2304]{1,0:T(8,128)(2,1)} custom-call(s32[4]{0:T(128)} %reshape.112.refs_0_, bf16[960,2304]{1,0:T(8,128)(2,1)} %get-tuple-element.160.refs_1_, bf16[960,768]{1,0:T(8,128)(2,1)} %get-tuple-element.235.refs_2_), custom_call_target="tpu_custom_call" | custom-call | flops 3538944000 | bytes 10321920 | tf_op jit(solution)/shard_map/attn_backward/pallas_call | solution.py:195
  424.1 15.5 %attn_backward.3.refs_2_ = bf16[960,2304]{1,0:T(8,128)(2,1)} custom-call(s32[4]{0:T(128)} %reshape.112.refs_0_, bf16[960,2304]{1,0:T(8,128)(2,1)} %get-tuple-element.160.refs_1_, bf16[960,768]{1,0:T(8,128)(2,1)} %get-tuple-element.235.refs_2_, bf16[960,2304]{1,0:T(8,128)(2,1)} %attn_backward.2.refs_3_), custom_call_target="tpu_custom_call", output_to_operand_aliasing={{}: (3, {})} | custom-call | flops 3538944000 | bytes 14745600 | tf_op jit(solution)/shard_map/attn_backward/pallas_call | solution.py:195
  455.4 21.6 %qkv_backward.1 = (bf16[4,336,768]{2,1,0:T(8,128)(2,1)}, f32[4,336,768]{2,1,0:T(8,128)}) custom-call(s32[2]{0:T(128)} %pad_add_fusion.refs_1_.refs_0_, s32[8]{0:T(128)} %pad_add_fusion.1.refs_0_.refs_1_.refs_2_.refs_3_, bf16[960,2304]{1,0:T(8,128)(2,1)} %attn_backward.3.refs_2_, bf16[960,768]{1,0:T(8,128)(2,1)} %get-tuple-element.246.refs_3_, ...), custom_call_target="tpu_custom_call" | custom-call | flops 6794772480 | bytes 28326912 | tf_op jit(solution)/shard_map/qkv_backward/pallas_call | solution.py:195
  493.8 9.4 %collective-permute-done.61 = bf16[240,768]{1,0:T(8,128)(2,1)} collective-permute-done((bf16[240,768]{1,0:T(8,128)(2,1)}, bf16[240,768]{1,0:T(8,128)(2,1)}, u32[]{:S(2)}, u32[]{:S(2)}) %collective-permute-start.61) | collective-permute-done | bytes 368672 | tf_op jit(solution)/shard_map/ppermute | solution.py:746
  512.5 9.8 %collective-permute-done.67 = bf16[256,768]{1,0:T(8,128)(2,1)S(1)} collective-permute-done((bf16[256,768]{1,0:T(8,128)(2,1)S(1)}, bf16[256,768]{1,0:T(8,128)(2,1)S(1)}, u32[]{:S(2)}, u32[]{:S(2)}) %collective-permute-start.67) | collective-permute-done | bytes 393248 | tf_op jit(solution)/shard_map/ppermute | solution.py:746
  563.0 12.3 %psum.7 = f32[]{:T(128)} all-reduce(f32[]{:T(128)S(6)} %add.301), channel_id=1, replica_groups=mesh['dp'=8,'rep'=4] {'dp'}, use_global_device_ids=true, to_apply=%region_7.8 | all-reduce | flops 1 | bytes 8 | tf_op jit(solution)/shard_map/psum | solution.py:1093
  (443 shorter events, 202.8 us)
Async XLA Ops:
  15.1 55.6 %collective-permute-start.5 = (bf16[96,10240]{1,0:T(8,128)(2,1)S(1)}, bf16[96,10240]{1,0:T(8,128)(2,1)S(1)}, u32[]{:S(2)}, u32[]{:S(2)}) collective-permute-start(bf16[96,10240]{1,0:T(8,128)(2,1)S(1)} %convert_dynamic-update-slice_fusion.2.refs_4_.refs_3_.refs_11_.refs_6_.refs_14_.refs_19_.refs_10_.refs_18_.r, ...), channel_id=1, source_target_pairs={{0,4},{1,5},{2,6},{3,7},{4,0},{5,1},{6,2},{7,3},{8,12},{9,13},{10,... | collective-permute-start | bytes 5898248 | tf_op jit(solution)/shard_map/ppermute | solution.py:746
  63.6 80.2 %collective-permute-start.18 = (bf16[160,16384]{1,0:T(8,128)(2,1)}, bf16[160,16384]{1,0:T(8,128)(2,1)}, u32[]{:S(2)}, u32[]{:S(2)}) collective-permute-start(bf16[160,16384]{1,0:T(8,128)(2,1)} %constant_dynamic-update-slice_fusion.refs_3_.refs_4_.refs_11_.refs_7_.refs_15_), channel_id=1, source_target_pairs={{0,4},{1,5},{2,6},{3,7},{4,0},{5,1},{6,2},{7,3},{8,12},{9,13},{10,... | collective-permute-start | bytes 15728648 | tf_op jit(solution)/shard_map/ppermute | solution.py:746
  72.7 36.7 %collective-permute-start.9 = (bf16[160,3840]{1,0:T(8,128)(2,1)}, bf16[160,3840]{1,0:T(8,128)(2,1)}, u32[]{:S(2)}, u32[]{:S(2)}) collective-permute-start(bf16[160,3840]{1,0:T(8,128)(2,1)} %param.35), channel_id=1, source_target_pairs={{0,8},{1,17},{2,10},{3,19},{4,12},{5,21},{6,14},{7,23},{8,0},{9,25... | collective-permute-start | bytes 3686408 | tf_op jit(solution)/shard_map/ppermute | solution.py:746
  73.3 36.1 %collective-permute-start.6 = (bf16[96,5120]{1,0:T(8,128)(2,1)S(1)}, bf16[96,5120]{1,0:T(8,128)(2,1)S(1)}, u32[]{:S(2)}, u32[]{:S(2)}) collective-permute-start(bf16[96,5120]{1,0:T(8,128)(2,1)S(1)} %collective-permute-done.4.refs_12_.refs_7_.refs_15_.refs_20_.refs_19_), channel_id=1, source_target_pairs={{0,16},{1,9},{2,18},{3,11},{4,20},{5,13},{6,22},{7,15},{8,24},{9,1... | collective-permute-start | bytes 2949128 | tf_op jit(solution)/shard_map/ppermute | solution.py:746
  74.8 34.6 %collective-permute-start.7 = (bf16[96,5120]{1,0:T(8,128)(2,1)S(1)}, bf16[96,5120]{1,0:T(8,128)(2,1)S(1)}, u32[]{:S(2)}, u32[]{:S(2)}) collective-permute-start(bf16[96,5120]{1,0:T(8,128)(2,1)S(1)} %collective-permute-done.4.refs_12_.refs_7_.refs_15_.refs_20_.refs_19_), channel_id=1, source_target_pairs={{0,1},{1,0},{2,3},{3,2},{4,5},{5,4},{6,7},{7,6},{8,9},{9,8},{10,11... | collective-permute-start | bytes 2949128 | tf_op jit(solution)/shard_map/ppermute | solution.py:746
  75.3 34.1 %collective-permute-start.8 = (bf16[96,5120]{1,0:T(8,128)(2,1)S(1)}, bf16[96,5120]{1,0:T(8,128)(2,1)}, u32[]{:S(2)}, u32[]{:S(2)}) collective-permute-start(bf16[96,5120]{1,0:T(8,128)(2,1)S(1)} %collective-permute-done.4.refs_12_.refs_7_.refs_15_.refs_20_.refs_19_), channel_id=1, source_target_pairs={{0,4},{1,5},{2,6},{3,7},{4,0},{5,1},{6,2},{7,3},{8,12},{9,13},{10,... | collective-permute-start | bytes 2949128 | tf_op jit(solution)/shard_map/ppermute | solution.py:746
  110.0 29.3 %collective-permute-start.12 = (bf16[160,3840]{1,0:T(8,128)(2,1)}, bf16[160,3840]{1,0:T(8,128)(2,1)}, u32[]{:S(2)}, u32[]{:S(2)}) collective-permute-start(bf16[160,3840]{1,0:T(8,128)(2,1)} %collective-permute-done.9.refs_4_), channel_id=1, source_target_pairs={{0,16},{1,9},{2,18},{3,11},{4,20},{5,13},{6,22},{7,15},{8,24},{9,1... | collective-permute-start | bytes 3686408 | tf_op jit(solution)/shard_map/ppermute | solution.py:746
  111.5 29.0 %collective-permute-start.13 = (bf16[160,3840]{1,0:T(8,128)(2,1)}, bf16[160,3840]{1,0:T(8,128)(2,1)}, u32[]{:S(2)}, u32[]{:S(2)}) collective-permute-start(bf16[160,3840]{1,0:T(8,128)(2,1)} %collective-permute-done.9.refs_4_), channel_id=1, source_target_pairs={{0,1},{1,0},{2,3},{3,2},{4,5},{5,4},{6,7},{7,6},{8,9},{9,8},{10,11... | collective-permute-start | bytes 3686408 | tf_op jit(solution)/shard_map/ppermute | solution.py:746
  112.9 27.6 %collective-permute-start.14 = (bf16[160,3840]{1,0:T(8,128)(2,1)}, bf16[160,3840]{1,0:T(8,128)(2,1)}, u32[]{:S(2)}, u32[]{:S(2)}) collective-permute-start(bf16[160,3840]{1,0:T(8,128)(2,1)} %collective-permute-done.9.refs_4_), channel_id=1, source_target_pairs={{0,4},{1,5},{2,6},{3,7},{4,0},{5,1},{6,2},{7,3},{8,12},{9,13},{10,... | collective-permute-start | bytes 3686408 | tf_op jit(solution)/shard_map/ppermute | solution.py:746
  114.4 29.4 %collective-permute-start.15 = (bf16[160,3840]{1,0:T(8,128)(2,1)}, bf16[160,3840]{1,0:T(8,128)(2,1)}, u32[]{:S(2)}, u32[]{:S(2)}) collective-permute-start(bf16[160,3840]{1,0:T(8,128)(2,1)} %pad_maximum_fusion), channel_id=1, source_target_pairs={{0,8},{1,17},{2,10},{3,19},{4,12},{5,21},{6,14},{7,23},{8,0},{9,25... | collective-permute-start | bytes 3686408 | tf_op jit(solution)/shard_map/ppermute | solution.py:746
  146.2 36.7 %collective-permute-start.19 = (bf16[160,3840]{1,0:T(8,128)(2,1)}, bf16[160,3840]{1,0:T(8,128)(2,1)S(1)}, u32[]{:S(2)}, u32[]{:S(2)}) collective-permute-start(bf16[160,3840]{1,0:T(8,128)(2,1)} %collective-permute-done.15.refs_5_.refs_4_), channel_id=1, source_target_pairs={{0,16},{1,9},{2,18},{3,11},{4,20},{5,13},{6,22},{7,15},{8,24},{9,1... | collective-permute-start | bytes 3686408 | tf_op jit(solution)/shard_map/ppermute | solution.py:746
  147.7 35.2 %collective-permute-start.20 = (bf16[160,3840]{1,0:T(8,128)(2,1)}, bf16[160,3840]{1,0:T(8,128)(2,1)S(1)}, u32[]{:S(2)}, u32[]{:S(2)}) collective-permute-start(bf16[160,3840]{1,0:T(8,128)(2,1)} %collective-permute-done.15.refs_5_.refs_4_), channel_id=1, source_target_pairs={{0,1},{1,0},{2,3},{3,2},{4,5},{5,4},{6,7},{7,6},{8,9},{9,8},{10,11... | collective-permute-start | bytes 3686408 | tf_op jit(solution)/shard_map/ppermute | solution.py:746
  149.1 33.8 %collective-permute-start.21 = (bf16[160,3840]{1,0:T(8,128)(2,1)}, bf16[160,3840]{1,0:T(8,128)(2,1)S(1)}, u32[]{:S(2)}, u32[]{:S(2)}) collective-permute-start(bf16[160,3840]{1,0:T(8,128)(2,1)} %collective-permute-done.15.refs_5_.refs_4_), channel_id=1, source_target_pairs={{0,4},{1,5},{2,6},{3,7},{4,0},{5,1},{6,2},{7,3},{8,12},{9,13},{10,... | collective-permute-start | bytes 3686408 | tf_op jit(solution)/shard_map/ppermute | solution.py:746
  149.1 33.7 %collective-permute-start.22 = (bf16[160,3584]{1,0:T(8,128)(2,1)}, bf16[160,3584]{1,0:T(8,128)(2,1)}, u32[]{:S(2)}, u32[]{:S(2)}) collective-permute-start(bf16[160,3584]{1,0:T(8,128)(2,1)} %pad_maximum_fusion.2), channel_id=1, source_target_pairs={{0,8},{1,17},{2,10},{3,19},{4,12},{5,21},{6,14},{7,23},{8,0},{9,25... | collective-permute-start | bytes 3440648 | tf_op jit(solution)/shard_map/ppermute | solution.py:746
  183.5 33.7 %collective-permute-start.25 = (bf16[160,3584]{1,0:T(8,128)(2,1)}, bf16[160,3584]{1,0:T(8,128)(2,1)}, u32[]{:S(2)}, u32[]{:S(2)}) collective-permute-start(bf16[160,3584]{1,0:T(8,128)(2,1)} %collective-permute-done.22.refs_12_.refs_16_), channel_id=1, source_target_pairs={{0,16},{1,9},{2,18},{3,11},{4,20},{5,13},{6,22},{7,15},{8,24},{9,1... | collective-permute-start | bytes 3440648 | tf_op jit(solution)/shard_map/ppermute | solution.py:746
  184.8 32.4 %collective-permute-start.26 = (bf16[160,3584]{1,0:T(8,128)(2,1)}, bf16[160,3584]{1,0:T(8,128)(2,1)}, u32[]{:S(2)}, u32[]{:S(2)}) collective-permute-start(bf16[160,3584]{1,0:T(8,128)(2,1)} %collective-permute-done.22.refs_12_.refs_16_), channel_id=1, source_target_pairs={{0,1},{1,0},{2,3},{3,2},{4,5},{5,4},{6,7},{7,6},{8,9},{9,8},{10,11... | collective-permute-start | bytes 3440648 | tf_op jit(solution)/shard_map/ppermute | solution.py:746
  185.5 31.8 %collective-permute-start.27 = (bf16[160,3584]{1,0:T(8,128)(2,1)}, bf16[160,3584]{1,0:T(8,128)(2,1)}, u32[]{:S(2)}, u32[]{:S(2)}) collective-permute-start(bf16[160,3584]{1,0:T(8,128)(2,1)} %collective-permute-done.22.refs_12_.refs_16_), channel_id=1, source_target_pairs={{0,4},{1,5},{2,6},{3,7},{4,0},{5,1},{6,2},{7,3},{8,12},{9,13},{10,... | collective-permute-start | bytes 3440648 | tf_op jit(solution)/shard_map/ppermute | solution.py:746
  186.9 30.3 %collective-permute-start.28 = (bf16[160,3072]{1,0:T(8,128)(2,1)}, bf16[160,3072]{1,0:T(8,128)(2,1)}, u32[]{:S(2)}, u32[]{:S(2)}) collective-permute-start(bf16[160,3072]{1,0:T(8,128)(2,1)} %pad_maximum_fusion.3), channel_id=1, source_target_pairs={{0,8},{1,17},{2,10},{3,19},{4,12},{5,21},{6,14},{7,23},{8,0},{9,25... | collective-permute-start | bytes 2949128 | tf_op jit(solution)/shard_map/ppermute | solution.py:746
  217.8 31.6 %collective-permute-start.31 = (bf16[160,3072]{1,0:T(8,128)(2,1)}, bf16[160,3072]{1,0:T(8,128)(2,1)S(1)}, u32[]{:S(2)}, u32[]{:S(2)}) collective-permute-start(bf16[160,3072]{1,0:T(8,128)(2,1)} %collective-permute-done.28.refs_4_), channel_id=1, source_target_pairs={{0,16},{1,9},{2,18},{3,11},{4,20},{5,13},{6,22},{7,15},{8,24},{9,1... | collective-permute-start | bytes 2949128 | tf_op jit(solution)/shard_map/ppermute | solution.py:746
  218.5 30.9 %collective-permute-start.32 = (bf16[160,3072]{1,0:T(8,128)(2,1)}, bf16[160,3072]{1,0:T(8,128)(2,1)}, u32[]{:S(2)}, u32[]{:S(2)}) collective-permute-start(bf16[160,3072]{1,0:T(8,128)(2,1)} %collective-permute-done.28.refs_4_), channel_id=1, source_target_pairs={{0,1},{1,0},{2,3},{3,2},{4,5},{5,4},{6,7},{7,6},{8,9},{9,8},{10,11... | collective-permute-start | bytes 2949128 | tf_op jit(solution)/shard_map/ppermute | solution.py:746
  219.5 30.0 %collective-permute-start.33 = (bf16[160,3072]{1,0:T(8,128)(2,1)}, bf16[160,3072]{1,0:T(8,128)(2,1)}, u32[]{:S(2)}, u32[]{:S(2)}) collective-permute-start(bf16[160,3072]{1,0:T(8,128)(2,1)} %collective-permute-done.28.refs_4_), channel_id=1, source_target_pairs={{0,4},{1,5},{2,6},{3,7},{4,0},{5,1},{6,2},{7,3},{8,12},{9,13},{10,... | collective-permute-start | bytes 2949128 | tf_op jit(solution)/shard_map/ppermute | solution.py:746
  220.3 29.0 %collective-permute-start.34 = (bf16[160,2048]{1,0:T(8,128)(2,1)}, bf16[160,2048]{1,0:T(8,128)(2,1)}, u32[]{:S(2)}, u32[]{:S(2)}) collective-permute-start(bf16[160,2048]{1,0:T(8,128)(2,1)} %pad_maximum_fusion.5), channel_id=1, source_target_pairs={{0,8},{1,17},{2,10},{3,19},{4,12},{5,21},{6,14},{7,23},{8,0},{9,25... | collective-permute-start | bytes 1966088 | tf_op jit(solution)/shard_map/ppermute | solution.py:746
  352.7 28.0 %collective-permute-start.44 = (bf16[4,512,768]{2,1,0:T(8,128)(2,1)}, bf16[4,512,768]{2,1,0:T(8,128)(2,1)S(1)}, u32[]{:S(2)}, u32[]{:S(2)}) collective-permute-start(bf16[4,512,768]{2,1,0:T(8,128)(2,1)} %get-tuple-element.214), channel_id=1, source_target_pairs={{0,4},{1,5},{2,6},{3,7},{4,0},{5,1},{6,2},{7,3},{8,12},{9,13},{10,... | collective-permute-start | bytes 9437192 | tf_op jit(solution)/shard_map/ppermute | solution.py:746
  420.0 26.7 %collective-permute-start.50 = (bf16[2,240,768]{2,1,0:T(8,128)(2,1)}, bf16[2,240,768]{2,1,0:T(8,128)(2,1)}, u32[]{:S(2)}, u32[]{:S(2)}) collective-permute-start(bf16[2,240,768]{2,1,0:T(8,128)(2,1)} %fusion.6), channel_id=1, source_target_pairs={{0,8},{1,9},{2,10},{3,11},{4,12},{5,13},{6,14},{7,15},{8,0},{9,1},... | collective-permute-start | bytes 2211848 | tf_op jit(solution)/shard_map/ppermute | solution.py:746
  (144 other events, 1286.4 us)

commit v3 on v2

--- a/solution.py
+++ b/solution.py
@@ -213,97 +213,93 @@
     return pl.BlockSpec((length, width), lambda i, *_: (i, 0))
 
 
-def image_qkv(tokens, gains, w, clips, length, tn):
+def attend(qkv_ref, out, d, heads, size):
+    length = qkv_ref.shape[0]
+    hd = d // heads
+    scale = hd ** (-0.5)
+    lane = lax.broadcasted_iota(jnp.int32, (1, 128), 1)
+    if size is not None:
+        ok = lax.broadcasted_iota(jnp.int32, (1, length), 1) < size
+    acc = {}
+    for h in range(heads):
+        lo, hi = h * hd, (h + 1) * hd
+        t0, t1 = lo // 128, (hi - 1) // 128
+        wide = (t1 - t0 + 1) * 128
+        col = lax.broadcasted_iota(jnp.int32, (1, wide), 1) + t0 * 128
+        q = qkv_ref[:, t0 * 128 : t0 * 128 + wide]
+        q = jnp.where((col >= lo) & (col < hi), q, jnp.zeros_like(q))
+        k = qkv_ref[:, d + t0 * 128 : d + t0 * 128 + wide]
+        v = qkv_ref[:, 2 * d + t0 * 128 : 2 * d + t0 * 128 + wide]
+        sc = dot_nt(q, k) * scale
+        if size is not None:
+            sc = jnp.where(ok, sc, -1e30)
+        e = jnp.exp(sc - jnp.max(sc, axis=-1, keepdims=True))
+        p = to_low(e * (1.0 / jnp.sum(e, axis=-1, keepdims=True)))
+        o = dot_f32(p, v)
+        for t in range(t0, t1 + 1):
+            part = o[:, (t - t0) * 128 : (t - t0 + 1) * 128]
+            full = lane + t * 128
+            acc[t] = jnp.where((full >= lo) & (full < hi), part, acc[t]) if t in acc else part
+            if min((t + 1) * 128, d) <= hi:
+                out[:, t * 128 : (t + 1) * 128] = to_low(acc.pop(t))
+
+
+def image_attention(tokens, gains, w, clips, length, heads, tn):
     d, n = w.k, w.n
 
-    def body(_s, ins, outs, _scr, wb, wait):
+    def body(_s, ins, outs, scr, wb, wait):
         h = to_low(normed(ins[0][...].astype(F32), ins[1][0:1, :]))
 
         def step(t, c):
             wait(0, t)
             at = pl.ds(pl.multiple_of(t * tn, tn), tn)
-            outs[0][:, at] = to_low(dot_f32(h, wb[0][:, at]))
+            scr[0][:, at] = to_low(dot_f32(h, wb[0][:, at]))
             return c
 
         lax.fori_loop(0, n // tn, step, 0)
-
+        attend(scr[0], outs[0], d, heads, None)
+
+    m = clips * length
     return run_kernel(
-        body, "image_qkv", (clips,), [],
+        body, "image_attention", (clips,), [],
         [(tokens, rows_spec(length, d)), (gains, full_spec((3, d)))], [(w, tn)],
-        [((clips * length, n), BF16, rows_spec(length, n))], [], 2 * clips * length * d * n,
+        [((m, d), BF16, rows_spec(length, d))], [pltpu.VMEM((length, n), BF16)], 2 * m * d * n,
     )[0]
 
 
-def audio_in(patches, w_patch, gains, w, clips, length, tn):
+def audio_attention(patches, w_patch, gains, lengths, w, w_out, clips, length, heads):
     d, n, pk = w.k, w.n, w_patch.shape[0]
 
-    def body(_s, ins, outs, _scr, wb, wait):
+    def body(s_refs, ins, outs, _scr, wb, wait):
+        x0_ref, h_ref, qkv_ref, mixed_ref, x1_ref, h2_ref = outs
         x0 = dot_f32(ins[0][...], ins[1][...])
-        outs[0][...] = x0
+        x0_ref[...] = x0
         h = to_low(normed(x0, ins[2][0:1, :]))
-        outs[1][...] = h
+        h_ref[...] = h
 
         def step(t, c):
             wait(0, t)
-            at = pl.ds(pl.multiple_of(t * tn, tn), tn)
-            outs[2][:, at] = to_low(dot_f32(h, wb[0][:, at]))
+            at = pl.ds(pl.multiple_of(t * d, d), d)
+            qkv_ref[:, at] = to_low(dot_f32(h, wb[0][:, at]))
             return c
 
-        lax.fori_loop(0, n // tn, step, 0)
+        lax.fori_loop(0, n // d, step, 0)
+        attend(qkv_ref, mixed_ref, d, heads, s_refs[0][pl.program_id(0)])
+        wait(1, 0)
+        x1 = x0_ref[...] + dot_f32(mixed_ref[...], wb[1][...])
+        x1_ref[...] = x1
+        h2_ref[...] = to_low(normed(x1, ins[2][1:2, :]))
 
     m = clips * length
+    rows = rows_spec(length, d)
     return run_kernel(
-        body, "audio_in", (clips,), [],
-        [(patches, rows_spec(length, pk)), (w_patch, full_spec((pk, d))), (gains, full_spec((3, d)))], [(w, tn)],
-        [((m, d), F32, rows_spec(length, d)), ((m, d), BF16, rows_spec(length, d)),
-         ((m, n), BF16, rows_spec(length, n))],
-        [], 2 * m * d * (n + pk),
+        body, "audio_attention", (clips,), [lengths],
+        [(patches, rows_spec(length, pk)), (w_patch, full_spec((pk, d))), (gains, full_spec((3, d)))],
+        [(w, d), (w_out, d)],
+        [((m, d), F32, rows), ((m, d), BF16, rows), ((m, n), BF16, rows_spec(length, n)), ((m, d), BF16, rows),
+         ((m, d), F32, rows), ((m, d), BF16, rows)],
+        [], 2 * m * d * (n + pk + d),
     )
-
-
-def attn_forward(qkv, lengths, clips, length, heads, masked):
-    d = qkv.shape[1] // 3
-    hd = d // heads
-    scale = hd ** (-0.5)
-    tiles = d // 128
-
-    def body(s_refs, ins, outs, _scr, _wb, _wait):
-        qkv_ref, out = ins[0], outs[0]
-        lane = lax.broadcasted_iota(jnp.int32, (1, 128), 1)
-        if masked:
-            keys = lax.broadcasted_iota(jnp.int32, (1, length), 1)
-            ok = keys < s_refs[0][pl.program_id(0)]
-        acc = {}
-        for h in range(heads):
-            lo, hi = h * hd, (h + 1) * hd
-            t0, t1 = lo // 128, (hi - 1) // 128
-            wide = (t1 - t0 + 1) * 128
-            at = slice(t0 * 128, t0 * 128 + wide)
-            col = lax.broadcasted_iota(jnp.int32, (1, wide), 1) + t0 * 128
-            mine = (col >= lo) & (col < hi)
-            q = qkv_ref[:, at]
-            q = jnp.where(mine, q, jnp.zeros_like(q))
-            k = qkv_ref[:, d + t0 * 128 : d + t0 * 128 + wide]
-            v = qkv_ref[:, 2 * d + t0 * 128 : 2 * d + t0 * 128 + wide]
-            sc = dot_nt(q, k) * scale
-            if masked:
-                sc = jnp.where(ok, sc, -1e30)
-            e = jnp.exp(sc - jnp.max(sc, axis=-1, keepdims=True))
-            p = to_low(e * (1.0 / jnp.sum(e, axis=-1, keepdims=True)))
-            o = dot_f32(p, v)
-            for t in range(t0, t1 + 1):
-                part = o[:, (t - t0) * 128 : (t - t0 + 1) * 128]
-                full = lane + t * 128
-                sel = (full >= lo) & (full < hi)
-                acc[t] = jnp.where(sel, part, acc[t]) if t in acc else part
-                if min((t + 1) * 128, d) <= hi:
-                    out[:, t * 128 : (t + 1) * 128] = to_low(acc.pop(t))
-
-    m = clips * length
-    return run_kernel(
-        body, "attn_forward", (clips,), [lengths], [(qkv, rows_spec(length, 3 * d))], [],
-        [((m, d), BF16, rows_spec(length, d))], [], 4 * m * length * 256 * heads,
-    )[0]
 
 
 def out_norm(mixed, resid, gains, w, clips, length):
@@ -438,7 +434,7 @@
     def body(s_refs, ins, outs, _scr, _wb, _wait):
         qkv_ref, do_ref, out = ins[0], ins[1], outs[0]
         lane = lax.broadcasted_iota(jnp.int32, (1, 128), 1)
-        ok = lax.broadcasted_iota(jnp.int32, (1, length), 1) < s_refs[0][pl.program_id(0) + first]
+        ok = lax.broadcasted_iota(jnp.int32, (length, 1), 0) < s_refs[0][pl.program_id(0) + first]
         for t in range(d // 128):
             at = slice(t * 128, (t + 1) * 128)
             q, do = qkv_ref[:, at], do_ref[:, at]
@@ -449,14 +445,14 @@
                 mine = (lane >= h * hd) & (lane < (h + 1) * hd)
                 qm = jnp.where(mine, q, jnp.zeros_like(q))
                 dom = jnp.where(mine, do, jnp.zeros_like(do))
-                sc = jnp.where(ok, dot_nt(qm, k) * scale, -1e30)
-                e = jnp.exp(sc - jnp.max(sc, axis=-1, keepdims=True))
-                p = e * (1.0 / jnp.sum(e, axis=-1, keepdims=True))
-                dp = dot_nt(dom, v)
-                ds = to_low(p * (dp - jnp.sum(p * dp, axis=-1, keepdims=True)))
-                dv_h = dot_tn(to_low(p), do)
-                dq_h = dot_f32(ds, k)
-                dk_h = dot_tn(ds, q)
+                sc = jnp.where(ok, dot_nt(k, qm) * scale, -1e30)
+                e = jnp.exp(sc - jnp.max(sc, axis=0, keepdims=True))
+                p = e * (1.0 / jnp.sum(e, axis=0, keepdims=True))
+                dp = dot_nt(v, dom)
+                ds = to_low(p * (dp - jnp.sum(p * dp, axis=0, keepdims=True)))
+                dv_h = dot_f32(to_low(p), do)
+                dq_h = dot_tn(ds, k)
+                dk_h = dot_f32(ds, q)
                 dq = dq_h if dq is None else jnp.where(mine, dq_h, dq)
                 dk = dk_h if dk is None else jnp.where(mine, dk_h, dk)
                 dv = dv_h if dv is None else jnp.where(mine, dv_h, dv)
@@ -902,15 +898,16 @@
     patches = patches.reshape(clips * PAD_LEN, -1)
     half, sub_i, sub_a = ff_i // 2, ff_i // d_i, ff_a // d_a
     dl = d_i * 3 // 5
-    fr = d_a * 8 // 3
-    if fast:
-        down_i, down_a = as_columns(i_down, i_qkv.shape[0]), as_columns(a_down, a_qkv.shape[0])
+    if fast:
+        down_a = as_columns(a_down, a_qkv.shape[0])
+        own_a = jnp.concatenate([a_qkv, a_out, a_up, down_a, a_proj], axis=1)
+        small, own_a, i_qkv, i_out, i_up, i_down, i_proj = lax.optimization_barrier(
+            (small, own_a, i_qkv, i_out, i_up, i_down, i_proj))
+        down_i = as_columns(i_down, i_qkv.shape[0])
         left = [down_i[:, j * d_i : j * d_i + dl] for j in range(sub_i)]
         right = [down_i[:, j * d_i + dl : (j + 1) * d_i] for j in range(sub_i)]
-        own_a = jnp.concatenate([a_qkv, a_out, a_up, down_a, a_proj], axis=1)
         own_i = jnp.concatenate([i_qkv, i_out, i_up, i_proj] + left + right, axis=1)
-        small, own_a = lax.optimization_barrier((small, own_a))
-        cut_a = 4 * d_a + fr
+        cut_a = 4 * d_a
         ca = Ring(own_a, 0, cut_a, rep_size), Ring(own_a, cut_a, own_a.shape[1] - cut_a, rep_size)
         widths, at, ci = [3 * d_i, d_i + half, half + pj, sub_i * dl, sub_i * (d_i - dl)], 0, []
         for wd in widths:
@@ -920,7 +917,7 @@
         twin_a = swap(own_a)
 
         ca[0].first()
-        fence([(ca[0], "near"), (ca[1], "mine")], ())
+        (own_i,) = fence([(ca[0], "near"), (ca[1], "mine")] + [(c, "mine") for c in ci], (own_i,))
         ca[0].second()
         ca[0].twin("near")
         ca[1].first()
@@ -944,11 +941,8 @@
     unpack = lambda v, g: v[:, : g.size].reshape(dp_size, 3, -1).transpose(1, 0, 2).reshape(3, -1).astype(F32)
     gains_a, gains_i = unpack(small[:, rp], a_gains), unpack(small[:, rp + 1], i_gains)
 
-    got = audio_in(patches, w_patch, gains_a, wa_qkv, clips, PAD_LEN, d_a)
-    resid_in, h_one, qkv = got[:3]
-    mixed = attn_forward(qkv, sizes, clips, PAD_LEN, HEADS_A, True)
-    got = out_norm(mixed, resid_in, gains_a, wa_out, clips, PAD_LEN)
-    resid_mid, h_two = got[:2]
+    resid_in, h_one, qkv, mixed, resid_mid, h_two = audio_attention(
+        patches, w_patch, gains_a, sizes, wa_qkv, wa_out, clips, PAD_LEN, HEADS_A)
 
     if fast:
         (h_two,) = fence([(ca[1], "diag other near_twin"), (ci[0], "near"), (ci[1], "mine")], (h_two,))
@@ -958,9 +952,9 @@
         ci[1].first()
         twin_i = swap(own_i)
         ga1 = ca[1].group(twin_a)
-        wa_up = Weight(d_a, ff_a, [(ga0, 4 * d_a, fr, 0, 0), (ga1, 0, ff_a - fr, fr, 0)])
-        wa_down = Weight(ff_a, d_a, [(ga1, ff_a - fr + j * d_a, d_a, 0, j) for j in range(sub_a)], sub=sub_a)
-        wa_proj = Weight(d_a, pj, [(ga1, 2 * ff_a - fr, pj, 0, 0)])
+        wa_up = Weight(d_a, ff_a, [(ga1, 0, ff_a, 0, 0)])
+        wa_down = Weight(ff_a, d_a, [(ga1, ff_a + j * d_a, d_a, 0, j) for j in range(sub_a)], sub=sub_a)
+        wa_proj = Weight(d_a, pj, [(ga1, 2 * ff_a, pj, 0, 0)])
     got = up_gelu(h_two, wa_up, clips, PAD_LEN, 1024, True)
     hidden, slope = got[:2]
 
@@ -973,8 +967,7 @@
         ci[2].first()
         gi = [ci[0].group(twin_i)]
         wi_qkv = Weight(d_i, 3 * d_i, [(gi[0], 0, 3 * d_i, 0, 0)])
-    qkv_i = image_qkv(tokens, gains_i, wi_qkv, clips, IMG_LEN, d_i)
-    mixed_i = attn_forward(qkv_i, img_sizes, clips, IMG_LEN, HEADS_I, False)
+    mixed_i = image_attention(tokens, gains_i, wi_qkv, clips, IMG_LEN, HEADS_I, d_i)
 
     if fast:
         mixed_i, hidden = fence(

time: 596 us -> 587 us (0.985)
  Pallas kernels: 283 us -> 269 us
    pallas_call x16 -> x13, Pallas kernels: 283 us -> 269 us  [run_kernel(): pl.pallas_call(kernel, grid_spec=pltpu.PrefetchScalarGridSpec(num_scalar_...]
    unnamed x214 -> x201, local copies, waits for them, and re-layouts: 21.8 us -> 19.1 us
  transfers between devices with their start and end apart: 68 -> 68, of which waited for: 26 -> 26; matrix products, arithmetic and copies ran while one was open for 6% -> 6% of each run, Pallas kernels for 39% -> 38%
where the time goes in v3:
time: 587 us; the launch traced here: 582 us
  Pallas kernels  269 us (46%)
  waiting for transfers between devices  102 us (17%)
  starting transfers between devices  58.1 us (10%)
  other arithmetic  54.8 us (9%)
  blocking collectives  51.3 us (9%)
  local copies, waits for them, and re-layouts  37.6 us (6%)
  between operations  8.69 us (1%)
    pallas_call x13, Pallas kernels, run_kernel(): pl.pallas_call(kernel, grid_spec=pltpu.PrefetchScalarGridSpec(num_scalar_...  269 us
    ppermute x68, waiting for transfers between devices, send(): return lax.ppermute(value, AXES, joint_perm(reps, fn))  102 us
    ppermute x68, starting transfers between devices, send(): return lax.ppermute(value, AXES, joint_perm(reps, fn))  58.1 us
    unnamed x201, local copies, waits for them, and re-layouts  19.1 us
    all_gather x1, blocking collectives, local(): lax.all_gather(joined, 'rep', axis=1, tiled=True)  14.6 us
    sub x7, other arithmetic, adam_step(): return (weight - step_rate * update, first_new, second_new)  13.3 us
    psum x1, blocking collectives, local(): grad_norm = jnp.sqrt(lax.psum(local_squares, 'dp'))  12.6 us
    all_gather x1, blocking collectives, local(): small = lax.all_gather(small, 'dp', axis=0)  12.5 us
  transfers between devices with their start and end apart: 68, of which 26 were waited for; matrix products, arithmetic and copies ran while one was open for 6% of the time, Pallas kernels for 38%

profile of v3, /device:TPU:0, one launch (start us, length us, event | category | flops | bytes accessed | tf_op | source)
XLA Modules:
  0.0 582.1 jit_solution(16386267412113779513)
XLA Ops:
  3.8 12.5 %all-gather.1 = bf16[8,34,768]{2,1,0:T(8,128)(2,1)} all-gather(bf16[1,34,768]{2,1,0:T(8,128)(2,1)S(1)} %fusion.26), channel_id=2, replica_groups=mesh['dp'=8,'rep'=4] {'dp'}, dimensions={0}, use_global_device_ids=true | all-gather | bytes 470016 | tf_op jit(solution)/shard_map/all_gather | solution.py:893
  36.6 11.8 %collective-permute-done.1.refs_8_.refs_16_.refs_19_.refs_12_ = bf16[96,3072]{1,0:T(8,128)(2,1)S(1)} collective-permute-done((bf16[96,3072]{1,0:T(8,128)(2,1)S(1)}, bf16[96,3072]{1,0:T(8,128)(2,1)S(1)}, u32[]{:S(2)}, u32[]{:S(2)}) %collective-permute-start.1) | collective-permute-done | bytes 589856 | tf_op jit(solution)/shard_map/ppermute | solution.py:742
  50.8 14.2 %collective-permute-done.4.refs_3_.refs_7_.refs_15_.refs_12_.refs_20_.refs_10_ = bf16[96,7168]{1,0:T(8,128)(2,1)S(1)} collective-permute-done((bf16[96,7168]{1,0:T(8,128)(2,1)S(1)}, bf16[96,7168]{1,0:T(8,128)(2,1)S(1)}, u32[]{:S(2)}, u32[]{:S(2)}) %collective-permute-start.4) | collective-permute-done | bytes 1376288 | tf_op jit(solution)/shard_map/ppermute | solution.py:742
  75.6 23.4 %audio_attention.1 = (f32[960,768]{1,0:T(8,128)}, bf16[960,768]{1,0:T(8,128)(2,1)}, bf16[960,2304]{1,0:T(8,128)(2,1)}, bf16[960,768]{1,0:T(8,128)(2,1)}, f32[960,768]{1,0:T(8,128)}, /*index=5*/bf16[960,768]{1,0:T(8,128)(2,1)}) custom-call(s32[4]{0:T(128)} %reshape.112.refs_0_, s32[8]{0:T(128)} %pad_add_fusion.1.refs_1_.refs_2_.refs_0_.refs_3_, ...), custom_call_target="tpu_custom_call" | custom-call | flops 4907335680 | bytes 30581760 | tf_op jit(solution)/shard_map/audio_attention/pallas_call | solution.py:195
  106.3 17.3 %up_gelu.2 = (bf16[960,3072]{1,0:T(8,128)(2,1)}, bf16[960,3072]{1,0:T(8,128)(2,1)}) custom-call(s32[8]{0:T(128)} %pad_add_fusion.1.refs_1_.refs_2_.refs_0_.refs_3_, bf16[960,768]{1,0:T(8,128)(2,1)} %get-tuple-element.183.refs_1_.refs_4_, bf16[96,10240]{1,0:T(8,128)(2,1)} %copy-done, bf16[96,7168]{1,0:T(8,128)(2,1)} %copy-done.2, bf16[96,7168]{1,0:T(8,128)(2,1)} %copy-done.3, ...), custom_call_target="tpu_custom_call" | custom-call | flops 4529848320 | bytes 25460736 | tf_op jit(solution)/shard_map/up_gelu/pallas_call | solution.py:195
  141.3 29.1 %image_attention.1.refs_1_ = bf16[1024,1280]{1,0:T(8,128)(2,1)} custom-call(s32[8]{0:T(128)} %pad_add_fusion.1.refs_1_.refs_2_.refs_0_.refs_3_, bf16[1024,1280]{1,0:T(8,128)(2,1)} %bitcast.114, f32[3,1280]{1,0:T(4,128)} %reshape.124.refs_2_.refs_3_.refs_5_, bf16[160,16384]{1,0:T(8,128)(2,1)} %get-tuple-element.188.refs_3_.refs_4_.refs_11_.refs_7_.refs_15_, ...), custom_call_target="tpu_custom_call" | custom-call | flops 10066329600 | bytes 23116800 | tf_op jit(solution)/shard_map/image_attention/pallas_call | solution.py:195
  176.0 16.0 %down_embed.2 = (bf16[4,1024]{1,0:T(4,128)(2,1)}, f32[4,1024]{1,0:T(4,128)}, f32[4,768]{1,0:T(4,128)}, f32[960,768]{1,0:T(8,128)}) custom-call(s32[4]{0:T(128)} %reshape.112.refs_0_, s32[8]{0:T(128)} %pad_add_fusion.1.refs_1_.refs_2_.refs_0_.refs_3_, s32[8]{0:T(128)} %pad_add_fusion.1.refs_1_.refs_2_.refs_0_.refs_3_, ...), custom_call_target="tpu_custom_call" | custom-call | flops 4529848320 | bytes 36221952 | tf_op jit(solution)/shard_map/down_embed/pallas_call | solution.py:195
  192.0 11.2 %out_norm.1 = (f32[1024,1280]{1,0:T(8,128)}, bf16[1024,1280]{1,0:T(8,128)(2,1)}) custom-call(s32[8]{0:T(128)} %pad_add_fusion.1.refs_1_.refs_2_.refs_0_.refs_3_, bf16[1024,1280]{1,0:T(8,128)(2,1)} %image_attention.1.refs_1_, bf16[1024,1280]{1,0:T(8,128)(2,1)} %bitcast.115, f32[3,1280]{1,0:T(4,128)} %reshape.124.refs_2_.refs_3_.refs_5_, ...), custom_call_target="tpu_custom_call" | custom-call | flops 3355443200 | bytes 30981120 | tf_op jit(solution)/shard_map/out_norm/pallas_call | solution.py:195
  209.0 26.6 %up_gelu.3.refs_1_.refs_3_ = bf16[1024,5120]{1,0:T(8,128)(2,1)} custom-call(s32[8]{0:T(128)} %pad_add_fusion.1.refs_1_.refs_2_.refs_0_.refs_3_, s32[8]{0:T(128)} %pad_add_fusion.1.refs_1_.refs_2_.refs_0_.refs_3_, bf16[1024,1280]{1,0:T(8,128)(2,1)} %get-tuple-element.212.refs_2_, ...), custom_call_target="tpu_custom_call" | custom-call | flops 13421772800 | bytes 48332800 | tf_op jit(solution)/shard_map/up_gelu/pallas_call | solution.py:195
  240.8 18.8 %down_left.1.refs_6_ = f32[1024,768]{1,0:T(8,128)} custom-call(s32[8]{0:T(128)} %pad_add_fusion.1.refs_1_.refs_2_.refs_0_.refs_3_, bf16[1024,5120]{1,0:T(8,128)(2,1)} %up_gelu.3.refs_1_.refs_3_, f32[1024,1280]{1,0:T(8,128)} %get-tuple-element.217.refs_2_.refs_4_, bf16[160,16384]{1,0:T(8,128)(2,1)} %get-tuple-element.188.refs_3_.refs_4_.refs_11_.refs_7_.refs_15_, ...), custom_call_target="tpu_custom_call" | custom-call | flops 8053063680 | bytes 35258368 | tf_op jit(solution)/shard_map/down_left/pallas_call | solution.py:195
  263.8 19.4 %down_embed.3 = (bf16[4,1024]{1,0:T(4,128)(2,1)}, f32[4,1024]{1,0:T(4,128)}, f32[4,1280]{1,0:T(4,128)}) custom-call(s32[4]{0:T(128)} %broadcast_15_refs_0_.2.refs_0_, s32[8]{0:T(128)} %pad_add_fusion.1.refs_1_.refs_2_.refs_0_.refs_3_, s32[8]{0:T(128)} %pad_add_fusion.1.refs_1_.refs_2_.refs_0_.refs_3_, bf16[1024,5120]{1,0:T(8,128)(2,1)} %up_gelu.3.refs_1_.refs_3_, ...), custom_call_target="tpu_custom_call" | custom-call | flops 5368709120 | bytes 50719744 | tf_op jit(solution)/shard_map/down_embed/pallas_call | solution.py:195
  284.1 14.6 %all_gather.14 = bf16[2,8,2176]{2,0,1:T(2,128)(2,1)S(1)} all-gather(bf16[2,2,2176]{2,0,1:T(2,128)(2,1)S(1)} %copy.78), channel_id=1, replica_groups=mesh['dp'=8,'rep'=4] {'rep'}, dimensions={1}, use_global_device_ids=true | all-gather | bytes 87040 | tf_op jit(solution)/shard_map/all_gather | solution.py:1016
  298.7 11.7 %all_gather.15.refs_4_ = bf16[2,64,2176]{2,1,0:T(8,128)(2,1)} all-gather(bf16[2,8,2176]{2,1,0:T(8,128)(2,1)S(1)} %copy.79), channel_id=1, replica_groups=mesh['dp'=8,'rep'=4] {'dp'}, dimensions={1}, use_global_device_ids=true | all-gather | bytes 626688 | tf_op jit(solution)/shard_map/all_gather | solution.py:1016
  310.4 31.4 %down_backward.1 = (f32[1,128]{1,0:T(1,128)}, bf16[960,3072]{1,0:T(8,128)(2,1)}, f32[960,768]{1,0:T(8,128)}, f32[1,768]{1,0:T(1,128)}, bf16[4,512,768]{2,1,0:T(8...) custom-call(s32[4]{0:T(128)} %reshape.112.refs_0_, s32[2]{0:T(128)} %pad_add_fusion.refs_1_.refs_0_, ...), custom_call_target="tpu_custom_call" | custom-call | flops 9059696640 | bytes 61153792 | tf_op jit(solution)/shard_map/down_backward/pallas_call | solution.py:195
  342.3 27.4 %up_backward.1 = (f32[960,768]{1,0:T(8,128)}, bf16[960,768]{1,0:T(8,128)(2,1)}, f32[1,768]{1,0:T(1,128)}, bf16[4,480,768]{2,1,0:T(8,128)(2,1)}, f32[4,480,768]{2,1,0:T(8,128)}) custom-call(s32[2]{0:T(128)} %pad_add_fusion.refs_1_.refs_0_, s32[8]{0:T(128)} %pad_add_fusion.1.refs_1_.refs_2_.refs_0_.refs_3_, s32[8]{0:T(128)} %pad_add_fusion.1.refs_1_.refs_2_.refs_0_.refs_3_, ...), custom_call_target="tpu_custom_call" | custom-call | flops 11324620800 | bytes 47689728 | tf_op jit(solution)/shard_map/up_backward/pallas_call | solution.py:195
  378.3 13.7 %attn_backward.2.refs_3_ = bf16[960,2304]{1,0:T(8,128)(2,1)} custom-call(s32[4]{0:T(128)} %reshape.112.refs_0_, bf16[960,2304]{1,0:T(8,128)(2,1)} %get-tuple-element.246.refs_1_, bf16[960,768]{1,0:T(8,128)(2,1)} %get-tuple-element.258.refs_2_), custom_call_target="tpu_custom_call" | custom-call | flops 3538944000 | bytes 10321920 | tf_op jit(solution)/shard_map/attn_backward/pallas_call | solution.py:195
  413.1 13.8 %attn_backward.3.refs_2_ = bf16[960,2304]{1,0:T(8,128)(2,1)} custom-call(s32[4]{0:T(128)} %reshape.112.refs_0_, bf16[960,2304]{1,0:T(8,128)(2,1)} %get-tuple-element.246.refs_1_, bf16[960,768]{1,0:T(8,128)(2,1)} %get-tuple-element.258.refs_2_, bf16[960,2304]{1,0:T(8,128)(2,1)} %attn_backward.2.refs_3_), custom_call_target="tpu_custom_call", output_to_operand_aliasing={{}: (3, {})} | custom-call | flops 3538944000 | bytes 14745600 | tf_op jit(solution)/shard_map/attn_backward/pallas_call | solution.py:195
  426.9 9.5 %collective-permute-done.48 = bf16[256,768]{1,0:T(8,128)(2,1)S(1)} collective-permute-done((bf16[256,768]{1,0:T(8,128)(2,1)}, bf16[256,768]{1,0:T(8,128)(2,1)S(1)}, u32[]{:S(2)}, u32[]{:S(2)}) %collective-permute-start.48) | collective-permute-done | bytes 393248 | tf_op jit(solution)/shard_map/ppermute | solution.py:742
  446.0 21.3 %qkv_backward.1 = (bf16[4,336,768]{2,1,0:T(8,128)(2,1)}, f32[4,336,768]{2,1,0:T(8,128)}) custom-call(s32[2]{0:T(128)} %pad_add_fusion.refs_1_.refs_0_, s32[8]{0:T(128)} %pad_add_fusion.1.refs_1_.refs_2_.refs_0_.refs_3_, bf16[960,2304]{1,0:T(8,128)(2,1)} %attn_backward.3.refs_2_, bf16[960,768]{1,0:T(8,128)(2,1)} %get-tuple-element.269.refs_3_, ...), custom_call_target="tpu_custom_call" | custom-call | flops 6794772480 | bytes 25967616 | tf_op jit(solution)/shard_map/qkv_backward/pallas_call | solution.py:195
  484.1 9.9 %collective-permute-done.61 = bf16[240,768]{1,0:T(8,128)(2,1)} collective-permute-done((bf16[240,768]{1,0:T(8,128)(2,1)}, bf16[240,768]{1,0:T(8,128)(2,1)}, u32[]{:S(2)}, u32[]{:S(2)}) %collective-permute-start.61) | collective-permute-done | bytes 368672 | tf_op jit(solution)/shard_map/ppermute | solution.py:742
  502.9 10.0 %collective-permute-done.67 = bf16[256,768]{1,0:T(8,128)(2,1)S(1)} collective-permute-done((bf16[256,768]{1,0:T(8,128)(2,1)S(1)}, bf16[256,768]{1,0:T(8,128)(2,1)S(1)}, u32[]{:S(2)}, u32[]{:S(2)}) %collective-permute-start.67) | collective-permute-done | bytes 393248 | tf_op jit(solution)/shard_map/ppermute | solution.py:742
  518.8 6.0 %collective-permute-done.63 = bf16[168,768]{1,0:T(8,128)(2,1)S(1)} collective-permute-done((bf16[168,768]{1,0:T(8,128)(2,1)S(1)}, bf16[168,768]{1,0:T(8,128)(2,1)S(1)}, u32[]{:S(2)}, u32[]{:S(2)}) %collective-permute-start.63) | collective-permute-done | bytes 258080 | tf_op jit(solution)/shard_map/ppermute | solution.py:742
  529.7 6.7 %collective-permute-done.66 = bf16[240,768]{1,0:T(8,128)(2,1)S(1)} collective-permute-done((bf16[240,768]{1,0:T(8,128)(2,1)S(1)}, bf16[240,768]{1,0:T(8,128)(2,1)S(1)}, u32[]{:S(2)}, u32[]{:S(2)}) %collective-permute-start.66) | collective-permute-done | bytes 368672 | tf_op jit(solution)/shard_map/ppermute | solution.py:742
  553.3 12.6 %psum.7 = f32[]{:T(128)} all-reduce(f32[]{:T(128)S(6)} %add.301), channel_id=1, replica_groups=mesh['dp'=8,'rep'=4] {'dp'}, use_global_device_ids=true, to_apply=%region_7.8 | all-reduce | flops 1 | bytes 8 | tf_op jit(solution)/shard_map/psum | solution.py:1086
  (427 shorter events, 184.6 us)
Async XLA Ops:
  16.3 48.7 %collective-permute-start.5 = (bf16[96,10240]{1,0:T(8,128)(2,1)S(1)}, bf16[96,10240]{1,0:T(8,128)(2,1)S(1)}, u32[]{:S(2)}, u32[]{:S(2)}) collective-permute-start(bf16[96,10240]{1,0:T(8,128)(2,1)S(1)} %convert_dynamic-update-slice_fusion.2.refs_6_.refs_14_.refs_2_.refs_11_.refs_19_.refs_9_.refs_17_.refs_10_), channel_id=1, source_target_pairs={{0,4},{1,5},{2,6},{3,7},{4,0},{5,1},{6,2},{7,3},{8,12},{9,13},{10,... | collective-permute-start | bytes 5898248 | tf_op jit(solution)/shard_map/ppermute | solution.py:742
  33.0 32.0 %collective-permute-start.4 = (bf16[96,7168]{1,0:T(8,128)(2,1)S(1)}, bf16[96,7168]{1,0:T(8,128)(2,1)S(1)}, u32[]{:S(2)}, u32[]{:S(2)}) collective-permute-start(bf16[96,7168]{1,0:T(8,128)(2,1)S(1)} %slice.170), channel_id=1, source_target_pairs={{0,8},{1,17},{2,10},{3,19},{4,12},{5,21},{6,14},{7,23},{8,0},{9,25... | collective-permute-start | bytes 4128776 | tf_op jit(solution)/shard_map/ppermute | solution.py:742
  35.1 99.2 %collective-permute-start.18 = (bf16[160,16384]{1,0:T(8,128)(2,1)}, bf16[160,16384]{1,0:T(8,128)(2,1)}, u32[]{:S(2)}, u32[]{:S(2)}) collective-permute-start(bf16[160,16384]{1,0:T(8,128)(2,1)} %get-tuple-element.188.refs_3_.refs_4_.refs_11_.refs_7_.refs_15_), channel_id=1, source_target_pairs={{0,4},{1,5},{2,6},{3,7},{4,0},{5,1},{6,2},{7,3},{8,12},{9,13},{10,... | collective-permute-start | bytes 15728648 | tf_op jit(solution)/shard_map/ppermute | solution.py:742
  66.9 32.2 %collective-permute-start.6 = (bf16[96,7168]{1,0:T(8,128)(2,1)S(1)}, bf16[96,7168]{1,0:T(8,128)(2,1)S(1)}, u32[]{:S(2)}, u32[]{:S(2)}) collective-permute-start(bf16[96,7168]{1,0:T(8,128)(2,1)S(1)} %collective-permute-done.4.refs_3_.refs_7_.refs_15_.refs_12_.refs_20_.refs_10_), channel_id=1, source_target_pairs={{0,16},{1,9},{2,18},{3,11},{4,20},{5,13},{6,22},{7,15},{8,24},{9,1... | collective-permute-start | bytes 4128776 | tf_op jit(solution)/shard_map/ppermute | solution.py:742
  67.5 31.9 %collective-permute-start.7 = (bf16[96,7168]{1,0:T(8,128)(2,1)S(1)}, bf16[96,7168]{1,0:T(8,128)(2,1)}, u32[]{:S(2)}, u32[]{:S(2)}) collective-permute-start(bf16[96,7168]{1,0:T(8,128)(2,1)S(1)} %collective-permute-done.4.refs_3_.refs_7_.refs_15_.refs_12_.refs_20_.refs_10_), channel_id=1, source_target_pairs={{0,1},{1,0},{2,3},{3,2},{4,5},{5,4},{6,7},{7,6},{8,9},{9,8},{10,11... | collective-permute-start | bytes 4128776 | tf_op jit(solution)/shard_map/ppermute | solution.py:742
  69.1 30.3 %collective-permute-start.8 = (bf16[96,7168]{1,0:T(8,128)(2,1)S(1)}, bf16[96,7168]{1,0:T(8,128)(2,1)}, u32[]{:S(2)}, u32[]{:S(2)}) collective-permute-start(bf16[96,7168]{1,0:T(8,128)(2,1)S(1)} %collective-permute-done.4.refs_3_.refs_7_.refs_15_.refs_12_.refs_20_.refs_10_), channel_id=1, source_target_pairs={{0,4},{1,5},{2,6},{3,7},{4,0},{5,1},{6,2},{7,3},{8,12},{9,13},{10,... | collective-permute-start | bytes 4128776 | tf_op jit(solution)/shard_map/ppermute | solution.py:742
  69.2 29.9 %collective-permute-start.9 = (bf16[160,3840]{1,0:T(8,128)(2,1)}, bf16[160,3840]{1,0:T(8,128)(2,1)}, u32[]{:S(2)}, u32[]{:S(2)}) collective-permute-start(bf16[160,3840]{1,0:T(8,128)(2,1)} %param.35), channel_id=1, source_target_pairs={{0,8},{1,17},{2,10},{3,19},{4,12},{5,21},{6,14},{7,23},{8,0},{9,25... | collective-permute-start | bytes 3686408 | tf_op jit(solution)/shard_map/ppermute | solution.py:742
  99.9 29.2 %collective-permute-start.12 = (bf16[160,3840]{1,0:T(8,128)(2,1)}, bf16[160,3840]{1,0:T(8,128)(2,1)}, u32[]{:S(2)}, u32[]{:S(2)}) collective-permute-start(bf16[160,3840]{1,0:T(8,128)(2,1)} %collective-permute-done.9.refs_4_), channel_id=1, source_target_pairs={{0,16},{1,9},{2,18},{3,11},{4,20},{5,13},{6,22},{7,15},{8,24},{9,1... | collective-permute-start | bytes 3686408 | tf_op jit(solution)/shard_map/ppermute | solution.py:742
  101.4 29.0 %collective-permute-start.13 = (bf16[160,3840]{1,0:T(8,128)(2,1)}, bf16[160,3840]{1,0:T(8,128)(2,1)}, u32[]{:S(2)}, u32[]{:S(2)}) collective-permute-start(bf16[160,3840]{1,0:T(8,128)(2,1)} %collective-permute-done.9.refs_4_), channel_id=1, source_target_pairs={{0,1},{1,0},{2,3},{3,2},{4,5},{5,4},{6,7},{7,6},{8,9},{9,8},{10,11... | collective-permute-start | bytes 3686408 | tf_op jit(solution)/shard_map/ppermute | solution.py:742
  104.9 29.4 %collective-permute-start.15 = (bf16[160,3840]{1,0:T(8,128)(2,1)}, bf16[160,3840]{1,0:T(8,128)(2,1)}, u32[]{:S(2)}, u32[]{:S(2)}) collective-permute-start(bf16[160,3840]{1,0:T(8,128)(2,1)} %get-tuple-element.181), channel_id=1, source_target_pairs={{0,8},{1,17},{2,10},{3,19},{4,12},{5,21},{6,14},{7,23},{8,0},{9,25... | collective-permute-start | bytes 3686408 | tf_op jit(solution)/shard_map/ppermute | solution.py:742
  134.8 35.6 %collective-permute-start.19 = (bf16[160,3840]{1,0:T(8,128)(2,1)}, bf16[160,3840]{1,0:T(8,128)(2,1)S(1)}, u32[]{:S(2)}, u32[]{:S(2)}) collective-permute-start(bf16[160,3840]{1,0:T(8,128)(2,1)} %collective-permute-done.15.refs_5_.refs_4_), channel_id=1, source_target_pairs={{0,16},{1,9},{2,18},{3,11},{4,20},{5,13},{6,22},{7,15},{8,24},{9,1... | collective-permute-start | bytes 3686408 | tf_op jit(solution)/shard_map/ppermute | solution.py:742
  136.2 34.2 %collective-permute-start.20 = (bf16[160,3840]{1,0:T(8,128)(2,1)}, bf16[160,3840]{1,0:T(8,128)(2,1)S(1)}, u32[]{:S(2)}, u32[]{:S(2)}) collective-permute-start(bf16[160,3840]{1,0:T(8,128)(2,1)} %collective-permute-done.15.refs_5_.refs_4_), channel_id=1, source_target_pairs={{0,1},{1,0},{2,3},{3,2},{4,5},{5,4},{6,7},{7,6},{8,9},{9,8},{10,11... | collective-permute-start | bytes 3686408 | tf_op jit(solution)/shard_map/ppermute | solution.py:742
  137.8 32.7 %collective-permute-start.21 = (bf16[160,3840]{1,0:T(8,128)(2,1)}, bf16[160,3840]{1,0:T(8,128)(2,1)}, u32[]{:S(2)}, u32[]{:S(2)}) collective-permute-start(bf16[160,3840]{1,0:T(8,128)(2,1)} %collective-permute-done.15.refs_5_.refs_4_), channel_id=1, source_target_pairs={{0,4},{1,5},{2,6},{3,7},{4,0},{5,1},{6,2},{7,3},{8,12},{9,13},{10,... | collective-permute-start | bytes 3686408 | tf_op jit(solution)/shard_map/ppermute | solution.py:742
  139.1 31.3 %collective-permute-start.22 = (bf16[160,3584]{1,0:T(8,128)(2,1)}, bf16[160,3584]{1,0:T(8,128)(2,1)}, u32[]{:S(2)}, u32[]{:S(2)}) collective-permute-start(bf16[160,3584]{1,0:T(8,128)(2,1)} %pad_maximum_fusion.2), channel_id=1, source_target_pairs={{0,8},{1,17},{2,10},{3,19},{4,12},{5,21},{6,14},{7,23},{8,0},{9,25... | collective-permute-start | bytes 3440648 | tf_op jit(solution)/shard_map/ppermute | solution.py:742
  171.0 32.2 %collective-permute-start.25 = (bf16[160,3584]{1,0:T(8,128)(2,1)}, bf16[160,3584]{1,0:T(8,128)(2,1)}, u32[]{:S(2)}, u32[]{:S(2)}) collective-permute-start(bf16[160,3584]{1,0:T(8,128)(2,1)} %collective-permute-done.22.refs_12_.refs_16_), channel_id=1, source_target_pairs={{0,16},{1,9},{2,18},{3,11},{4,20},{5,13},{6,22},{7,15},{8,24},{9,1... | collective-permute-start | bytes 3440648 | tf_op jit(solution)/shard_map/ppermute | solution.py:742
  172.1 31.2 %collective-permute-start.26 = (bf16[160,3584]{1,0:T(8,128)(2,1)}, bf16[160,3584]{1,0:T(8,128)(2,1)}, u32[]{:S(2)}, u32[]{:S(2)}) collective-permute-start(bf16[160,3584]{1,0:T(8,128)(2,1)} %collective-permute-done.22.refs_12_.refs_16_), channel_id=1, source_target_pairs={{0,1},{1,0},{2,3},{3,2},{4,5},{5,4},{6,7},{7,6},{8,9},{9,8},{10,11... | collective-permute-start | bytes 3440648 | tf_op jit(solution)/shard_map/ppermute | solution.py:742
  173.6 29.6 %collective-permute-start.27 = (bf16[160,3584]{1,0:T(8,128)(2,1)}, bf16[160,3584]{1,0:T(8,128)(2,1)}, u32[]{:S(2)}, u32[]{:S(2)}) collective-permute-start(bf16[160,3584]{1,0:T(8,128)(2,1)} %collective-permute-done.22.refs_12_.refs_16_), channel_id=1, source_target_pairs={{0,4},{1,5},{2,6},{3,7},{4,0},{5,1},{6,2},{7,3},{8,12},{9,13},{10,... | collective-permute-start | bytes 3440648 | tf_op jit(solution)/shard_map/ppermute | solution.py:742
  175.4 27.8 %collective-permute-start.28 = (bf16[160,3072]{1,0:T(8,128)(2,1)S(1)}, bf16[160,3072]{1,0:T(8,128)(2,1)}, u32[]{:S(2)}, u32[]{:S(2)}) collective-permute-start(bf16[160,3072]{1,0:T(8,128)(2,1)S(1)} %copy-done.62), channel_id=1, source_target_pairs={{0,8},{1,17},{2,10},{3,19},{4,12},{5,21},{6,14},{7,23},{8,0},{9,25... | collective-permute-start | bytes 2949128 | tf_op jit(solution)/shard_map/ppermute | solution.py:742
  203.8 31.7 %collective-permute-start.31 = (bf16[160,3072]{1,0:T(8,128)(2,1)}, bf16[160,3072]{1,0:T(8,128)(2,1)S(1)}, u32[]{:S(2)}, u32[]{:S(2)}) collective-permute-start(bf16[160,3072]{1,0:T(8,128)(2,1)} %collective-permute-done.28.refs_4_), channel_id=1, source_target_pairs={{0,16},{1,9},{2,18},{3,11},{4,20},{5,13},{6,22},{7,15},{8,24},{9,1... | collective-permute-start | bytes 2949128 | tf_op jit(solution)/shard_map/ppermute | solution.py:742
  205.3 30.3 %collective-permute-start.32 = (bf16[160,3072]{1,0:T(8,128)(2,1)}, bf16[160,3072]{1,0:T(8,128)(2,1)}, u32[]{:S(2)}, u32[]{:S(2)}) collective-permute-start(bf16[160,3072]{1,0:T(8,128)(2,1)} %collective-permute-done.28.refs_4_), channel_id=1, source_target_pairs={{0,1},{1,0},{2,3},{3,2},{4,5},{5,4},{6,7},{7,6},{8,9},{9,8},{10,11... | collective-permute-start | bytes 2949128 | tf_op jit(solution)/shard_map/ppermute | solution.py:742
  206.8 28.8 %collective-permute-start.33 = (bf16[160,3072]{1,0:T(8,128)(2,1)}, bf16[160,3072]{1,0:T(8,128)(2,1)}, u32[]{:S(2)}, u32[]{:S(2)}) collective-permute-start(bf16[160,3072]{1,0:T(8,128)(2,1)} %collective-permute-done.28.refs_4_), channel_id=1, source_target_pairs={{0,4},{1,5},{2,6},{3,7},{4,0},{5,1},{6,2},{7,3},{8,12},{9,13},{10,... | collective-permute-start | bytes 2949128 | tf_op jit(solution)/shard_map/ppermute | solution.py:742
  206.8 28.7 %collective-permute-start.34 = (bf16[160,2048]{1,0:T(8,128)(2,1)}, bf16[160,2048]{1,0:T(8,128)(2,1)}, u32[]{:S(2)}, u32[]{:S(2)}) collective-permute-start(bf16[160,2048]{1,0:T(8,128)(2,1)} %pad_maximum_fusion.5), channel_id=1, source_target_pairs={{0,8},{1,17},{2,10},{3,19},{4,12},{5,21},{6,14},{7,23},{8,0},{9,25... | collective-permute-start | bytes 1966088 | tf_op jit(solution)/shard_map/ppermute | solution.py:742
  341.8 27.8 %collective-permute-start.44 = (bf16[4,512,768]{2,1,0:T(8,128)(2,1)}, bf16[4,512,768]{2,1,0:T(8,128)(2,1)S(1)}, u32[]{:S(2)}, u32[]{:S(2)}) collective-permute-start(bf16[4,512,768]{2,1,0:T(8,128)(2,1)} %get-tuple-element.235), channel_id=1, source_target_pairs={{0,4},{1,5},{2,6},{3,7},{4,0},{5,1},{6,2},{7,3},{8,12},{9,13},{10,... | collective-permute-start | bytes 9437192 | tf_op jit(solution)/shard_map/ppermute | solution.py:742
  409.1 27.3 %collective-permute-start.50 = (bf16[2,240,768]{2,1,0:T(8,128)(2,1)}, bf16[2,240,768]{2,1,0:T(8,128)(2,1)}, u32[]{:S(2)}, u32[]{:S(2)}) collective-permute-start(bf16[2,240,768]{2,1,0:T(8,128)(2,1)} %fusion.6), channel_id=1, source_target_pairs={{0,8},{1,9},{2,10},{3,11},{4,12},{5,13},{6,14},{7,15},{8,0},{9,1},... | collective-permute-start | bytes 2211848 | tf_op jit(solution)/shard_map/ppermute | solution.py:742
  (137 other events, 1212.2 us)

commit v4 on v3

--- a/solution.py
+++ b/solution.py
@@ -322,9 +322,9 @@
 
 def gelu_parts(z):
     zz = z * z
-    t = jnp.tanh(GELU_C * z * (1.0 + GELU_A * zz))
-    half = 0.5 * (1.0 + t)
-    return z * half, half, t, zz
+    t = jnp.tanh(z * (GELU_C + (GELU_C * GELU_A) * zz))
+    hz = 0.5 * z
+    return hz + hz * t, hz, t, zz
 
 
 def up_gelu(h_two, w, clips, length, tn, keep):
@@ -337,10 +337,10 @@
             wait(0, t)
             at = pl.ds(pl.multiple_of(t * tn, tn), tn)
             z = dot_f32(h, wb[0][:, at])
-            u, half, tz, zz = gelu_parts(z)
+            u, hz, tz, zz = gelu_parts(z)
             outs[0][:, at] = to_low(u)
             if keep:
-                slope = half + z * (0.5 * GELU_C) * (1.0 - tz * tz) * (1.0 + (3.0 * GELU_A) * zz)
+                slope = 0.5 + 0.5 * tz + (hz - hz * (tz * tz)) * (GELU_C + (3.0 * GELU_C * GELU_A) * zz)
                 outs[1][:, at] = to_low(slope)
             return c
 
@@ -1032,18 +1032,27 @@
         s_up = Sum(up[3], up[4], [(d_a, ff_a, d_a), (d_a, d_a, d_a)], rep_size)
         s_up.core()
         (d_mixed,) = go([s_down, s_up], d_mixed)
-    d_qkv = attn_backward(qkv, d_mixed, sizes, clip_dev, PAD_LEN, HEADS_A)
-    if fast:
-        d_qkv, d_mixed = order([s_down, s_up], d_qkv, d_mixed)
-        s_down.plane_again()
-        s_up.plane()
-        d_qkv, d_mixed = go([s_down, s_up], d_qkv, d_mixed)
-    d_qkv = attn_backward(qkv, d_mixed, sizes, clips - clip_dev, PAD_LEN, HEADS_A, clip_dev, d_qkv)
-    if fast:
-        (d_qkv,) = order([s_down, s_up], d_qkv)
-        s_down.pair()
-        s_up.plane_again()
-        (d_qkv,) = go([s_down, s_up], d_qkv)
+    done, d_qkv = 0, None
+    calls = [clip_dev, (clips - clip_dev) // 2, clips - clip_dev - (clips - clip_dev) // 2]
+    for turn, count in enumerate(calls):
+        if count:
+            d_qkv = attn_backward(qkv, d_mixed, sizes, count, PAD_LEN, HEADS_A, done, d_qkv)
+        done += count
+        if fast:
+            if turn == 0:
+                d_qkv, d_mixed = order([s_down, s_up], d_qkv, d_mixed)
+                s_down.plane_again()
+                s_up.plane()
+                d_qkv, d_mixed = go([s_down, s_up], d_qkv, d_mixed)
+            elif turn == 1:
+                d_qkv, d_mixed = order([s_down], d_qkv, d_mixed)
+                s_down.pair()
+                d_qkv, d_mixed = go([s_down], d_qkv, d_mixed)
+            else:
+                (d_qkv,) = order([s_down, s_up], d_qkv)
+                s_down.across()
+                s_up.plane_again()
+                (d_qkv,) = go([s_down, s_up], d_qkv)
     last = qkv_backward(d_qkv, h_one, resid_in, d_mid, patches, gains_a, g_two, g_three, place, wa_qkv, clips, PAD_LEN,
                         fast)
     share = d_a // dp_size
@@ -1052,26 +1061,25 @@
         leave, stay = order([s_down, s_up], last[0], last[1])
         s_qkv = Sum(leave, stay, [(d_a, 3 * d_a, d_a), (w_patch.shape[0], d_a, d_a), (128, d_a, d_a)], rep_size)
         s_qkv.core()
-        s_down.across()
+        s_down.share()
         s_up.pair()
-        go([s_qkv, s_down, s_up])
+        go([s_qkv, s_up, s_down])
         order([s_qkv])
         s_qkv.plane()
         go([s_qkv])
-        order([s_down, s_up])
+        order([s_up])
         s_up.across()
-        s_down.share()
-        go([s_up, s_down])
+        go([s_up])
         order([s_qkv])
         s_qkv.plane_again()
         go([s_qkv])
+        order([s_qkv])
+        s_qkv.pair()
+        go([s_qkv])
         order([s_qkv, s_up])
-        s_qkv.pair()
+        s_qkv.across()
         s_up.share()
         go([s_qkv, s_up])
-        order([s_qkv])
-        s_qkv.across()
-        go([s_qkv])
         s_qkv.share()
         go([s_qkv])
         r_down, r_proj = s_down.result()

time: 587 us -> 581 us (0.990)
  waiting for transfers between devices: 102 us -> 90.7 us
    ppermute x68, waiting for transfers between devices: 102 us -> 90.7 us  [send(): return lax.ppermute(value, AXES, joint_perm(reps, fn))]
    pallas_call x13 -> x14, Pallas kernels: 269 us -> 272 us  [run_kernel(): pl.pallas_call(kernel, grid_spec=pltpu.PrefetchScalarGridSpec(num_scalar_...]
    unnamed x201 -> x193, local copies, waits for them, and re-layouts: 19.1 us -> 18.9 us
  transfers between devices with their start and end apart: 68 -> 68, of which waited for: 26 -> 25; matrix products, arithmetic and copies ran while one was open for 6% -> 5% of each run, Pallas kernels for 38% -> 38%
where the time goes in v4:
time: 581 us; the launch traced here: 576 us
  Pallas kernels  272 us (47%)
  waiting for transfers between devices  90.7 us (16%)
  starting transfers between devices  63.2 us (11%)
  other arithmetic  54.9 us (9%)
  blocking collectives  49.9 us (9%)
  local copies, waits for them, and re-layouts  37.4 us (6%)
  between operations  8.58 us (1%)
    pallas_call x14, Pallas kernels, run_kernel(): pl.pallas_call(kernel, grid_spec=pltpu.PrefetchScalarGridSpec(num_scalar_...  272 us
    ppermute x68, waiting for transfers between devices, send(): return lax.ppermute(value, AXES, joint_perm(reps, fn))  90.7 us
    ppermute x68, starting transfers between devices, send(): return lax.ppermute(value, AXES, joint_perm(reps, fn))  63.2 us
    unnamed x193, local copies, waits for them, and re-layouts  18.9 us
    all_gather x1, blocking collectives, local(): lax.all_gather(joined, 'rep', axis=1, tiled=True)  13.4 us
    sub x7, other arithmetic, adam_step(): return (weight - step_rate * update, first_new, second_new)  13.3 us
    all_gather x1, blocking collectives, local(): small = lax.all_gather(small, 'dp', axis=0)  12.5 us
    psum x1, blocking collectives, local(): grad_norm = jnp.sqrt(lax.psum(local_squares, 'dp'))  12.3 us
  transfers between devices with their start and end apart: 68, of which 25 were waited for; matrix products, arithmetic and copies ran while one was open for 5% of the time, Pallas kernels for 38%

profile of v4, /device:TPU:0, one launch (start us, length us, event | category | flops | bytes accessed | tf_op | source)
XLA Modules:
  0.0 576.5 jit_solution(10731383933378431070)
XLA Ops:
  3.8 12.5 %all-gather.1 = bf16[8,34,768]{2,1,0:T(8,128)(2,1)} all-gather(bf16[1,34,768]{2,1,0:T(8,128)(2,1)S(1)} %fusion.26), channel_id=2, replica_groups=mesh['dp'=8,'rep'=4] {'dp'}, dimensions={0}, use_global_device_ids=true | all-gather | bytes 470016 | tf_op jit(solution)/shard_map/all_gather | solution.py:893
  36.8 11.8 %collective-permute-done.1.refs_8_.refs_16_.refs_19_.refs_12_ = bf16[96,3072]{1,0:T(8,128)(2,1)S(1)} collective-permute-done((bf16[96,3072]{1,0:T(8,128)(2,1)S(1)}, bf16[96,3072]{1,0:T(8,128)(2,1)S(1)}, u32[]{:S(2)}, u32[]{:S(2)}) %collective-permute-start.1) | collective-permute-done | bytes 589856 | tf_op jit(solution)/shard_map/ppermute | solution.py:742
  51.0 14.2 %collective-permute-done.4.refs_3_.refs_7_.refs_15_.refs_12_.refs_20_.refs_10_ = bf16[96,7168]{1,0:T(8,128)(2,1)S(1)} collective-permute-done((bf16[96,7168]{1,0:T(8,128)(2,1)S(1)}, bf16[96,7168]{1,0:T(8,128)(2,1)S(1)}, u32[]{:S(2)}, u32[]{:S(2)}) %collective-permute-start.4) | collective-permute-done | bytes 1376288 | tf_op jit(solution)/shard_map/ppermute | solution.py:742
  75.8 23.4 %audio_attention.1 = (f32[960,768]{1,0:T(8,128)}, bf16[960,768]{1,0:T(8,128)(2,1)}, bf16[960,2304]{1,0:T(8,128)(2,1)}, bf16[960,768]{1,0:T(8,128)(2,1)}, f32[960,768]{1,0:T(8,128)}, /*index=5*/bf16[960,768]{1,0:T(8,128)(2,1)}) custom-call(s32[4]{0:T(128)} %reshape.112.refs_0_, s32[8]{0:T(128)} %pad_add_fusion.1.refs_1_.refs_2_.refs_0_.refs_3_, ...), custom_call_target="tpu_custom_call" | custom-call | flops 4907335680 | bytes 30581760 | tf_op jit(solution)/shard_map/audio_attention/pallas_call | solution.py:195
  106.4 17.6 %up_gelu.2 = (bf16[960,3072]{1,0:T(8,128)(2,1)}, bf16[960,3072]{1,0:T(8,128)(2,1)}) custom-call(s32[8]{0:T(128)} %pad_add_fusion.1.refs_1_.refs_2_.refs_0_.refs_3_, bf16[960,768]{1,0:T(8,128)(2,1)} %get-tuple-element.186.refs_1_.refs_4_, bf16[96,10240]{1,0:T(8,128)(2,1)} %copy-done, bf16[96,7168]{1,0:T(8,128)(2,1)} %copy-done.2, bf16[96,7168]{1,0:T(8,128)(2,1)} %copy-done.3, ...), custom_call_target="tpu_custom_call" | custom-call | flops 4529848320 | bytes 25460736 | tf_op jit(solution)/shard_map/up_gelu/pallas_call | solution.py:195
  124.1 5.3 collective-permute-done.12.refs_5_
  141.5 29.0 %image_attention.1.refs_1_ = bf16[1024,1280]{1,0:T(8,128)(2,1)} custom-call(s32[8]{0:T(128)} %pad_add_fusion.1.refs_1_.refs_2_.refs_0_.refs_3_, bf16[1024,1280]{1,0:T(8,128)(2,1)} %bitcast.114, f32[3,1280]{1,0:T(4,128)} %reshape.124.refs_2_.refs_3_.refs_5_, bf16[160,16384]{1,0:T(8,128)(2,1)} %get-tuple-element.191.refs_3_.refs_4_.refs_11_.refs_7_.refs_15_, ...), custom_call_target="tpu_custom_call" | custom-call | flops 10066329600 | bytes 23116800 | tf_op jit(solution)/shard_map/image_attention/pallas_call | solution.py:195
  176.0 16.0 %down_embed.2 = (bf16[4,1024]{1,0:T(4,128)(2,1)}, f32[4,1024]{1,0:T(4,128)}, f32[4,768]{1,0:T(4,128)}, f32[960,768]{1,0:T(8,128)}) custom-call(s32[4]{0:T(128)} %reshape.112.refs_0_, s32[8]{0:T(128)} %pad_add_fusion.1.refs_1_.refs_2_.refs_0_.refs_3_, s32[8]{0:T(128)} %pad_add_fusion.1.refs_1_.refs_2_.refs_0_.refs_3_, ...), custom_call_target="tpu_custom_call" | custom-call | flops 4529848320 | bytes 36221952 | tf_op jit(solution)/shard_map/down_embed/pallas_call | solution.py:195
  192.0 11.2 %out_norm.1 = (f32[1024,1280]{1,0:T(8,128)}, bf16[1024,1280]{1,0:T(8,128)(2,1)}) custom-call(s32[8]{0:T(128)} %pad_add_fusion.1.refs_1_.refs_2_.refs_0_.refs_3_, bf16[1024,1280]{1,0:T(8,128)(2,1)} %image_attention.1.refs_1_, bf16[1024,1280]{1,0:T(8,128)(2,1)} %bitcast.115, f32[3,1280]{1,0:T(4,128)} %reshape.124.refs_2_.refs_3_.refs_5_, ...), custom_call_target="tpu_custom_call" | custom-call | flops 3355443200 | bytes 30981120 | tf_op jit(solution)/shard_map/out_norm/pallas_call | solution.py:195
  209.0 25.8 %up_gelu.3.refs_1_.refs_3_ = bf16[1024,5120]{1,0:T(8,128)(2,1)} custom-call(s32[8]{0:T(128)} %pad_add_fusion.1.refs_1_.refs_2_.refs_0_.refs_3_, s32[8]{0:T(128)} %pad_add_fusion.1.refs_1_.refs_2_.refs_0_.refs_3_, bf16[1024,1280]{1,0:T(8,128)(2,1)} %get-tuple-element.215.refs_2_, ...), custom_call_target="tpu_custom_call" | custom-call | flops 13421772800 | bytes 48332800 | tf_op jit(solution)/shard_map/up_gelu/pallas_call | solution.py:195
  241.3 18.8 %down_left.1.refs_6_ = f32[1024,768]{1,0:T(8,128)} custom-call(s32[8]{0:T(128)} %pad_add_fusion.1.refs_1_.refs_2_.refs_0_.refs_3_, bf16[1024,5120]{1,0:T(8,128)(2,1)} %up_gelu.3.refs_1_.refs_3_, f32[1024,1280]{1,0:T(8,128)} %get-tuple-element.220.refs_2_.refs_4_, bf16[160,16384]{1,0:T(8,128)(2,1)} %get-tuple-element.191.refs_3_.refs_4_.refs_11_.refs_7_.refs_15_, ...), custom_call_target="tpu_custom_call" | custom-call | flops 8053063680 | bytes 35258368 | tf_op jit(solution)/shard_map/down_left/pallas_call | solution.py:195
  264.4 19.5 %down_embed.3 = (bf16[4,1024]{1,0:T(4,128)(2,1)}, f32[4,1024]{1,0:T(4,128)}, f32[4,1280]{1,0:T(4,128)}) custom-call(s32[4]{0:T(128)} %broadcast_15_refs_0_.2.refs_0_, s32[8]{0:T(128)} %pad_add_fusion.1.refs_1_.refs_2_.refs_0_.refs_3_, s32[8]{0:T(128)} %pad_add_fusion.1.refs_1_.refs_2_.refs_0_.refs_3_, bf16[1024,5120]{1,0:T(8,128)(2,1)} %up_gelu.3.refs_1_.refs_3_, ...), custom_call_target="tpu_custom_call" | custom-call | flops 5368709120 | bytes 50719744 | tf_op jit(solution)/shard_map/down_embed/pallas_call | solution.py:195
  284.7 13.4 %all_gather.14 = bf16[2,8,2176]{2,0,1:T(2,128)(2,1)S(1)} all-gather(bf16[2,2,2176]{2,0,1:T(2,128)(2,1)S(1)} %copy.79), channel_id=1, replica_groups=mesh['dp'=8,'rep'=4] {'rep'}, dimensions={1}, use_global_device_ids=true | all-gather | bytes 87040 | tf_op jit(solution)/shard_map/all_gather | solution.py:1016
  298.1 11.7 %all_gather.15.refs_4_ = bf16[2,64,2176]{2,1,0:T(8,128)(2,1)} all-gather(bf16[2,8,2176]{2,1,0:T(8,128)(2,1)S(1)} %copy.80), channel_id=1, replica_groups=mesh['dp'=8,'rep'=4] {'dp'}, dimensions={1}, use_global_device_ids=true | all-gather | bytes 626688 | tf_op jit(solution)/shard_map/all_gather | solution.py:1016
  309.8 31.5 %down_backward.1 = (f32[1,128]{1,0:T(1,128)}, bf16[960,3072]{1,0:T(8,128)(2,1)}, f32[960,768]{1,0:T(8,128)}, f32[1,768]{1,0:T(1,128)}, bf16[4,512,768]{2,1,0:T(8...) custom-call(s32[4]{0:T(128)} %reshape.112.refs_0_, s32[2]{0:T(128)} %pad_add_fusion.refs_1_.refs_0_, ...), custom_call_target="tpu_custom_call" | custom-call | flops 9059696640 | bytes 61153792 | tf_op jit(solution)/shard_map/down_backward/pallas_call | solution.py:195
  341.7 27.4 %up_backward.1 = (f32[960,768]{1,0:T(8,128)}, bf16[960,768]{1,0:T(8,128)(2,1)}, f32[1,768]{1,0:T(1,128)}, bf16[4,480,768]{2,1,0:T(8,128)(2,1)}, f32[4,480,768]{2,1,0:T(8,128)}) custom-call(s32[2]{0:T(128)} %pad_add_fusion.refs_1_.refs_0_, s32[8]{0:T(128)} %pad_add_fusion.1.refs_1_.refs_2_.refs_0_.refs_3_, s32[8]{0:T(128)} %pad_add_fusion.1.refs_1_.refs_2_.refs_0_.refs_3_, ...), custom_call_target="tpu_custom_call" | custom-call | flops 11324620800 | bytes 47689728 | tf_op jit(solution)/shard_map/up_backward/pallas_call | solution.py:195
  377.7 13.7 %attn_backward.3.refs_3_ = bf16[960,2304]{1,0:T(8,128)(2,1)} custom-call(s32[4]{0:T(128)} %reshape.112.refs_0_, bf16[960,2304]{1,0:T(8,128)(2,1)} %get-tuple-element.249.refs_1_, bf16[960,768]{1,0:T(8,128)(2,1)} %get-tuple-element.268.refs_2_), custom_call_target="tpu_custom_call" | custom-call | flops 3538944000 | bytes 10321920 | tf_op jit(solution)/shard_map/attn_backward/pallas_call | solution.py:195
  412.5 8.2 %attn_backward.4.refs_3_ = bf16[960,2304]{1,0:T(8,128)(2,1)} custom-call(s32[4]{0:T(128)} %reshape.112.refs_0_, bf16[960,2304]{1,0:T(8,128)(2,1)} %get-tuple-element.249.refs_1_, bf16[960,768]{1,0:T(8,128)(2,1)} %get-tuple-element.268.refs_2_, bf16[960,2304]{1,0:T(8,128)(2,1)} %attn_backward.3.refs_3_), custom_call_target="tpu_custom_call", output_to_operand_aliasing={{}: (3, {})} | custom-call | flops 1769472000 | bytes 14745600 | tf_op jit(solution)/shard_map/attn_backward/pallas_call | solution.py:195
  424.9 8.3 %attn_backward.5.refs_2_ = bf16[960,2304]{1,0:T(8,128)(2,1)} custom-call(s32[4]{0:T(128)} %reshape.112.refs_0_, bf16[960,2304]{1,0:T(8,128)(2,1)} %get-tuple-element.249.refs_1_, bf16[960,768]{1,0:T(8,128)(2,1)} %get-tuple-element.268.refs_2_, bf16[960,2304]{1,0:T(8,128)(2,1)} %attn_backward.4.refs_3_), custom_call_target="tpu_custom_call", output_to_operand_aliasing={{}: (3, {})} | custom-call | flops 1769472000 | bytes 14745600 | tf_op jit(solution)/shard_map/attn_backward/pallas_call | solution.py:195
  445.5 21.5 %qkv_backward.1 = (bf16[4,336,768]{2,1,0:T(8,128)(2,1)}, f32[4,336,768]{2,1,0:T(8,128)}) custom-call(s32[2]{0:T(128)} %pad_add_fusion.refs_1_.refs_0_, s32[8]{0:T(128)} %pad_add_fusion.1.refs_1_.refs_2_.refs_0_.refs_3_, bf16[960,2304]{1,0:T(8,128)(2,1)} %attn_backward.5.refs_2_, bf16[960,768]{1,0:T(8,128)(2,1)} %get-tuple-element.278.refs_3_, ...), custom_call_target="tpu_custom_call" | custom-call | flops 6794772480 | bytes 25967616 | tf_op jit(solution)/shard_map/qkv_backward/pallas_call | solution.py:195
  486.1 9.7 %collective-permute-done.62 = bf16[240,768]{1,0:T(8,128)(2,1)} collective-permute-done((bf16[240,768]{1,0:T(8,128)(2,1)}, bf16[240,768]{1,0:T(8,128)(2,1)}, u32[]{:S(2)}, u32[]{:S(2)}) %collective-permute-start.62) | collective-permute-done | bytes 368672 | tf_op jit(solution)/shard_map/ppermute | solution.py:742
  510.6 8.4 %collective-permute-done.63 = bf16[240,768]{1,0:T(8,128)(2,1)S(1)} collective-permute-done((bf16[240,768]{1,0:T(8,128)(2,1)S(1)}, bf16[240,768]{1,0:T(8,128)(2,1)S(1)}, u32[]{:S(2)}, u32[]{:S(2)}) %collective-permute-start.63) | collective-permute-done | bytes 368672 | tf_op jit(solution)/shard_map/ppermute | solution.py:742
  525.5 6.6 %collective-permute-done.64 = bf16[168,768]{1,0:T(8,128)(2,1)S(1)} collective-permute-done((bf16[168,768]{1,0:T(8,128)(2,1)S(1)}, bf16[168,768]{1,0:T(8,128)(2,1)S(1)}, u32[]{:S(2)}, u32[]{:S(2)}) %collective-permute-start.64) | collective-permute-done | bytes 258080 | tf_op jit(solution)/shard_map/ppermute | solution.py:742
  547.9 12.3 %psum.7 = f32[]{:T(128)} all-reduce(f32[]{:T(128)S(6)} %add.301), channel_id=1, replica_groups=mesh['dp'=8,'rep'=4] {'dp'}, use_global_device_ids=true, to_apply=%region_7.8 | all-reduce | flops 1 | bytes 8 | tf_op jit(solution)/shard_map/psum | solution.py:1094
  (420 shorter events, 190.1 us)
Async XLA Ops:
  16.3 48.9 %collective-permute-start.5 = (bf16[96,10240]{1,0:T(8,128)(2,1)S(1)}, bf16[96,10240]{1,0:T(8,128)(2,1)S(1)}, u32[]{:S(2)}, u32[]{:S(2)}) collective-permute-start(bf16[96,10240]{1,0:T(8,128)(2,1)S(1)} %convert_dynamic-update-slice_fusion.2.refs_6_.refs_14_.refs_2_.refs_11_.refs_19_.refs_9_.refs_17_.refs_10_), channel_id=1, source_target_pairs={{0,4},{1,5},{2,6},{3,7},{4,0},{5,1},{6,2},{7,3},{8,12},{9,13},{10,... | collective-permute-start | bytes 5898248 | tf_op jit(solution)/shard_map/ppermute | solution.py:742
  33.2 32.0 %collective-permute-start.4 = (bf16[96,7168]{1,0:T(8,128)(2,1)S(1)}, bf16[96,7168]{1,0:T(8,128)(2,1)S(1)}, u32[]{:S(2)}, u32[]{:S(2)}) collective-permute-start(bf16[96,7168]{1,0:T(8,128)(2,1)S(1)} %slice.170), channel_id=1, source_target_pairs={{0,8},{1,17},{2,10},{3,19},{4,12},{5,21},{6,14},{7,23},{8,0},{9,25... | collective-permute-start | bytes 4128776 | tf_op jit(solution)/shard_map/ppermute | solution.py:742
  35.2 99.2 %collective-permute-start.18 = (bf16[160,16384]{1,0:T(8,128)(2,1)}, bf16[160,16384]{1,0:T(8,128)(2,1)}, u32[]{:S(2)}, u32[]{:S(2)}) collective-permute-start(bf16[160,16384]{1,0:T(8,128)(2,1)} %get-tuple-element.191.refs_3_.refs_4_.refs_11_.refs_7_.refs_15_), channel_id=1, source_target_pairs={{0,4},{1,5},{2,6},{3,7},{4,0},{5,1},{6,2},{7,3},{8,12},{9,13},{10,... | collective-permute-start | bytes 15728648 | tf_op jit(solution)/shard_map/ppermute | solution.py:742
  67.0 32.2 %collective-permute-start.6 = (bf16[96,7168]{1,0:T(8,128)(2,1)S(1)}, bf16[96,7168]{1,0:T(8,128)(2,1)S(1)}, u32[]{:S(2)}, u32[]{:S(2)}) collective-permute-start(bf16[96,7168]{1,0:T(8,128)(2,1)S(1)} %collective-permute-done.4.refs_3_.refs_7_.refs_15_.refs_12_.refs_20_.refs_10_), channel_id=1, source_target_pairs={{0,16},{1,9},{2,18},{3,11},{4,20},{5,13},{6,22},{7,15},{8,24},{9,1... | collective-permute-start | bytes 4128776 | tf_op jit(solution)/shard_map/ppermute | solution.py:742
  67.6 31.9 %collective-permute-start.7 = (bf16[96,7168]{1,0:T(8,128)(2,1)S(1)}, bf16[96,7168]{1,0:T(8,128)(2,1)}, u32[]{:S(2)}, u32[]{:S(2)}) collective-permute-start(bf16[96,7168]{1,0:T(8,128)(2,1)S(1)} %collective-permute-done.4.refs_3_.refs_7_.refs_15_.refs_12_.refs_20_.refs_10_), channel_id=1, source_target_pairs={{0,1},{1,0},{2,3},{3,2},{4,5},{5,4},{6,7},{7,6},{8,9},{9,8},{10,11... | collective-permute-start | bytes 4128776 | tf_op jit(solution)/shard_map/ppermute | solution.py:742
  69.2 30.3 %collective-permute-start.8 = (bf16[96,7168]{1,0:T(8,128)(2,1)S(1)}, bf16[96,7168]{1,0:T(8,128)(2,1)}, u32[]{:S(2)}, u32[]{:S(2)}) collective-permute-start(bf16[96,7168]{1,0:T(8,128)(2,1)S(1)} %collective-permute-done.4.refs_3_.refs_7_.refs_15_.refs_12_.refs_20_.refs_10_), channel_id=1, source_target_pairs={{0,4},{1,5},{2,6},{3,7},{4,0},{5,1},{6,2},{7,3},{8,12},{9,13},{10,... | collective-permute-start | bytes 4128776 | tf_op jit(solution)/shard_map/ppermute | solution.py:742
  69.4 29.8 %collective-permute-start.9 = (bf16[160,3840]{1,0:T(8,128)(2,1)}, bf16[160,3840]{1,0:T(8,128)(2,1)}, u32[]{:S(2)}, u32[]{:S(2)}) collective-permute-start(bf16[160,3840]{1,0:T(8,128)(2,1)} %param.35), channel_id=1, source_target_pairs={{0,8},{1,17},{2,10},{3,19},{4,12},{5,21},{6,14},{7,23},{8,0},{9,25... | collective-permute-start | bytes 3686408 | tf_op jit(solution)/shard_map/ppermute | solution.py:742
  100.1 29.2 %collective-permute-start.12 = (bf16[160,3840]{1,0:T(8,128)(2,1)}, bf16[160,3840]{1,0:T(8,128)(2,1)}, u32[]{:S(2)}, u32[]{:S(2)}) collective-permute-start(bf16[160,3840]{1,0:T(8,128)(2,1)} %collective-permute-done.9.refs_4_), channel_id=1, source_target_pairs={{0,16},{1,9},{2,18},{3,11},{4,20},{5,13},{6,22},{7,15},{8,24},{9,1... | collective-permute-start | bytes 3686408 | tf_op jit(solution)/shard_map/ppermute | solution.py:742
  101.5 29.0 %collective-permute-start.13 = (bf16[160,3840]{1,0:T(8,128)(2,1)}, bf16[160,3840]{1,0:T(8,128)(2,1)}, u32[]{:S(2)}, u32[]{:S(2)}) collective-permute-start(bf16[160,3840]{1,0:T(8,128)(2,1)} %collective-permute-done.9.refs_4_), channel_id=1, source_target_pairs={{0,1},{1,0},{2,3},{3,2},{4,5},{5,4},{6,7},{7,6},{8,9},{9,8},{10,11... | collective-permute-start | bytes 3686408 | tf_op jit(solution)/shard_map/ppermute | solution.py:742
  104.6 25.9 %collective-permute-start.14 = (bf16[160,3840]{1,0:T(8,128)(2,1)}, bf16[160,3840]{1,0:T(8,128)(2,1)}, u32[]{:S(2)}, u32[]{:S(2)}) collective-permute-start(bf16[160,3840]{1,0:T(8,128)(2,1)} %collective-permute-done.9.refs_4_), channel_id=1, source_target_pairs={{0,4},{1,5},{2,6},{3,7},{4,0},{5,1},{6,2},{7,3},{8,12},{9,13},{10,... | collective-permute-start | bytes 3686408 | tf_op jit(solution)/shard_map/ppermute | solution.py:742
  105.0 29.4 %collective-permute-start.15 = (bf16[160,3840]{1,0:T(8,128)(2,1)}, bf16[160,3840]{1,0:T(8,128)(2,1)}, u32[]{:S(2)}, u32[]{:S(2)}) collective-permute-start(bf16[160,3840]{1,0:T(8,128)(2,1)} %get-tuple-element.184), channel_id=1, source_target_pairs={{0,8},{1,17},{2,10},{3,19},{4,12},{5,21},{6,14},{7,23},{8,0},{9,25... | collective-permute-start | bytes 3686408 | tf_op jit(solution)/shard_map/ppermute | solution.py:742
  134.9 35.6 %collective-permute-start.19 = (bf16[160,3840]{1,0:T(8,128)(2,1)}, bf16[160,3840]{1,0:T(8,128)(2,1)S(1)}, u32[]{:S(2)}, u32[]{:S(2)}) collective-permute-start(bf16[160,3840]{1,0:T(8,128)(2,1)} %collective-permute-done.15.refs_5_.refs_4_), channel_id=1, source_target_pairs={{0,16},{1,9},{2,18},{3,11},{4,20},{5,13},{6,22},{7,15},{8,24},{9,1... | collective-permute-start | bytes 3686408 | tf_op jit(solution)/shard_map/ppermute | solution.py:742
  136.3 34.2 %collective-permute-start.20 = (bf16[160,3840]{1,0:T(8,128)(2,1)}, bf16[160,3840]{1,0:T(8,128)(2,1)S(1)}, u32[]{:S(2)}, u32[]{:S(2)}) collective-permute-start(bf16[160,3840]{1,0:T(8,128)(2,1)} %collective-permute-done.15.refs_5_.refs_4_), channel_id=1, source_target_pairs={{0,1},{1,0},{2,3},{3,2},{4,5},{5,4},{6,7},{7,6},{8,9},{9,8},{10,11... | collective-permute-start | bytes 3686408 | tf_op jit(solution)/shard_map/ppermute | solution.py:742
  137.9 32.7 %collective-permute-start.21 = (bf16[160,3840]{1,0:T(8,128)(2,1)}, bf16[160,3840]{1,0:T(8,128)(2,1)}, u32[]{:S(2)}, u32[]{:S(2)}) collective-permute-start(bf16[160,3840]{1,0:T(8,128)(2,1)} %collective-permute-done.15.refs_5_.refs_4_), channel_id=1, source_target_pairs={{0,4},{1,5},{2,6},{3,7},{4,0},{5,1},{6,2},{7,3},{8,12},{9,13},{10,... | collective-permute-start | bytes 3686408 | tf_op jit(solution)/shard_map/ppermute | solution.py:742
  139.2 31.3 %collective-permute-start.22 = (bf16[160,3584]{1,0:T(8,128)(2,1)}, bf16[160,3584]{1,0:T(8,128)(2,1)}, u32[]{:S(2)}, u32[]{:S(2)}) collective-permute-start(bf16[160,3584]{1,0:T(8,128)(2,1)} %pad_maximum_fusion.2), channel_id=1, source_target_pairs={{0,8},{1,17},{2,10},{3,19},{4,12},{5,21},{6,14},{7,23},{8,0},{9,25... | collective-permute-start | bytes 3440648 | tf_op jit(solution)/shard_map/ppermute | solution.py:742
  171.2 32.0 %collective-permute-start.25 = (bf16[160,3584]{1,0:T(8,128)(2,1)}, bf16[160,3584]{1,0:T(8,128)(2,1)}, u32[]{:S(2)}, u32[]{:S(2)}) collective-permute-start(bf16[160,3584]{1,0:T(8,128)(2,1)} %collective-permute-done.22.refs_12_.refs_16_), channel_id=1, source_target_pairs={{0,16},{1,9},{2,18},{3,11},{4,20},{5,13},{6,22},{7,15},{8,24},{9,1... | collective-permute-start | bytes 3440648 | tf_op jit(solution)/shard_map/ppermute | solution.py:742
  172.2 31.0 %collective-permute-start.26 = (bf16[160,3584]{1,0:T(8,128)(2,1)}, bf16[160,3584]{1,0:T(8,128)(2,1)}, u32[]{:S(2)}, u32[]{:S(2)}) collective-permute-start(bf16[160,3584]{1,0:T(8,128)(2,1)} %collective-permute-done.22.refs_12_.refs_16_), channel_id=1, source_target_pairs={{0,1},{1,0},{2,3},{3,2},{4,5},{5,4},{6,7},{7,6},{8,9},{9,8},{10,11... | collective-permute-start | bytes 3440648 | tf_op jit(solution)/shard_map/ppermute | solution.py:742
  173.8 29.4 %collective-permute-start.27 = (bf16[160,3584]{1,0:T(8,128)(2,1)}, bf16[160,3584]{1,0:T(8,128)(2,1)}, u32[]{:S(2)}, u32[]{:S(2)}) collective-permute-start(bf16[160,3584]{1,0:T(8,128)(2,1)} %collective-permute-done.22.refs_12_.refs_16_), channel_id=1, source_target_pairs={{0,4},{1,5},{2,6},{3,7},{4,0},{5,1},{6,2},{7,3},{8,12},{9,13},{10,... | collective-permute-start | bytes 3440648 | tf_op jit(solution)/shard_map/ppermute | solution.py:742
  175.6 27.6 %collective-permute-start.28 = (bf16[160,3072]{1,0:T(8,128)(2,1)S(1)}, bf16[160,3072]{1,0:T(8,128)(2,1)}, u32[]{:S(2)}, u32[]{:S(2)}) collective-permute-start(bf16[160,3072]{1,0:T(8,128)(2,1)S(1)} %copy-done.57), channel_id=1, source_target_pairs={{0,8},{1,17},{2,10},{3,19},{4,12},{5,21},{6,14},{7,23},{8,0},{9,25... | collective-permute-start | bytes 2949128 | tf_op jit(solution)/shard_map/ppermute | solution.py:742
  203.8 31.0 %collective-permute-start.31 = (bf16[160,3072]{1,0:T(8,128)(2,1)}, bf16[160,3072]{1,0:T(8,128)(2,1)S(1)}, u32[]{:S(2)}, u32[]{:S(2)}) collective-permute-start(bf16[160,3072]{1,0:T(8,128)(2,1)} %collective-permute-done.28.refs_4_), channel_id=1, source_target_pairs={{0,16},{1,9},{2,18},{3,11},{4,20},{5,13},{6,22},{7,15},{8,24},{9,1... | collective-permute-start | bytes 2949128 | tf_op jit(solution)/shard_map/ppermute | solution.py:742
  205.4 29.4 %collective-permute-start.32 = (bf16[160,3072]{1,0:T(8,128)(2,1)}, bf16[160,3072]{1,0:T(8,128)(2,1)}, u32[]{:S(2)}, u32[]{:S(2)}) collective-permute-start(bf16[160,3072]{1,0:T(8,128)(2,1)} %collective-permute-done.28.refs_4_), channel_id=1, source_target_pairs={{0,1},{1,0},{2,3},{3,2},{4,5},{5,4},{6,7},{7,6},{8,9},{9,8},{10,11... | collective-permute-start | bytes 2949128 | tf_op jit(solution)/shard_map/ppermute | solution.py:742
  207.0 27.9 %collective-permute-start.33 = (bf16[160,3072]{1,0:T(8,128)(2,1)}, bf16[160,3072]{1,0:T(8,128)(2,1)}, u32[]{:S(2)}, u32[]{:S(2)}) collective-permute-start(bf16[160,3072]{1,0:T(8,128)(2,1)} %collective-permute-done.28.refs_4_), channel_id=1, source_target_pairs={{0,4},{1,5},{2,6},{3,7},{4,0},{5,1},{6,2},{7,3},{8,12},{9,13},{10,... | collective-permute-start | bytes 2949128 | tf_op jit(solution)/shard_map/ppermute | solution.py:742
  207.0 27.8 %collective-permute-start.34 = (bf16[160,2048]{1,0:T(8,128)(2,1)}, bf16[160,2048]{1,0:T(8,128)(2,1)}, u32[]{:S(2)}, u32[]{:S(2)}) collective-permute-start(bf16[160,2048]{1,0:T(8,128)(2,1)} %pad_maximum_fusion.5), channel_id=1, source_target_pairs={{0,8},{1,17},{2,10},{3,19},{4,12},{5,21},{6,14},{7,23},{8,0},{9,25... | collective-permute-start | bytes 1966088 | tf_op jit(solution)/shard_map/ppermute | solution.py:742
  341.3 27.9 %collective-permute-start.44 = (bf16[4,512,768]{2,1,0:T(8,128)(2,1)}, bf16[4,512,768]{2,1,0:T(8,128)(2,1)S(1)}, u32[]{:S(2)}, u32[]{:S(2)}) collective-permute-start(bf16[4,512,768]{2,1,0:T(8,128)(2,1)} %get-tuple-element.238), channel_id=1, source_target_pairs={{0,4},{1,5},{2,6},{3,7},{4,0},{5,1},{6,2},{7,3},{8,12},{9,13},{10,... | collective-permute-start | bytes 9437192 | tf_op jit(solution)/shard_map/ppermute | solution.py:742
  (133 other events, 1149.6 us)
